TPU v7x, 32 devices: a whole 2x2x4 slice. The times are simulated.
32 devices in a mesh: seq: 8 (over z, x), tp: 4 (over y, core).
Axes of the slice: x: 2, y: 2, z: 4, core: 2. Of those that a mesh axis runs over, the one named last changes fastest.
Arguments:
- hidden_in: bfloat16 [16, 2048], replicated, may hold values from -6 to 6
- lengths: int32 [16], replicated, may hold values from 1 to 511, 2431 in all
- positions: int32 [16], replicated, may hold values from 0 to 1023
- query_weight: bfloat16 [2, 2048, 2048], P(None, 'seq', 'tp'), may hold values from -0.125 to 0.125
- key_weight: bfloat16 [2, 2048, 512], P(None, 'seq', 'tp'), may hold values from -4 to 4
- value_weight: bfloat16 [2, 2048, 512], P(None, 'seq', 'tp'), may hold values from -0.125 to 0.125
- out_weight: bfloat16 [2, 2048, 2048], P(None, 'tp', 'seq'), may hold values from -0.125 to 0.125
- gate_weight: bfloat16 [2, 2048, 8192], P(None, 'seq', 'tp'), may hold values from -0.125 to 0.125
- up_weight: bfloat16 [2, 2048, 8192], P(None, 'seq', 'tp'), may hold values from -0.125 to 0.125
- down_weight: bfloat16 [2, 8192, 2048], P(None, 'tp', 'seq'), may hold values from -0.0625 to 0.0625
- key_cache: bfloat16 [2, 16, 512, 512], P(None, None, 'seq', 'tp'), may hold values from -80 to 80
- value_cache: bfloat16 [2, 16, 512, 512], P(None, None, 'seq', 'tp'), may hold values from -6 to 6
Outputs:
- hidden_out: bfloat16 [16, 2048], replicated
- key_out: bfloat16 [2, 16, 512, 512], P(None, None, 'seq', 'tp')
- value_out: bfloat16 [2, 16, 512, 512], P(None, None, 'seq', 'tp')
Inputs may be any that keep to these rules, and one draw needn't show every extreme that they name: Request b has its cached rows at positions 0 .. lengths[b] - 1 and its new token goes to row lengths[b]; rows above are padding. The longest request has exactly 511 cached rows.
All inputs are finite; a program needn't handle non-finite values.
Results may differ from a plain program's by a relative error of at most 0.015.
Values may be sent and summed in bfloat16 or wider, within the bound.
No kernel may reach another device: no remote copies, remote signals or barrier semaphores. Data moves between devices by JAX's collectives and lax.ppermute only.
A program may use at most 64 MiB of HBM per device.

v0:
```python
import math

import jax
import jax.numpy as jnp
from jax import lax
from jax.sharding import PartitionSpec as P

HEAD_DIM = 64
LAYERS = 2


eps_norm = 1e-05
neg_fill = -1e30


def rms_norm(stream):
    as_float = stream.astype(jnp.float32)
    spread = jnp.mean(as_float * as_float, axis=-1, keepdims=True)
    return (as_float * lax.rsqrt(spread + eps_norm)).astype(jnp.bfloat16)


def rotate(heads, positions):
    half_dim = heads.shape[-1] // 2
    inverse = 500000.0 ** (-(2.0 * jnp.arange(half_dim, dtype=jnp.float32)) / heads.shape[-1])
    angles = positions.astype(jnp.float32)[:, None] * inverse[None, :]
    cosine = jnp.cos(angles)[:, None, :]
    sine = jnp.sin(angles)[:, None, :]
    first_half = heads[..., :half_dim]
    second_half = heads[..., half_dim:]
    return jnp.concatenate(
        [first_half * cosine - second_half * sine, second_half * cosine + first_half * sine],
        axis=-1,
    )


def per_device(
    hidden_in,
    lengths,
    positions,
    query_weight,
    key_weight,
    value_weight,
    out_weight,
    gate_weight,
    up_weight,
    down_weight,
    key_cache,
    value_cache,
):
    seq_index = lax.axis_index("seq")
    row_count = query_weight.shape[1]
    row_start = seq_index * row_count
    col_count = out_weight.shape[2]
    col_start = seq_index * col_count
    block_len = key_cache.shape[2]
    kv_width_here = key_cache.shape[3]
    query_width = query_weight.shape[2]
    requests = hidden_in.shape[0]
    group_heads = query_width // HEAD_DIM
    kv_here = kv_width_here // HEAD_DIM
    repeat = group_heads // kv_here
    score_scale = 1.0 / math.sqrt(HEAD_DIM)
    global_slots = seq_index * block_len + jnp.arange(block_len, dtype=jnp.int32)
    new_slot = (global_slots[None, :] == lengths[:, None])[:, :, None]
    live_mask = (global_slots[None, :] <= lengths[:, None])[:, None, None, :]

    def finish(part_terms, stream_now):
        summed = lax.psum(part_terms, "tp")
        own_cols = lax.dynamic_slice_in_dim(stream_now, col_start, col_count, 1).astype(jnp.float32)
        return lax.all_gather((own_cols + summed).astype(jnp.bfloat16), "seq", axis=1, tiled=True)

    stream = hidden_in
    key_layers = []
    value_layers = []
    for layer_idx in range(LAYERS):
        normed = rms_norm(stream)
        own_rows = lax.dynamic_slice_in_dim(normed, row_start, row_count, 1)
        query_part = jnp.dot(own_rows, query_weight[layer_idx], preferred_element_type=jnp.float32)
        key_part = jnp.dot(own_rows, key_weight[layer_idx], preferred_element_type=jnp.float32)
        value_part = jnp.dot(own_rows, value_weight[layer_idx], preferred_element_type=jnp.float32)
        query, key_new, value_new = lax.psum((query_part, key_part, value_part), "seq")
        query = rotate(query.reshape(requests, group_heads, HEAD_DIM), positions).astype(
            jnp.bfloat16
        )
        query = query.reshape(requests, kv_here, repeat, HEAD_DIM)
        key_new = (
            rotate(key_new.reshape(requests, kv_here, HEAD_DIM), positions)
            .astype(jnp.bfloat16)
            .reshape(requests, kv_width_here)
        )
        value_new = value_new.astype(jnp.bfloat16)
        key_rows = jnp.where(new_slot, key_new[:, None, :], key_cache[layer_idx])
        value_rows = jnp.where(new_slot, value_new[:, None, :], value_cache[layer_idx])
        key_heads = key_rows.reshape(requests, block_len, kv_here, HEAD_DIM)
        value_heads = value_rows.reshape(requests, block_len, kv_here, HEAD_DIM)
        scores = (
            jnp.einsum("bkrd,bskd->bkrs", query, key_heads, preferred_element_type=jnp.float32)
            * score_scale
        )
        scores = jnp.where(live_mask, scores, neg_fill)
        row_top = lax.pmax(jnp.max(scores, axis=3), "seq")
        weights = jnp.where(live_mask, jnp.exp(scores - row_top[..., None]), 0.0)
        local_sums = jnp.sum(weights, axis=3)
        local_acc = jnp.einsum(
            "bkrs,bskd->bkrd",
            weights.astype(jnp.bfloat16),
            value_heads,
            preferred_element_type=jnp.float32,
        )
        totals, weighted = lax.psum((local_sums, local_acc), "seq")
        attended = (
            (weighted / totals[..., None]).astype(jnp.bfloat16).reshape(requests, query_width)
        )
        attn_terms = jnp.dot(attended, out_weight[layer_idx], preferred_element_type=jnp.float32)
        mid = finish(attn_terms, stream)
        normed_two = rms_norm(mid)
        rows_two = lax.dynamic_slice_in_dim(normed_two, row_start, row_count, 1)
        gate_part = jnp.dot(rows_two, gate_weight[layer_idx], preferred_element_type=jnp.float32)
        up_part = jnp.dot(rows_two, up_weight[layer_idx], preferred_element_type=jnp.float32)
        gate_sum, up_sum = lax.psum((gate_part, up_part), "seq")
        hidden = (jax.nn.silu(gate_sum) * up_sum).astype(jnp.bfloat16)
        down_terms = jnp.dot(hidden, down_weight[layer_idx], preferred_element_type=jnp.float32)
        stream = finish(down_terms, mid)
        key_layers.append(key_rows)
        value_layers.append(value_rows)
    return (stream, jnp.stack(key_layers), jnp.stack(value_layers))


def solution(mesh):
    return jax.shard_map(
        per_device,
        mesh=mesh,
        in_specs=(
            P(),
            P(),
            P(),
            P(None, "seq", "tp"),
            P(None, "seq", "tp"),
            P(None, "seq", "tp"),
            P(None, "tp", "seq"),
            P(None, "seq", "tp"),
            P(None, "seq", "tp"),
            P(None, "tp", "seq"),
            P(None, None, "seq", "tp"),
            P(None, None, "seq", "tp"),
        ),
        out_specs=(P(), P(None, None, "seq", "tp"), P(None, None, "seq", "tp")),
        check_vma=False,
    )
```

profile of v0, /device:TPU:0, one launch (start us, length us, event | category | flops | bytes accessed | tf_op | source)
XLA Modules:
  0.0 562.6 jit_solution(6855281874656980006)
XLA Ops:
  7.2 0.9 convert_element_type.105
  8.1 1.0 multiply_reduce_fusion.3
  9.1 1.0 fusion.46
  10.2 1.0 fusion.48
  11.3 1.1 fusion.32
  12.5 1.0 slice.86
  13.7 39.8 %all-reduce.3 = (bf16[16,128]{1,0:T(8,128)(2,1)S(1)}, f32[16,2,64]{2,1,0:T(2,128)S(1)}, f32[16,8,64]{2,1,0:T(8,128)S(1)}) all-reduce(f32[16,128]{1,0:T(8,128)S(1)} %fusion.46, f32[16,2,64]{2,1,0:T(2,128)S(1)} %reshape.206, f32[16,8,64]{2,1,0:T(8,128)S(1)} %reshape.205), channel_id=1, replica_groups=mesh['seq'=8,'tp'=4] {'seq'}, use_global_device_ids=true, to_apply=%region_5.6 | all-reduce | flops 12288 | bytes 94208 | tf_op jit(solution)/shard_map/psum | solution.py:81
  53.6 0.7 broadcast_in_dim.117
  54.3 1.1 squeeze.56
  55.8 1.7 fusion.88
  57.5 33.0 %pmax.14 = f32[16,2,4]{2,1,0:T(2,128)S(1)} all-reduce(f32[16,2,4]{2,1,0:T(2,128)S(1)} %get-tuple-element.38), channel_id=1, replica_groups=mesh['seq'=8,'tp'=4] {'seq'}, use_global_device_ids=true, to_apply=%region_4.5 | all-reduce | flops 128 | bytes 1024 | tf_op jit(solution)/shard_map/pmax | solution.py:101
  90.7 1.0 fusion.21
  91.8 33.8 %all-reduce.2 = (f32[16,2,4,64]{3,2,1,0:T(4,128)S(1)}, f32[16,2,4]{2,1,0:T(2,128)S(1)}) all-reduce(f32[16,2,4,64]{3,2,1,0:T(4,128)S(1)} %fusion.21, f32[16,2,4]{2,1,0:T(2,128)S(1)} %fusion.56), channel_id=1, replica_groups=mesh['seq'=8,'tp'=4] {'seq'}, use_global_device_ids=true, to_apply=%region_6.7 | all-reduce | flops 8320 | bytes 66560 | tf_op jit(solution)/shard_map/psum | solution.py:110
  126.0 10.1 %psum.131 = f32[16,256]{1,0:T(8,128)S(1)} all-reduce(f32[16,256]{1,0:T(8,128)S(1)} %fusion.30), channel_id=1, replica_groups=mesh['seq'=8,'tp'=4] {'tp'}, use_global_device_ids=true, to_apply=%region_9.10 | all-reduce | flops 4096 | bytes 32768 | tf_op jit(solution)/shard_map/psum | solution.py:68
  136.1 0.7 add_convert_fusion.5
  136.8 30.5 %all_gather.12 = bf16[16,2048]{1,0:T(8,128)(2,1)S(1)} all-gather(bf16[16,256]{1,0:T(8,128)(2,1)S(1)} %add_convert_fusion.5), channel_id=1, replica_groups=mesh['seq'=8,'tp'=4] {'seq'}, dimensions={1}, use_global_device_ids=true | all-gather | bytes 73728 | tf_op jit(solution)/shard_map/all_gather | solution.py:70
  167.5 1.0 fusion.10
  168.4 2.3 fusion.12
  170.8 0.7 convert_element_type.131
  171.4 69.2 %all-reduce.11.cloned.1.call-done = (f32[16,2048]{1,0:T(8,128)}, f32[16,2048]{1,0:T(8,128)}) async-done(((f32[16,2048]{1,0:T(8,128)}, f32[16,2048]{1,0:T(8,128)}), (f32[16,2048]{1,0:T(8,128)}, f32[16,2048]{1,0:T(8,128)})) %all-reduce.11.cloned.1.call-update) | async-done | bytes 262160 | tf_op jit(solution)/shard_map/psum | solution.py:120
  240.6 1.6 fusion.8
  242.2 10.1 %psum.134 = f32[16,256]{1,0:T(8,128)S(1)} all-reduce(f32[16,256]{1,0:T(8,128)S(1)} %fusion.8), channel_id=1, replica_groups=mesh['seq'=8,'tp'=4] {'tp'}, use_global_device_ids=true, to_apply=%region_13.14 | all-reduce | flops 4096 | bytes 32768 | tf_op jit(solution)/shard_map/psum | solution.py:68
  252.3 30.5 %all_gather.13 = bf16[16,2048]{1,0:T(8,128)(2,1)S(1)} all-gather(bf16[16,256]{1,0:T(8,128)(2,1)S(1)} %add_convert_fusion.4), channel_id=1, replica_groups=mesh['seq'=8,'tp'=4] {'seq'}, dimensions={1}, use_global_device_ids=true | all-gather | bytes 73728 | tf_op jit(solution)/shard_map/all_gather | solution.py:70
  283.0 1.0 fusion.42
  284.0 1.0 fusion.44
  285.1 1.1 fusion.28
  286.4 36.4 %all-reduce.1 = (bf16[16,128]{1,0:T(8,128)(2,1)S(1)}, f32[16,2,64]{2,1,0:T(2,128)S(1)}, f32[16,8,64]{2,1,0:T(8,128)S(1)}) all-reduce(f32[16,128]{1,0:T(8,128)S(1)} %fusion.42, f32[16,2,64]{2,1,0:T(2,128)S(1)} %reshape.209, f32[16,8,64]{2,1,0:T(8,128)S(1)} %reshape.208), channel_id=1, replica_groups=mesh['seq'=8,'tp'=4] {'seq'}, use_global_device_ids=true, to_apply=%region_19.20 | all-reduce | flops 12288 | bytes 94208 | tf_op jit(solution)/shard_map/psum | solution.py:81
  323.0 0.7 convert_element_type.132
  323.7 0.7 broadcast_in_dim.120
  324.4 1.9 broadcast_select_fusion.1
  326.2 1.2 squeeze.67
  327.4 0.2 squeeze.65
  327.8 1.2 fusion.89
  329.0 33.0 %pmax.15 = f32[16,2,4]{2,1,0:T(2,128)S(1)} all-reduce(f32[16,2,4]{2,1,0:T(2,128)S(1)} %get-tuple-element.40), channel_id=1, replica_groups=mesh['seq'=8,'tp'=4] {'seq'}, use_global_device_ids=true, to_apply=%region_18.19 | all-reduce | flops 128 | bytes 1024 | tf_op jit(solution)/shard_map/pmax | solution.py:101
  362.0 0.9 fusion.58
  362.9 1.1 fusion.20
  364.0 34.0 %all-reduce = (f32[16,2,4,64]{3,2,1,0:T(4,128)S(1)}, f32[16,2,4]{2,1,0:T(2,128)S(1)}) all-reduce(f32[16,2,4,64]{3,2,1,0:T(4,128)S(1)} %fusion.20, f32[16,2,4]{2,1,0:T(2,128)S(1)} %fusion.58), channel_id=1, replica_groups=mesh['seq'=8,'tp'=4] {'seq'}, use_global_device_ids=true, to_apply=%region_20.21 | all-reduce | flops 8320 | bytes 66560 | tf_op jit(solution)/shard_map/psum | solution.py:110
  398.2 1.1 fusion.26
  399.3 10.1 %psum.140 = f32[16,256]{1,0:T(8,128)S(1)} all-reduce(f32[16,256]{1,0:T(8,128)S(1)} %fusion.26), channel_id=1, replica_groups=mesh['seq'=8,'tp'=4] {'tp'}, use_global_device_ids=true, to_apply=%region_23.24 | all-reduce | flops 4096 | bytes 32768 | tf_op jit(solution)/shard_map/psum | solution.py:68
  409.4 30.5 %all_gather.14 = bf16[16,2048]{1,0:T(8,128)(2,1)S(1)} all-gather(bf16[16,256]{1,0:T(8,128)(2,1)S(1)} %add_convert_fusion.3), channel_id=1, replica_groups=mesh['seq'=8,'tp'=4] {'seq'}, dimensions={1}, use_global_device_ids=true | all-gather | bytes 73728 | tf_op jit(solution)/shard_map/all_gather | solution.py:70
  440.0 0.9 fusion.4
  441.0 2.3 fusion.6
  443.4 1.1 pad_maximum_fusion
  444.4 68.8 %all-reduce.9.cloned.1.call-done = (f32[16,2048]{1,0:T(8,128)}, f32[16,2048]{1,0:T(8,128)}) async-done(((f32[16,2048]{1,0:T(8,128)}, f32[16,2048]{1,0:T(8,128)}), (f32[16,2048]{1,0:T(8,128)}, f32[16,2048]{1,0:T(8,128)})) %all-reduce.9.cloned.1.call-update) | async-done | bytes 262160 | tf_op jit(solution)/shard_map/psum | solution.py:120
  513.3 1.2 fusion.2
  514.5 10.1 %psum.143 = f32[16,256]{1,0:T(8,128)S(1)} all-reduce(f32[16,256]{1,0:T(8,128)S(1)} %fusion.2), channel_id=1, replica_groups=mesh['seq'=8,'tp'=4] {'tp'}, use_global_device_ids=true, to_apply=%region_27.28 | all-reduce | flops 4096 | bytes 32768 | tf_op jit(solution)/shard_map/psum | solution.py:68
  524.6 30.5 %all_gather.15 = bf16[16,2048]{1,0:T(8,128)(2,1)S(1)} all-gather(bf16[16,256]{1,0:T(8,128)(2,1)S(1)} %add_convert_fusion.2), channel_id=1, replica_groups=mesh['seq'=8,'tp'=4] {'seq'}, dimensions={1}, use_global_device_ids=true | all-gather | bytes 73728 | tf_op jit(solution)/shard_map/all_gather | solution.py:70
  555.1 0.6 copy.36
  (73 shorter events, 2.7 us)
Async XLA Ops:
  7.2 47.1 %slice-start = ((bf16[2,16,64,128]{3,2,1,0:T(8,128)(2,1)}), bf16[1,16,64,128]{3,2,1,0:T(8,128)(2,1)S(1)}, s32[]{:S(2)}) async-start(bf16[2,16,64,128]{3,2,1,0:T(8,128)(2,1)} %param.22), calls=%async_computation.2 | async-start | bytes 524288 | tf_op jit(solution)/shard_map/slice | solution.py:92
  7.2 48.1 %copy-start.15 = (s32[16]{0:T(128)S(1)}, s32[16]{0:T(128)}, u32[]{:S(2)}) copy-start(s32[16]{0:T(128)} %param.14) | copy-start | bytes 196
  7.2 48.5 %copy-start.13 = (s32[16]{0:T(128)S(1)}, s32[16]{0:T(128)}, u32[]{:S(2)}) copy-start(s32[16]{0:T(128)} %param.13) | copy-start | bytes 196
  7.2 233.4 %all-reduce.11.cloned.1.call-start = ((), (), s32[]{:S(2)}) async-start(), calls=%async_computation.1 | async-start | bytes 524288 | tf_op jit(solution)/shard_map/psum | solution.py:120
  53.6 0.7 copy-start.10
  54.3 71.6 %copy-start.7 = (bf16[2,512,256]{2,1,0:T(8,128)(2,1)S(1)}, bf16[2,512,256]{2,1,0:T(8,128)(2,1)}, u32[]{:S(2)}) copy-start(bf16[2,512,256]{2,1,0:T(8,128)(2,1)} %param.18) | copy-start | bytes 1572868
  55.5 111.9 %copy-start = (bf16[2,256,2048]{2,1,0:T(8,128)(2,1)S(1)}, bf16[2,256,2048]{2,1,0:T(8,128)(2,1)}, u32[]{:S(2)}) copy-start(bf16[2,256,2048]{2,1,0:T(8,128)(2,1)} %param.20) | copy-start | bytes 6291460
  55.7 112.7 %copy-start.9 = (pred[16,64]{1,0:T(8,128)(4,1)}, pred[16,64]{1,0:T(8,128)(4,1)S(1)}, u32[]{:S(2)}) copy-start(pred[16,64]{1,0:T(8,128)(4,1)S(1)} %get-tuple-element.34) | copy-start | bytes 3076
  55.7 112.7 %copy-start.12 = (pred[16,64]{1,0:T(8,128)(4,1)}, pred[16,64]{1,0:T(8,128)(4,1)S(1)}, u32[]{:S(2)}) copy-start(pred[16,64]{1,0:T(8,128)(4,1)S(1)} %get-tuple-element.35) | copy-start | bytes 3076
  168.4 155.9 %copy-start.1 = (bf16[2,16,64,128]{3,2,1,0:T(8,128)(2,1)S(1)}, bf16[2,16,64,128]{3,2,1,0:T(8,128)(2,1)}, u32[]{:S(2)}) copy-start(bf16[2,16,64,128]{3,2,1,0:T(8,128)(2,1)} %param.23) | copy-start | bytes 1572868
  168.4 155.9 %copy-start.2 = (bf16[2,16,64,128]{3,2,1,0:T(8,128)(2,1)S(1)}, bf16[2,16,64,128]{3,2,1,0:T(8,128)(2,1)}, u32[]{:S(2)}) copy-start(bf16[2,16,64,128]{3,2,1,0:T(8,128)(2,1)} %param.22) | copy-start | bytes 1572868
  170.7 342.6 %all-reduce.9.cloned.1.call-start = ((), (), s32[]{:S(2)}) async-start(), calls=%async_computation | async-start | bytes 524288 | tf_op jit(solution)/shard_map/psum | solution.py:120
  322.8 0.9 copy-start.11
  323.0 0.7 copy-start.8
  364.0 79.4 %copy-start.3 = (bf16[1,16,64,128]{3,2,1,0:T(8,128)(2,1)S(1)}, bf16[1,16,64,128]{3,2,1,0:T(8,128)(2,1)}, u32[]{:S(2)}) copy-start(bf16[1,16,64,128]{3,2,1,0:T(8,128)(2,1)} %get-tuple-element.17) | copy-start | bytes 786436
  364.0 79.4 %copy-start.4 = (bf16[1,16,64,128]{3,2,1,0:T(8,128)(2,1)S(1)}, bf16[1,16,64,128]{3,2,1,0:T(8,128)(2,1)}, u32[]{:S(2)}) copy-start(bf16[1,16,64,128]{3,2,1,0:T(8,128)(2,1)} %get-tuple-element.18) | copy-start | bytes 786436
  364.0 79.4 %copy-start.5 = (bf16[1,16,64,128]{3,2,1,0:T(8,128)(2,1)S(1)}, bf16[1,16,64,128]{3,2,1,0:T(8,128)(2,1)}, u32[]{:S(2)}) copy-start(bf16[1,16,64,128]{3,2,1,0:T(8,128)(2,1)} %get-tuple-element.32) | copy-start | bytes 786436
  364.0 79.4 %copy-start.6 = (bf16[1,16,64,128]{3,2,1,0:T(8,128)(2,1)S(1)}, bf16[1,16,64,128]{3,2,1,0:T(8,128)(2,1)}, u32[]{:S(2)}) copy-start(bf16[1,16,64,128]{3,2,1,0:T(8,128)(2,1)} %get-tuple-element.33) | copy-start | bytes 786436
  441.0 72.3 %copy-start.14 = (bf16[2,2048,256]{2,1,0:T(8,128)(2,1)S(1)}, bf16[2,2048,256]{2,1,0:T(8,128)(2,1)}, u32[]{:S(2)}) copy-start(bf16[2,2048,256]{2,1,0:T(8,128)(2,1)} %param.21) | copy-start | bytes 6291460
Sparse Core Ops, SparseCore 0:
  170.8 69.7 all-reduce.10
  443.5 69.7 all-reduce.8
where the time goes:
time: 564 us; the launch traced here: 563 us
  blocking collectives  372 us (66%)
  waiting for transfers between devices  138 us (24%)
  matrix products  22 us (4%)
  between operations  14.4 us (3%)
  other arithmetic  8.02 us (1%)
  local copies, waits for them, and re-layouts  7.62 us (1%)
    psum x2, waiting for transfers between devices, per_device(): gate_sum, up_sum = lax.psum((gate_part, up_part), 'seq')  138 us
    all_gather x4, blocking collectives, finish(): lax.all_gather((own_cols + summed).astype(jnp.bfloat16), 'seq', axis=1, t...  122 us
    psum x2, blocking collectives, per_device(): lax.psum((query_part, key_part, value_part), 'seq')  76.3 us
    psum x2, blocking collectives, per_device(): totals, weighted = lax.psum((local_sums, local_acc), 'seq')  67.8 us
    pmax x2, blocking collectives, per_device(): row_top = lax.pmax(jnp.max(scores, axis=3), 'seq')  66 us
    psum x4, blocking collectives, finish(): summed = lax.psum(part_terms, 'tp')  40.5 us
  transfers between devices with their start and end apart: 2, of which 2 were waited for; matrix products, arithmetic and copies ran while one was open for 0% of the time, Pallas kernels for 0%

commit v1 on v0

v1 whole, which is shorter than its diff:
```python
import math

import jax
import jax.numpy as jnp
from jax import lax
from jax.sharding import PartitionSpec as P

HEAD_DIM = 64
LAYERS = 2
eps_norm = 1e-05
neg_fill = -1e30


def split_hi_lo(value, parts):
    out = []
    rest = value
    for _ in range(parts):
        head = lax.reduce_precision(rest, 8, 7)
        out.append(head.astype(jnp.bfloat16))
        rest = rest - head
    return out


def seq_swap(chunks):
    return lax.all_to_all(chunks, "seq", 0, 0)


def make_per_device(n_seq, n_tp):
    def tp_sum(part):
        total = part
        for k in range(1, n_tp):
            total = total + lax.ppermute(part, "tp", [(i, (i + k) % n_tp) for i in range(n_tp)])
        return total

    def per_device(
        hidden_in,
        lengths,
        positions,
        query_weight,
        key_weight,
        value_weight,
        out_weight,
        gate_weight,
        up_weight,
        down_weight,
        key_cache,
        value_cache,
    ):
        seq_index = lax.axis_index("seq")
        requests, width = hidden_in.shape
        col_count = out_weight.shape[2]
        col_start = seq_index * col_count
        block_len = key_cache.shape[2]
        kv_width = key_cache.shape[3]
        query_width = query_weight.shape[2]
        heads = query_width // HEAD_DIM
        kv_heads = kv_width // HEAD_DIM
        repeat = heads // kv_heads
        ff_here = gate_weight.shape[2]
        ff_own = ff_here // n_seq
        scale = 1.0 / math.sqrt(HEAD_DIM)
        slots = seq_index * block_len + jnp.arange(block_len, dtype=jnp.int32)
        new_slot = (slots[None, :] == lengths[:, None])[:, :, None]
        live = (slots[None, :] <= lengths[:, None])[:, None, None, :]

        half = HEAD_DIM // 2
        inverse = 500000.0 ** (-(2.0 * jnp.arange(half, dtype=jnp.float32)) / HEAD_DIM)
        angles = positions.astype(jnp.float32)[:, None] * inverse[None, :]
        cosine = jnp.cos(angles)[:, None, :]
        sine = jnp.sin(angles)[:, None, :]

        def rotate(x):
            a, b = x[..., :half], x[..., half:]
            return jnp.concatenate([a * cosine - b * sine, b * cosine + a * sine], axis=-1)

        def stats_of(x):
            f = x.astype(jnp.float32)
            return jnp.sum(f * f, axis=-1, keepdims=True)

        def pad_lanes(cols):
            joined = jnp.concatenate(cols, axis=-1)
            return jnp.pad(joined, ((0, 0), (0, -joined.shape[-1] % 128)))

        own = lax.dynamic_slice_in_dim(hidden_in, col_start, col_count, 1)
        key_layers = []
        value_layers = []
        for layer in range(LAYERS):
            part = jnp.concatenate(
                [
                    jnp.dot(own, w[layer], preferred_element_type=jnp.float32)
                    for w in (query_weight, key_weight, value_weight)
                ],
                axis=1,
            ).astype(jnp.bfloat16)
            packed = jnp.concatenate([part, pad_lanes(split_hi_lo(stats_of(own), 2))], axis=1)
            got = seq_swap(jnp.broadcast_to(packed[None], (n_seq,) + packed.shape))
            got = jnp.sum(got.astype(jnp.float32), axis=0)
            qkv = query_width + 2 * kv_width
            spread = (got[:, qkv : qkv + 1] + got[:, qkv + 1 : qkv + 2]) / width
            got = got[:, :qkv] * lax.rsqrt(spread + eps_norm)
            query = rotate(got[:, :query_width].reshape(requests, heads, HEAD_DIM))
            query = query.astype(jnp.bfloat16).reshape(requests, kv_heads, repeat, HEAD_DIM)
            key_new = rotate(
                got[:, query_width : query_width + kv_width].reshape(requests, kv_heads, HEAD_DIM)
            )
            key_new = key_new.astype(jnp.bfloat16).reshape(requests, kv_width)
            value_new = got[:, query_width + kv_width :].astype(jnp.bfloat16)
            key_rows = jnp.where(new_slot, key_new[:, None, :], key_cache[layer])
            value_rows = jnp.where(new_slot, value_new[:, None, :], value_cache[layer])
            key_layers.append(key_rows)
            value_layers.append(value_rows)
            key_heads = key_rows.reshape(requests, block_len, kv_heads, HEAD_DIM)
            value_heads = value_rows.reshape(requests, block_len, kv_heads, HEAD_DIM)
            scores = (
                jnp.einsum("bkrd,bskd->bkrs", query, key_heads, preferred_element_type=jnp.float32)
                * scale
            )
            scores = jnp.where(live, scores, neg_fill)
            top = jnp.max(scores, axis=3)
            weights = jnp.where(live, jnp.exp(scores - top[..., None]), 0.0)
            sums = jnp.sum(weights, axis=3)
            acc = jnp.einsum(
                "bkrs,bskd->bkrd",
                weights.astype(jnp.bfloat16),
                value_heads,
                preferred_element_type=jnp.float32,
            )
            packed = jnp.concatenate(
                [
                    acc.reshape(requests, query_width).astype(jnp.bfloat16),
                    pad_lanes(
                        split_hi_lo(top.reshape(requests, heads), 3)
                        + split_hi_lo(sums.reshape(requests, heads), 2)
                    ),
                ],
                axis=1,
            )
            got = seq_swap(jnp.broadcast_to(packed[None], (n_seq,) + packed.shape))
            got = got.astype(jnp.float32)
            acc = got[:, :, :query_width].reshape(n_seq, requests, heads, HEAD_DIM)
            side = got[:, :, query_width : query_width + 5 * heads].reshape(
                n_seq, requests, 5, heads
            )
            tops = side[:, :, 0] + side[:, :, 1] + side[:, :, 2]
            factor = jnp.exp(tops - jnp.max(tops, axis=0, keepdims=True))
            total = jnp.sum(factor * (side[:, :, 3] + side[:, :, 4]), axis=0)
            attended = jnp.sum(acc * factor[..., None], axis=0) / total[..., None]
            attended = attended.astype(jnp.bfloat16).reshape(requests, query_width)

            part = jnp.dot(attended, out_weight[layer], preferred_element_type=jnp.float32)
            mid = (own.astype(jnp.float32) + tp_sum(part)).astype(jnp.bfloat16)

            gate = jnp.dot(mid, gate_weight[layer], preferred_element_type=jnp.float32)
            up = jnp.dot(mid, up_weight[layer], preferred_element_type=jnp.float32)
            side = pad_lanes(split_hi_lo(stats_of(mid), 2))
            packed = jnp.concatenate(
                [
                    gate.astype(jnp.bfloat16).reshape(requests, n_seq, ff_own),
                    up.astype(jnp.bfloat16).reshape(requests, n_seq, ff_own),
                    jnp.broadcast_to(side[:, None], (requests, n_seq, side.shape[1])),
                ],
                axis=2,
            )
            got = seq_swap(packed.transpose(1, 0, 2))
            got = jnp.sum(got.astype(jnp.float32), axis=0)
            spread = (got[:, 2 * ff_own : 2 * ff_own + 1] + got[:, 2 * ff_own + 1 : 2 * ff_own + 2]) / width
            inv = lax.rsqrt(spread + eps_norm)
            hidden = jax.nn.silu(got[:, :ff_own] * inv) * (got[:, ff_own : 2 * ff_own] * inv)
            hidden = hidden.astype(jnp.bfloat16)
            hidden = seq_swap(jnp.broadcast_to(hidden[None], (n_seq,) + hidden.shape))
            hidden = hidden.transpose(1, 0, 2).reshape(requests, ff_here)
            part = jnp.dot(hidden, down_weight[layer], preferred_element_type=jnp.float32)
            own = (mid.astype(jnp.float32) + tp_sum(part)).astype(jnp.bfloat16)

        stream = seq_swap(jnp.broadcast_to(own[None], (n_seq,) + own.shape))
        stream = stream.transpose(1, 0, 2).reshape(requests, width)
        return (stream, jnp.stack(key_layers), jnp.stack(value_layers))

    return per_device


def solution(mesh):
    return jax.shard_map(
        make_per_device(mesh.shape["seq"], mesh.shape["tp"]),
        mesh=mesh,
        in_specs=(
            P(),
            P(),
            P(),
            P(None, "seq", "tp"),
            P(None, "seq", "tp"),
            P(None, "seq", "tp"),
            P(None, "tp", "seq"),
            P(None, "seq", "tp"),
            P(None, "seq", "tp"),
            P(None, "tp", "seq"),
            P(None, None, "seq", "tp"),
            P(None, None, "seq", "tp"),
        ),
        out_specs=(P(), P(None, None, "seq", "tp"), P(None, None, "seq", "tp")),
        check_vma=False,
    )
```

time: 564 us -> 143 us (0.25)
  blocking collectives: 372 us -> 60 us
  waiting for transfers between devices: 138 us -> 31 us
  starting transfers between devices: 0.08 us -> 19.2 us
  between operations: 14.4 us -> 1.2 us
  matrix products: 22 us -> 9.72 us
    psum x8 -> x0, blocking collectives: 185 us -> none  [the longest x2 76.3 us: per_device(): lax.psum((query_part, key_part, value_part), 'seq')]
    psum x2 -> x0, waiting for transfers between devices: 138 us -> none  [per_device(): gate_sum, up_sum = lax.psum((gate_part, up_part), 'seq')]
    all_gather x4 -> x0, blocking collectives: 122 us -> none  [finish(): lax.all_gather((own_cols + summed).astype(jnp.bfloat16), 'seq', axis=1, t...]
    pmax x2 -> x0, blocking collectives: 66 us -> none  [per_device(): row_top = lax.pmax(jnp.max(scores, axis=3), 'seq')]
    all_to_all x0 -> x6, blocking collectives: none -> 60 us  [seq_swap(): return lax.all_to_all(chunks, 'seq', 0, 0)]
    all_to_all x0 -> x3, waiting for transfers between devices: none -> 19.9 us  [seq_swap(): return lax.all_to_all(chunks, 'seq', 0, 0)]
    all_to_all x0 -> x3, starting transfers between devices: none -> 14 us  [seq_swap(): return lax.all_to_all(chunks, 'seq', 0, 0)]
    ppermute x0 -> x12, waiting for transfers between devices: none -> 11.1 us  [tp_sum(): lax.ppermute(part, 'tp', [(i, (i + k) % n_tp) for i in range(n_tp)])]
  transfers between devices with their start and end apart: 2 -> 15, of which waited for: 2 -> 13; matrix products, arithmetic and copies ran while one was open for 0% -> 3% of each run, Pallas kernels for 0% -> 0%
where the time goes in v1:
time: 143 us; the launch traced here: 142 us
  blocking collectives  60 us (42%)
  waiting for transfers between devices  31 us (22%)
  starting transfers between devices  19.2 us (13%)
  local copies, waits for them, and re-layouts  12.1 us (8%)
  matrix products  9.72 us (7%)
  other arithmetic  8.82 us (6%)
    all_to_all x6, blocking collectives, seq_swap(): return lax.all_to_all(chunks, 'seq', 0, 0)  60 us
    all_to_all x3, waiting for transfers between devices, seq_swap(): return lax.all_to_all(chunks, 'seq', 0, 0)  19.9 us
    all_to_all x3, starting transfers between devices, seq_swap(): return lax.all_to_all(chunks, 'seq', 0, 0)  14 us
    ppermute x12, waiting for transfers between devices, tp_sum(): lax.ppermute(part, 'tp', [(i, (i + k) % n_tp) for i in range(n_tp)])  11.1 us
    ppermute x12, starting transfers between devices, tp_sum(): lax.ppermute(part, 'tp', [(i, (i + k) % n_tp) for i in range(n_tp)])  5.21 us
    dot_general x6, matrix products, per_device(): jnp.dot(own, w[layer], preferred_element_type=jnp.float32)  3.5 us
  transfers between devices with their start and end apart: 15, of which 13 were waited for; matrix products, arithmetic and copies ran while one was open for 3% of the time, Pallas kernels for 0%

profile of v1, /device:TPU:0, one launch (start us, length us, event | category | flops | bytes accessed | tf_op | source)
XLA Modules:
  0.0 142.1 jit_solution(15467325504494470074)
XLA Ops:
  0.7 0.9 fusion.82
  1.6 1.0 convolution_convert_fusion.11
  2.6 1.0 convolution_convert_fusion.10
  3.6 1.1 convolution_convert_fusion.7
  4.7 0.7 broadcast_in_dim.159
  5.5 7.3 %all-to-all-start = ((bf16[8,16,896]{2,1,0:T(8,128)(2,1)}), bf16[8,16,896]{2,1,0:T(8,128)(2,1)S(1)}, u32[]{:S(2)}, u32[]{:S(2)}) async-start(bf16[8,16,896]{2,1,0:T(8,128)(2,1)} %broadcast_in_dim.159), calls=%async_computation | async-start | bytes 458752 | tf_op jit(solution)/shard_map/all_to_all | solution.py:25
  12.7 0.7 convert_element_type.271
  13.4 1.0 slice.194
  15.1 6.1 %all-to-all-done = bf16[8,16,896]{2,1,0:T(8,128)(2,1)S(1)} async-done(((bf16[8,16,896]{2,1,0:T(8,128)(2,1)}), bf16[8,16,896]{2,1,0:T(8,128)(2,1)S(1)}, u32[]{:S(2)}, u32[]{:S(2)}) %all-to-all-start) | async-done | bytes 229408 | tf_op jit(solution)/shard_map/all_to_all | solution.py:25
  22.0 0.5 fusion.145
  23.4 0.4 convolution_convert_fusion.5
  24.0 10.7 %all_to_all.45 = bf16[8,16,640]{2,1,0:T(8,128)(2,1)S(1)} all-to-all(bf16[8,16,640]{2,1,0:T(8,128)(2,1)S(1)} %broadcast_in_dim.166), channel_id=1, replica_groups=mesh['seq'=8,'tp'=4] {'seq'}, dimensions={0} | all-to-all | bytes 327680 | tf_op jit(solution)/shard_map/all_to_all | solution.py:25
  34.7 0.6 copy.193
  35.9 0.7 copy-done.10
  36.7 1.6 %collective-permute-start.1 = (f32[16,256]{1,0:T(8,128)S(1)}, f32[16,256]{1,0:T(8,128)S(1)}, u32[]{:S(2)}, u32[]{:S(2)}) collective-permute-start(f32[16,256]{1,0:T(8,128)S(1)} %fusion.25), channel_id=1, source_target_pairs={{0,2},{1,3},{2,0},{3,1},{4,6},{5,7},{6,4},{7,5},{8,10},{9,11},{10,... | collective-permute-start | bytes 49160 | tf_op jit(solution)/shard_map/ppermute | solution.py:32
  38.5 2.0 %collective-permute-done.1 = f32[16,256]{1,0:T(8,128)S(1)} collective-permute-done((f32[16,256]{1,0:T(8,128)S(1)}, f32[16,256]{1,0:T(8,128)S(1)}, u32[]{:S(2)}, u32[]{:S(2)}) %collective-permute-start.1) | collective-permute-done | bytes 16416 | tf_op jit(solution)/shard_map/ppermute | solution.py:32
  40.5 0.9 collective-permute-done
  41.5 0.8 fusion.84
  42.7 1.6 %convolution_convert_fusion.3 = bf16[16,2048]{1,0:T(8,128)(2,1)S(1)} fusion(bf16[16,256]{1,0:T(8,128)(2,1)S(1)} %get-tuple-element.10, bf16[2,256,2048]{2,1,0:T(8,128)(2,1)} %param.19), kind=kOutput, calls=%fused_computation.3 | convolution fusion | flops 16809984 | bytes 1122304 | tf_op jit(solution)/shard_map/dot_general | solution.py:153
  44.3 10.0 %all_to_all.46 = bf16[8,16,640]{2,1,0:T(8,128)(2,1)S(1)} all-to-all(bf16[8,16,640]{2,1,0:T(8,128)(2,1)S(1)} %maximum_bitcast_fusion), channel_id=1, replica_groups=mesh['seq'=8,'tp'=4] {'seq'}, dimensions={0} | all-to-all | bytes 327680 | tf_op jit(solution)/shard_map/all_to_all | solution.py:25
  54.6 9.3 %all_to_all.47 = bf16[8,16,256]{2,1,0:T(8,128)(2,1)S(1)} all-to-all(bf16[8,16,256]{2,1,0:T(8,128)(2,1)S(1)} %broadcast_in_dim.168), channel_id=1, replica_groups=mesh['seq'=8,'tp'=4] {'seq'}, dimensions={0} | all-to-all | bytes 131072 | tf_op jit(solution)/shard_map/all_to_all | solution.py:25
  64.2 0.7 collective-permute-start.4
  65.1 0.5 collective-permute-done.5
  65.6 2.4 %collective-permute-done.4 = f32[16,256]{1,0:T(8,128)S(1)} collective-permute-done((f32[16,256]{1,0:T(8,128)S(1)}, f32[16,256]{1,0:T(8,128)S(1)}, u32[]{:S(2)}, u32[]{:S(2)}) %collective-permute-start.4) | collective-permute-done | bytes 16416 | tf_op jit(solution)/shard_map/ppermute | solution.py:32
  68.8 0.7 broadcast_in_dim.169
  69.5 3.4 %all-to-all-start.4 = ((bf16[8,16,896]{2,1,0:T(8,128)(2,1)}), bf16[8,16,896]{2,1,0:T(8,128)(2,1)S(1)}, u32[]{:S(2)}, u32[]{:S(2)}) async-start(bf16[8,16,896]{2,1,0:T(8,128)(2,1)} %broadcast_in_dim.169), calls=%async_computation.4 | async-start | bytes 458752 | tf_op jit(solution)/shard_map/all_to_all | solution.py:25
  73.0 7.9 %all-to-all-done.4 = bf16[8,16,896]{2,1,0:T(8,128)(2,1)S(1)} async-done(((bf16[8,16,896]{2,1,0:T(8,128)(2,1)}), bf16[8,16,896]{2,1,0:T(8,128)(2,1)S(1)}, u32[]{:S(2)}, u32[]{:S(2)}) %all-to-all-start.4) | async-done | bytes 229408 | tf_op jit(solution)/shard_map/all_to_all | solution.py:25
  81.9 1.2 broadcast_select_fusion.1
  83.1 1.2 squeeze.77
  84.5 0.5 fusion.146
  86.5 10.8 %all_to_all.48 = bf16[8,16,640]{2,1,0:T(8,128)(2,1)} all-to-all(bf16[8,16,640]{2,1,0:T(8,128)(2,1)S(1)} %broadcast_in_dim.173), channel_id=1, replica_groups=mesh['seq'=8,'tp'=4] {'seq'}, dimensions={0} | all-to-all | bytes 327680 | tf_op jit(solution)/shard_map/all_to_all | solution.py:25
  97.3 1.5 %copy.215 = bf16[8,16,640]{1,2,0:T(8,128)(2,1)S(1)} copy(bf16[8,16,640]{2,1,0:T(8,128)(2,1)} %all_to_all.48) | data formatting | bytes 327680 | tf_op jit(solution)/shard_map/all_to_all | solution.py:25
  99.4 0.7 copy-done.11
  100.2 1.1 collective-permute-start.7
  101.7 2.3 %collective-permute-done.7 = f32[16,256]{1,0:T(8,128)S(1)} collective-permute-done((f32[16,256]{1,0:T(8,128)S(1)}, f32[16,256]{1,0:T(8,128)S(1)}, u32[]{:S(2)}, u32[]{:S(2)}) %collective-permute-start.7) | collective-permute-done | bytes 16416 | tf_op jit(solution)/shard_map/ppermute | solution.py:32
  104.0 0.5 collective-permute-done.6
  105.3 10.0 %all_to_all.49 = bf16[8,16,640]{2,1,0:T(8,128)(2,1)S(1)} all-to-all(bf16[8,16,640]{2,1,0:T(8,128)(2,1)S(1)} %maximum_bitcast_fusion.1), channel_id=1, replica_groups=mesh['seq'=8,'tp'=4] {'seq'}, dimensions={0} | all-to-all | bytes 327680 | tf_op jit(solution)/shard_map/all_to_all | solution.py:25
  115.6 9.3 %all_to_all.50 = bf16[8,16,256]{2,1,0:T(8,128)(2,1)S(1)} all-to-all(bf16[8,16,256]{2,1,0:T(8,128)(2,1)S(1)} %broadcast_in_dim.175), channel_id=1, replica_groups=mesh['seq'=8,'tp'=4] {'seq'}, dimensions={0} | all-to-all | bytes 131072 | tf_op jit(solution)/shard_map/all_to_all | solution.py:25
  124.9 1.5 %fusion.4 = f32[16,256]{1,0:T(8,128)S(1)} fusion(bf16[16,2048]{1,0:T(8,128)(2,1)S(1)} %bitcast.209, bf16[2,2048,256]{2,1,0:T(8,128)(2,1)} %param.21), kind=kOutput, calls=%fused_computation.20 | convolution fusion | flops 16777216 | bytes 1130496 | tf_op jit(solution)/shard_map/dot_general | solution.py:172
  126.4 1.0 collective-permute-start.10
  127.6 0.8 pad_maximum_fusion.1
  128.5 1.7 %collective-permute-done.10 = f32[16,256]{1,0:T(8,128)S(1)} collective-permute-done((f32[16,256]{1,0:T(8,128)S(1)}, f32[16,256]{1,0:T(8,128)S(1)}, u32[]{:S(2)}, u32[]{:S(2)}) %collective-permute-start.10) | collective-permute-done | bytes 16416 | tf_op jit(solution)/shard_map/ppermute | solution.py:32
  130.2 0.4 collective-permute-done.9
  130.6 0.6 broadcast_in_dim.176
  131.2 3.4 %all-to-all-start.8 = ((bf16[8,16,256]{2,1,0:T(8,128)(2,1)}), bf16[8,16,256]{2,1,0:T(8,128)(2,1)S(1)}, u32[]{:S(2)}, u32[]{:S(2)}) async-start(bf16[8,16,256]{2,1,0:T(8,128)(2,1)} %broadcast_in_dim.176), calls=%async_computation.8 | async-start | bytes 131072 | tf_op jit(solution)/shard_map/all_to_all | solution.py:25
  134.6 0.8 pad_maximum_fusion
  135.4 6.0 %all-to-all-done.8 = bf16[8,16,256]{2,1,0:T(8,128)(2,1)S(1)} async-done(((bf16[8,16,256]{2,1,0:T(8,128)(2,1)}), bf16[8,16,256]{2,1,0:T(8,128)(2,1)S(1)}, u32[]{:S(2)}, u32[]{:S(2)}) %all-to-all-start.8) | async-done | bytes 65568 | tf_op jit(solution)/shard_map/all_to_all | solution.py:25
  141.4 0.6 copy.255
  (165 shorter events, 10.6 us)
Async XLA Ops:
  0.6 14.0 %slice-start = ((bf16[2,16,64,128]{3,2,1,0:T(8,128)(2,1)}), bf16[1,16,64,128]{3,2,1,0:T(8,128)(2,1)S(1)}, s32[]{:S(2)}) async-start(bf16[2,16,64,128]{3,2,1,0:T(8,128)(2,1)} %param.23), calls=%async_computation.9 | async-start | bytes 524288 | tf_op jit(solution)/shard_map/slice | solution.py:109
  0.6 14.2 %copy-start.14 = (s32[16]{0:T(128)S(1)}, s32[16]{0:T(128)}, u32[]{:S(2)}) copy-start(s32[16]{0:T(128)} %param.13) | copy-start | bytes 196
  5.5 15.7 %all-to-all-start = ((bf16[8,16,896]{2,1,0:T(8,128)(2,1)}), bf16[8,16,896]{2,1,0:T(8,128)(2,1)S(1)}, u32[]{:S(2)}, u32[]{:S(2)}) async-start(bf16[8,16,896]{2,1,0:T(8,128)(2,1)} %broadcast_in_dim.159), calls=%async_computation | async-start | bytes 458752 | tf_op jit(solution)/shard_map/all_to_all | solution.py:25
  35.5 1.0 copy-start.10
  35.5 6.9 %copy-start = (bf16[2,256,2048]{2,1,0:T(8,128)(2,1)S(1)}, bf16[2,256,2048]{2,1,0:T(8,128)(2,1)}, u32[]{:S(2)}) copy-start(bf16[2,256,2048]{2,1,0:T(8,128)(2,1)} %param.20) | copy-start | bytes 6291460
  36.7 1.8 %collective-permute-start.2 = (f32[16,256]{1,0:T(8,128)S(1)}, f32[16,256]{1,0:T(8,128)S(1)}, u32[]{:S(2)}, u32[]{:S(2)}) collective-permute-start(f32[16,256]{1,0:T(8,128)S(1)} %fusion.25), channel_id=1, source_target_pairs={{0,3},{1,0},{2,1},{3,2},{4,7},{5,4},{6,5},{7,6},{8,11},{9,8},{10,9... | collective-permute-start | bytes 49160 | tf_op jit(solution)/shard_map/ppermute | solution.py:32
  36.7 3.8 %collective-permute-start.1 = (f32[16,256]{1,0:T(8,128)S(1)}, f32[16,256]{1,0:T(8,128)S(1)}, u32[]{:S(2)}, u32[]{:S(2)}) collective-permute-start(f32[16,256]{1,0:T(8,128)S(1)} %fusion.25), channel_id=1, source_target_pairs={{0,2},{1,3},{2,0},{3,1},{4,6},{5,7},{6,4},{7,5},{8,10},{9,11},{10,... | collective-permute-start | bytes 49160 | tf_op jit(solution)/shard_map/ppermute | solution.py:32
  38.3 3.2 %collective-permute-start = (f32[16,256]{1,0:T(8,128)S(1)}, f32[16,256]{1,0:T(8,128)S(1)}, u32[]{:S(2)}, u32[]{:S(2)}) collective-permute-start(f32[16,256]{1,0:T(8,128)S(1)} %fusion.25), channel_id=1, source_target_pairs={{0,1},{1,2},{2,3},{3,0},{4,5},{5,6},{6,7},{7,4},{8,9},{9,10},{10,1... | collective-permute-start | bytes 49160 | tf_op jit(solution)/shard_map/ppermute | solution.py:32
  42.4 21.5 %copy-start.2 = (bf16[2,2048,256]{2,1,0:T(8,128)(2,1)S(1)}, bf16[2,2048,256]{2,1,0:T(8,128)(2,1)}, u32[]{:S(2)}) copy-start(bf16[2,2048,256]{2,1,0:T(8,128)(2,1)} %param.21) | copy-start | bytes 6291460
  42.6 25.6 %copy-start.12 = (bf16[2,256,128]{2,1,0:T(8,128)(2,1)S(1)}, bf16[2,256,128]{2,1,0:T(8,128)(2,1)}, u32[]{:S(2)}) copy-start(bf16[2,256,128]{2,1,0:T(8,128)(2,1)} %param.17) | copy-start | bytes 393220
  42.6 25.7 %copy-start.13 = (bf16[2,256,128]{2,1,0:T(8,128)(2,1)S(1)}, bf16[2,256,128]{2,1,0:T(8,128)(2,1)}, u32[]{:S(2)}) copy-start(bf16[2,256,128]{2,1,0:T(8,128)(2,1)} %param.16) | copy-start | bytes 393220
  42.7 25.9 %copy-start.9 = (bf16[2,256,512]{2,1,0:T(8,128)(2,1)S(1)}, bf16[2,256,512]{2,1,0:T(8,128)(2,1)}, u32[]{:S(2)}) copy-start(bf16[2,256,512]{2,1,0:T(8,128)(2,1)} %param.15) | copy-start | bytes 1572868
  54.3 27.6 %copy-start.3 = (bf16[2,16,64,128]{3,2,1,0:T(8,128)(2,1)S(1)}, bf16[2,16,64,128]{3,2,1,0:T(8,128)(2,1)}, u32[]{:S(2)}) copy-start(bf16[2,16,64,128]{3,2,1,0:T(8,128)(2,1)} %param.23) | copy-start | bytes 1572868
  54.3 27.6 %copy-start.4 = (bf16[2,16,64,128]{3,2,1,0:T(8,128)(2,1)S(1)}, bf16[2,16,64,128]{3,2,1,0:T(8,128)(2,1)}, u32[]{:S(2)}) copy-start(bf16[2,16,64,128]{3,2,1,0:T(8,128)(2,1)} %param.22) | copy-start | bytes 1572868
  64.2 1.5 %collective-permute-start.5 = (f32[16,256]{1,0:T(8,128)S(1)}, f32[16,256]{1,0:T(8,128)S(1)}, u32[]{:S(2)}, u32[]{:S(2)}) collective-permute-start(f32[16,256]{1,0:T(8,128)S(1)} %fusion.8), channel_id=1, source_target_pairs={{0,3},{1,0},{2,1},{3,2},{4,7},{5,4},{6,5},{7,6},{8,11},{9,8},{10,9... | collective-permute-start | bytes 49160 | tf_op jit(solution)/shard_map/ppermute | solution.py:32
  64.2 3.8 %collective-permute-start.4 = (f32[16,256]{1,0:T(8,128)S(1)}, f32[16,256]{1,0:T(8,128)S(1)}, u32[]{:S(2)}, u32[]{:S(2)}) collective-permute-start(f32[16,256]{1,0:T(8,128)S(1)} %fusion.8), channel_id=1, source_target_pairs={{0,2},{1,3},{2,0},{3,1},{4,6},{5,7},{6,4},{7,5},{8,10},{9,11},{10,... | collective-permute-start | bytes 49160 | tf_op jit(solution)/shard_map/ppermute | solution.py:32
  64.9 3.2 %collective-permute-start.3 = (f32[16,256]{1,0:T(8,128)S(1)}, f32[16,256]{1,0:T(8,128)S(1)}, u32[]{:S(2)}, u32[]{:S(2)}) collective-permute-start(f32[16,256]{1,0:T(8,128)S(1)} %fusion.8), channel_id=1, source_target_pairs={{0,1},{1,2},{2,3},{3,0},{4,5},{5,6},{6,7},{7,4},{8,9},{9,10},{10,1... | collective-permute-start | bytes 49160 | tf_op jit(solution)/shard_map/ppermute | solution.py:32
  69.5 11.4 %all-to-all-start.4 = ((bf16[8,16,896]{2,1,0:T(8,128)(2,1)}), bf16[8,16,896]{2,1,0:T(8,128)(2,1)S(1)}, u32[]{:S(2)}, u32[]{:S(2)}) async-start(bf16[8,16,896]{2,1,0:T(8,128)(2,1)} %broadcast_in_dim.169), calls=%async_computation.4 | async-start | bytes 458752 | tf_op jit(solution)/shard_map/all_to_all | solution.py:25
  99.0 1.0 copy-start.11
  99.1 5.8 %copy-start.1 = (bf16[2,256,2048]{2,1,0:T(8,128)(2,1)S(1)}, bf16[2,256,2048]{2,1,0:T(8,128)(2,1)}, u32[]{:S(2)}) copy-start(bf16[2,256,2048]{2,1,0:T(8,128)(2,1)} %param.19) | copy-start | bytes 6291460
  100.2 1.5 %collective-permute-start.8 = (f32[16,256]{1,0:T(8,128)S(1)}, f32[16,256]{1,0:T(8,128)S(1)}, u32[]{:S(2)}, u32[]{:S(2)}) collective-permute-start(f32[16,256]{1,0:T(8,128)S(1)} %fusion.22), channel_id=1, source_target_pairs={{0,3},{1,0},{2,1},{3,2},{4,7},{5,4},{6,5},{7,6},{8,11},{9,8},{10,9... | collective-permute-start | bytes 49160 | tf_op jit(solution)/shard_map/ppermute | solution.py:32
  100.2 3.8 %collective-permute-start.7 = (f32[16,256]{1,0:T(8,128)S(1)}, f32[16,256]{1,0:T(8,128)S(1)}, u32[]{:S(2)}, u32[]{:S(2)}) collective-permute-start(f32[16,256]{1,0:T(8,128)S(1)} %fusion.22), channel_id=1, source_target_pairs={{0,2},{1,3},{2,0},{3,1},{4,6},{5,7},{6,4},{7,5},{8,10},{9,11},{10,... | collective-permute-start | bytes 49160 | tf_op jit(solution)/shard_map/ppermute | solution.py:32
  101.3 3.2 %collective-permute-start.6 = (f32[16,256]{1,0:T(8,128)S(1)}, f32[16,256]{1,0:T(8,128)S(1)}, u32[]{:S(2)}, u32[]{:S(2)}) collective-permute-start(f32[16,256]{1,0:T(8,128)S(1)} %fusion.22), channel_id=1, source_target_pairs={{0,1},{1,2},{2,3},{3,0},{4,5},{5,6},{6,7},{7,4},{8,9},{9,10},{10,1... | collective-permute-start | bytes 49160 | tf_op jit(solution)/shard_map/ppermute | solution.py:32
  104.9 22.7 %copy-start.7 = (bf16[1,16,64,128]{3,2,1,0:T(8,128)(2,1)S(1)}, bf16[1,16,64,128]{3,2,1,0:T(8,128)(2,1)}, u32[]{:S(2)}) copy-start(bf16[1,16,64,128]{3,2,1,0:T(8,128)(2,1)} %get-tuple-element.13) | copy-start | bytes 786436
  104.9 22.7 %copy-start.8 = (bf16[1,16,64,128]{3,2,1,0:T(8,128)(2,1)S(1)}, bf16[1,16,64,128]{3,2,1,0:T(8,128)(2,1)}, u32[]{:S(2)}) copy-start(bf16[1,16,64,128]{3,2,1,0:T(8,128)(2,1)} %get-tuple-element.14) | copy-start | bytes 786436
  105.1 29.4 %copy-start.5 = (bf16[1,16,64,128]{3,2,1,0:T(8,128)(2,1)S(1)}, bf16[1,16,64,128]{3,2,1,0:T(8,128)(2,1)}, u32[]{:S(2)}) copy-start(bf16[1,16,64,128]{3,2,1,0:T(8,128)(2,1)} %get-tuple-element.42) | copy-start | bytes 786436
  105.2 29.4 %copy-start.6 = (bf16[1,16,64,128]{3,2,1,0:T(8,128)(2,1)S(1)}, bf16[1,16,64,128]{3,2,1,0:T(8,128)(2,1)}, u32[]{:S(2)}) copy-start(bf16[1,16,64,128]{3,2,1,0:T(8,128)(2,1)} %get-tuple-element.43) | copy-start | bytes 786436
  126.4 2.1 %collective-permute-start.11 = (f32[16,256]{1,0:T(8,128)S(1)}, f32[16,256]{1,0:T(8,128)S(1)}, u32[]{:S(2)}, u32[]{:S(2)}) collective-permute-start(f32[16,256]{1,0:T(8,128)S(1)} %fusion.4), channel_id=1, source_target_pairs={{0,3},{1,0},{2,1},{3,2},{4,7},{5,4},{6,5},{7,6},{8,11},{9,8},{10,9... | collective-permute-start | bytes 49160 | tf_op jit(solution)/shard_map/ppermute | solution.py:32
  126.4 3.8 %collective-permute-start.10 = (f32[16,256]{1,0:T(8,128)S(1)}, f32[16,256]{1,0:T(8,128)S(1)}, u32[]{:S(2)}, u32[]{:S(2)}) collective-permute-start(f32[16,256]{1,0:T(8,128)S(1)} %fusion.4), channel_id=1, source_target_pairs={{0,2},{1,3},{2,0},{3,1},{4,6},{5,7},{6,4},{7,5},{8,10},{9,11},{10,... | collective-permute-start | bytes 49160 | tf_op jit(solution)/shard_map/ppermute | solution.py:32
  127.4 3.2 %collective-permute-start.9 = (f32[16,256]{1,0:T(8,128)S(1)}, f32[16,256]{1,0:T(8,128)S(1)}, u32[]{:S(2)}, u32[]{:S(2)}) collective-permute-start(f32[16,256]{1,0:T(8,128)S(1)} %fusion.4), channel_id=1, source_target_pairs={{0,1},{1,2},{2,3},{3,0},{4,5},{5,6},{6,7},{7,4},{8,9},{9,10},{10,1... | collective-permute-start | bytes 49160 | tf_op jit(solution)/shard_map/ppermute | solution.py:32
  131.2 10.2 %all-to-all-start.8 = ((bf16[8,16,256]{2,1,0:T(8,128)(2,1)}), bf16[8,16,256]{2,1,0:T(8,128)(2,1)S(1)}, u32[]{:S(2)}, u32[]{:S(2)}) async-start(bf16[8,16,256]{2,1,0:T(8,128)(2,1)} %broadcast_in_dim.176), calls=%async_computation.8 | async-start | bytes 131072 | tf_op jit(solution)/shard_map/all_to_all | solution.py:25

commit v2 on v1

--- a/solution.py
+++ b/solution.py
@@ -1,8 +1,11 @@
+import functools
 import math
 
 import jax
 import jax.numpy as jnp
 from jax import lax
+from jax.experimental import pallas as pl
+from jax.experimental.pallas import tpu as pltpu
 from jax.sharding import PartitionSpec as P
 
 HEAD_DIM = 64
@@ -25,7 +28,7 @@
     return lax.all_to_all(chunks, "seq", 0, 0)
 
 
-def make_per_device(n_seq, n_tp):
+def make_plain(n_seq, n_tp):
     def tp_sum(part):
         total = part
         for k in range(1, n_tp):
@@ -179,9 +182,387 @@
     return per_device
 
 
+LANES = 128
+VMEM_ROOM = 8 << 20
+
+
+def lane_ids(shape):
+    return lax.broadcasted_iota(jnp.int32, shape, len(shape) - 1)
+
+
+def as_hi_lo(value, lane):
+    wide = jnp.broadcast_to(value, lane.shape)
+    high = wide.astype(jnp.bfloat16).astype(jnp.float32)
+    return jnp.where(lane == 0, high, jnp.where(lane == 1, wide - high, 0.0)).astype(jnp.bfloat16)
+
+
+def square_sum(own):
+    wide = own.astype(jnp.float32)
+    return jnp.sum(wide * wide, axis=1, keepdims=True)
+
+
+def dot32(a, b):
+    return jnp.dot(a, b, preferred_element_type=jnp.float32)
+
+
+def call(body, out_shape, *args, name):
+    vmem = pl.BlockSpec(memory_space=pltpu.VMEM)
+    single = not isinstance(out_shape, (tuple, list))
+    return pl.pallas_call(
+        body,
+        out_shape=out_shape,
+        in_specs=[vmem] * len(args),
+        out_specs=vmem if single else [vmem] * len(out_shape),
+        compiler_params=pltpu.CompilerParams(vmem_limit_bytes=VMEM_ROOM),
+        name=name,
+    )(*[pltpu.with_memory_space_constraint(a, pltpu.VMEM) for a in args])
+
+
+def project_body(layer, own, wq_ref, wk_ref, wv_ref, out_ref):
+    part = [dot32(own, w[layer]).astype(jnp.bfloat16) for w in (wq_ref, wk_ref, wv_ref)]
+    lane = lane_ids((own.shape[0], LANES))
+    part.append(as_hi_lo(square_sum(own), lane))
+    for member in range(out_ref.shape[0]):
+        at = 0
+        for piece in part:
+            out_ref[member, :, at : at + piece.shape[1]] = piece
+            at += piece.shape[1]
+
+
+def first_kernel(own_ref, wq_ref, wk_ref, wv_ref, out_ref):
+    project_body(0, own_ref[...], wq_ref, wk_ref, wv_ref, out_ref)
+
+
+def sum_parts(base_ref, part_refs):
+    total = part_refs[0][...]
+    for ref in part_refs[1:]:
+        total = total + ref[...]
+    return (base_ref[...].astype(jnp.float32) + total).astype(jnp.bfloat16)
+
+
+def next_kernel(layer, n_parts, *refs):
+    base_ref, parts = refs[0], refs[1 : 1 + n_parts]
+    wq_ref, wk_ref, wv_ref, own_ref, out_ref = refs[1 + n_parts :]
+    own = sum_parts(base_ref, parts)
+    own_ref[...] = own
+    project_body(layer, own, wq_ref, wk_ref, wv_ref, out_ref)
+
+
+def last_kernel(n_parts, *refs):
+    base_ref, parts, out_ref = refs[0], refs[1 : 1 + n_parts], refs[1 + n_parts]
+    own = sum_parts(base_ref, parts)
+    for member in range(out_ref.shape[0]):
+        out_ref[member] = own
+
+
+def attend_kernel(
+    layer, width, heads, kv_heads, got_ref, cos_ref, sin_ref, first_ref, last_ref, fresh_ref,
+    key_ref, value_ref, out_ref, key_new_ref, value_new_ref,
+):
+    members, requests, _ = got_ref.shape
+    query_width = heads * HEAD_DIM
+    repeat = heads // kv_heads
+    block = key_ref.shape[2]
+
+    def summed(at):
+        total = got_ref[0, :, at : at + LANES].astype(jnp.float32)
+        for member in range(1, members):
+            total = total + got_ref[member, :, at : at + LANES].astype(jnp.float32)
+        return total
+
+    lane = lane_ids((requests, LANES))
+    low = lane < HEAD_DIM
+    side = summed(query_width + 2 * kv_heads * HEAD_DIM)
+    spread = (side[:, 0:1] + side[:, 1:2]) * (1.0 / width)
+    inv = lax.rsqrt(spread + eps_norm)
+    cosine = cos_ref[...]
+    sine = sin_ref[...]
+    half = HEAD_DIM // 2
+
+    def rotated(at):
+        x = summed(at) * inv
+        other = jnp.where(
+            lane % HEAD_DIM < half, pltpu.roll(x, LANES - half, 1), pltpu.roll(x, half, 1)
+        )
+        return x * cosine + other * sine
+
+    stacked = []
+    for pair in range(heads // 2):
+        x = rotated(pair * LANES)
+        turned = pltpu.roll(x, HEAD_DIM, 1)
+        if 2 * pair // repeat == 0:
+            stacked += [jnp.where(low, x, 0.0), jnp.where(low, turned, 0.0)]
+        else:
+            stacked += [jnp.where(low, 0.0, turned), jnp.where(low, 0.0, x)]
+    query = jnp.concatenate(stacked, axis=0).astype(jnp.bfloat16)
+    key_new = rotated(query_width).astype(jnp.bfloat16)
+    value_new = (summed(query_width + LANES) * inv).astype(jnp.bfloat16)
+    key_new_ref[...] = key_new
+    value_new_ref[...] = value_new
+
+    fresh = fresh_ref[...] > 0
+    keys = []
+    values = []
+    for b in range(requests):
+        here = fresh[b * block : (b + 1) * block]
+        k = key_ref[layer, b].astype(jnp.float32)
+        v = value_ref[layer, b].astype(jnp.float32)
+        keys.append(jnp.where(here, key_new[b : b + 1].astype(jnp.float32), k).astype(jnp.bfloat16))
+        values.append(
+            jnp.where(here, value_new[b : b + 1].astype(jnp.float32), v).astype(jnp.bfloat16)
+        )
+    keys = jnp.concatenate(keys, axis=0)
+    values = jnp.concatenate(values, axis=0)
+    scores = lax.dot_general(
+        query, keys, (((1,), (1,)), ((), ())), preferred_element_type=jnp.float32
+    ) * (1.0 / math.sqrt(HEAD_DIM))
+    column = lane_ids(scores.shape)
+    live = (column >= first_ref[...]) & (column < last_ref[...])
+    scores = jnp.where(live, scores, neg_fill)
+    top = jnp.max(scores, axis=1, keepdims=True)
+    weights = jnp.where(live, jnp.exp(scores - top), 0.0)
+    sums = jnp.sum(weights, axis=1, keepdims=True)
+    acc = dot32(weights.astype(jnp.bfloat16), values)
+    turned = pltpu.roll(acc, HEAD_DIM, 1)
+
+    side = jnp.zeros((requests, LANES), jnp.float32)
+    for h in range(heads):
+        rows = slice(h * requests, (h + 1) * requests)
+        for group in range(5):
+            side = jnp.where(lane == group * heads + h, (top if group < 3 else sums)[rows], side)
+    one = side.astype(jnp.bfloat16).astype(jnp.float32)
+    two = (side - one).astype(jnp.bfloat16).astype(jnp.float32)
+    three = side - one - two
+    second = ((lane >= heads) & (lane < 2 * heads)) | (lane >= 4 * heads)
+    third = (lane >= 2 * heads) & (lane < 3 * heads)
+    side = jnp.where(third, three, jnp.where(second, two, one)).astype(jnp.bfloat16)
+    pieces = []
+    for pair in range(heads // 2):
+        even = slice(2 * pair * requests, (2 * pair + 1) * requests)
+        odd = slice((2 * pair + 1) * requests, (2 * pair + 2) * requests)
+        if 2 * pair // repeat == 0:
+            pieces.append(jnp.where(low, acc[even], turned[odd]).astype(jnp.bfloat16))
+        else:
+            pieces.append(jnp.where(low, turned[even], acc[odd]).astype(jnp.bfloat16))
+    pieces.append(side)
+    for member in range(members):
+        for i, piece in enumerate(pieces):
+            out_ref[member, :, i * LANES : (i + 1) * LANES] = piece
+
+
+def combine_kernel(layer, heads, got_ref, w_ref, out_ref):
+    members, requests, _ = got_ref.shape
+    query_width = heads * HEAD_DIM
+    low = lane_ids((requests, LANES)) < HEAD_DIM
+    sides = [
+        got_ref[m, :, query_width : query_width + LANES].astype(jnp.float32) for m in range(members)
+    ]
+    tops = [
+        s[:, :heads] + s[:, heads : 2 * heads] + s[:, 2 * heads : 3 * heads] for s in sides
+    ]
+    sums = [s[:, 3 * heads : 4 * heads] + s[:, 4 * heads : 5 * heads] for s in sides]
+    top = tops[0]
+    for t in tops[1:]:
+        top = jnp.maximum(top, t)
+    factors = [jnp.exp(t - top) for t in tops]
+    total = factors[0] * sums[0]
+    for f, s in zip(factors[1:], sums[1:]):
+        total = total + f * s
+
+    def spread(column, pair):
+        return jnp.where(low, column[:, 2 * pair : 2 * pair + 1], column[:, 2 * pair + 1 : 2 * pair + 2])
+
+    attended = []
+    for pair in range(heads // 2):
+        acc = jnp.zeros((requests, LANES), jnp.float32)
+        for m in range(members):
+            piece = got_ref[m, :, pair * LANES : (pair + 1) * LANES].astype(jnp.float32)
+            acc = acc + piece * spread(factors[m], pair)
+        attended.append((acc / spread(total, pair)).astype(jnp.bfloat16))
+    out_ref[...] = dot32(jnp.concatenate(attended, axis=1), w_ref[layer])
+
+
+def widen_kernel(layer, n_parts, *refs):
+    base_ref, parts = refs[0], refs[1 : 1 + n_parts]
+    gate_ref, up_ref, mid_ref, out_ref = refs[1 + n_parts :]
+    mid = sum_parts(base_ref, parts)
+    mid_ref[...] = mid
+    side = as_hi_lo(square_sum(mid), lane_ids((mid.shape[0], LANES)))
+    members = out_ref.shape[0]
+    own = gate_ref.shape[2] // members
+    for member in range(members):
+        cols = slice(member * own, (member + 1) * own)
+        out_ref[member, :, :own] = dot32(mid, gate_ref[layer, :, cols]).astype(jnp.bfloat16)
+        out_ref[member, :, own : 2 * own] = dot32(mid, up_ref[layer, :, cols]).astype(jnp.bfloat16)
+        out_ref[member, :, 2 * own :] = side
+
+
+def silu_kernel(width, got_ref, out_ref):
+    members, _, span = got_ref.shape
+    own = (span - LANES) // 2
+    total = got_ref[0].astype(jnp.float32)
+    for member in range(1, members):
+        total = total + got_ref[member].astype(jnp.float32)
+    spread = (total[:, 2 * own : 2 * own + 1] + total[:, 2 * own + 1 : 2 * own + 2]) * (1.0 / width)
+    inv = lax.rsqrt(spread + eps_norm)
+    gate = total[:, :own] * inv
+    hidden = (gate / (1.0 + jnp.exp(-gate)) * (total[:, own : 2 * own] * inv)).astype(jnp.bfloat16)
+    for member in range(members):
+        out_ref[member] = hidden
+
+
+def down_kernel(layer, got_ref, w_ref, out_ref):
+    hidden = jnp.concatenate([got_ref[m] for m in range(got_ref.shape[0])], axis=1)
+    out_ref[...] = dot32(hidden, w_ref[layer])
+
+
+def make_with_kernels(n_seq, n_tp):
+    def tp_parts(part):
+        return [part] + [
+            lax.ppermute(part, "tp", [(i, (i + k) % n_tp) for i in range(n_tp)])
+            for k in range(1, n_tp)
+        ]
+
+    def per_device(
+        hidden_in,
+        lengths,
+        positions,
+        query_weight,
+        key_weight,
+        value_weight,
+        out_weight,
+        gate_weight,
+        up_weight,
+        down_weight,
+        key_cache,
+        value_cache,
+    ):
+        seq_index = lax.axis_index("seq")
+        requests, width = hidden_in.shape
+        col_count = out_weight.shape[2]
+        block_len = key_cache.shape[2]
+        kv_width = key_cache.shape[3]
+        query_width = query_weight.shape[2]
+        heads = query_width // HEAD_DIM
+        kv_heads = kv_width // HEAD_DIM
+        ff_own = gate_weight.shape[2] // n_seq
+        bf16, f32 = jnp.bfloat16, jnp.float32
+
+        def shape(dims, kind):
+            return pltpu.VMEM(dims, kind)
+
+        slots = seq_index * block_len + jnp.arange(block_len, dtype=jnp.int32)
+        new_slot = slots[None, :] == lengths[:, None]
+        fresh = new_slot.astype(jnp.int32).reshape(requests * block_len, 1)
+        row_request = jnp.arange(heads * requests, dtype=jnp.int32) % requests
+        first = row_request * block_len
+        count = jnp.clip(lengths + 1 - seq_index * block_len, 0, block_len)
+        last = first + jnp.tile(count, heads)
+        half = HEAD_DIM // 2
+        inverse = 500000.0 ** (-(2.0 * jnp.arange(half, dtype=jnp.float32)) / HEAD_DIM)
+        angles = positions.astype(jnp.float32)[:, None] * inverse[None, :]
+        cosine = jnp.cos(angles)
+        sine = jnp.sin(angles)
+        cosine = jnp.tile(cosine, (1, LANES // half))
+        sine = jnp.tile(jnp.concatenate([-sine, sine], axis=1), (1, LANES // HEAD_DIM))
+
+        own = lax.dynamic_slice_in_dim(hidden_in, seq_index * col_count, col_count, 1)
+        packed_shape = shape((n_seq, requests, query_width + 2 * kv_width + LANES), bf16)
+        part_shape = shape((requests, col_count), f32)
+        own_shape = shape((requests, col_count), bf16)
+        new_shape = shape((requests, kv_width), bf16)
+        key_layers = []
+        value_layers = []
+        parts = None
+        mid = None
+        for layer in range(LAYERS):
+            weights = (query_weight, key_weight, value_weight)
+            if parts is None:
+                packed = call(first_kernel, packed_shape, own, *weights, name="first")
+            else:
+                own, packed = call(
+                    functools.partial(next_kernel, layer, n_tp),
+                    (own_shape, packed_shape),
+                    mid,
+                    *parts,
+                    *weights,
+                    name="next",
+                )
+            packed, key_new, value_new = call(
+                functools.partial(attend_kernel, layer, width, heads, kv_heads),
+                (shape((n_seq, requests, query_width + LANES), bf16), new_shape, new_shape),
+                seq_swap(packed),
+                cosine,
+                sine,
+                first[:, None],
+                last[:, None],
+                fresh,
+                key_cache,
+                value_cache,
+                name="attend",
+            )
+            key_layers.append(jnp.where(new_slot[:, :, None], key_new[:, None, :], key_cache[layer]))
+            value_layers.append(
+                jnp.where(new_slot[:, :, None], value_new[:, None, :], value_cache[layer])
+            )
+            part = call(
+                functools.partial(combine_kernel, layer, heads),
+                part_shape,
+                seq_swap(packed),
+                out_weight,
+                name="combine",
+            )
+            mid, packed = call(
+                functools.partial(widen_kernel, layer, n_tp),
+                (own_shape, shape((n_seq, requests, 2 * ff_own + LANES), bf16)),
+                own,
+                *tp_parts(part),
+                gate_weight,
+                up_weight,
+                name="widen",
+            )
+            hidden = call(
+                functools.partial(silu_kernel, width),
+                shape((n_seq, requests, ff_own), bf16),
+                seq_swap(packed),
+                name="silu",
+            )
+            part = call(
+                functools.partial(down_kernel, layer),
+                part_shape,
+                seq_swap(hidden),
+                down_weight,
+                name="down",
+            )
+            parts = tp_parts(part)
+        stream = call(
+            functools.partial(last_kernel, n_tp),
+            shape((n_seq, requests, col_count), bf16),
+            mid,
+            *parts,
+            name="last",
+        )
+        stream = seq_swap(stream).transpose(1, 0, 2).reshape(requests, width)
+        return (stream, jnp.stack(key_layers), jnp.stack(value_layers))
+
+    return per_device
+
+
 def solution(mesh):
+    n_seq, n_tp = mesh.shape["seq"], mesh.shape["tp"]
+
+    def per_device(*args):
+        gate_weight, key_cache = args[7], args[10]
+        aligned = (
+            args[6].shape[2] % LANES == 0
+            and gate_weight.shape[2] // n_seq % LANES == 0
+            and key_cache.shape[3] == LANES
+        )
+        make = make_with_kernels if aligned else make_plain
+        return make(n_seq, n_tp)(*args)
+
     return jax.shard_map(
-        make_per_device(mesh.shape["seq"], mesh.shape["tp"]),
+        per_device,
         mesh=mesh,
         in_specs=(
             P(),

time: 143 us -> 131 us (0.916)
  matrix products: 9.72 us -> 0 us
  Pallas kernels: 0 us -> 6.77 us
  waiting for transfers between devices: 31 us -> 25.1 us
  local copies, waits for them, and re-layouts: 12.1 us -> 10 us
  other arithmetic: 8.82 us -> 6.75 us
  blocking collectives: 60 us -> 61.8 us
    dot_general x18 -> x0, matrix products: 9.72 us -> none  [the longest x6 3.5 us: per_device(): jnp.dot(own, w[layer], preferred_element_type=jnp.float32)]
    pallas_call x0 -> x13, Pallas kernels: none -> 6.77 us  [call(): pl.pallas_call(body, out_shape=out_shape, in_specs=[vmem] * len(args), ou...]
    all_to_all x3, waiting for transfers between devices: 19.9 us -> 14 us  [seq_swap(): return lax.all_to_all(chunks, 'seq', 0, 0)]
    unnamed x32 -> x46, local copies, waits for them, and re-layouts: 1.61 us -> 7.2 us
    reduce_sum x14 -> x0, other arithmetic: 2.98 us -> none  [the longest x4 1.91 us: stats_of(): return jnp.sum(f * f, axis=-1, keepdims=True)]
    broadcast_in_dim x11 -> x0, local copies, waits for them, and re-layouts: 2.28 us -> none  [the longest x4 1.46 us: per_device(): got = seq_swap(jnp.broadcast_to(packed[None], (n_seq,) + packed.shape))]
    all_to_all x2 -> x0, local copies, waits for them, and re-layouts: 2.07 us -> none  [seq_swap(): return lax.all_to_all(chunks, 'seq', 0, 0)]
    squeeze x4 -> x0, local copies, waits for them, and re-layouts: 1.92 us -> none  [the longest x2 1.43 us: per_device(): value_rows = jnp.where(new_slot, value_new[:, None, :], value_cache[layer])]
  transfers between devices with their start and end apart: 15 -> 15, of which waited for: 13 -> 13; matrix products, arithmetic and copies ran while one was open for 3% -> 7% of each run, Pallas kernels for 0% -> 0%
where the time goes in v2:
time: 131 us; the launch traced here: 130 us
  blocking collectives  61.8 us (47%)
  waiting for transfers between devices  25.1 us (19%)
  starting transfers between devices  19.2 us (15%)
  local copies, waits for them, and re-layouts  10 us (8%)
  Pallas kernels  6.77 us (5%)
  other arithmetic  6.75 us (5%)
    all_to_all x6, blocking collectives, seq_swap(): return lax.all_to_all(chunks, 'seq', 0, 0)  61.8 us
    all_to_all x3, waiting for transfers between devices, seq_swap(): return lax.all_to_all(chunks, 'seq', 0, 0)  14 us
    all_to_all x3, starting transfers between devices, seq_swap(): return lax.all_to_all(chunks, 'seq', 0, 0)  14 us
    ppermute x12, waiting for transfers between devices, tp_parts(): lax.ppermute(part, 'tp', [(i, (i + k) % n_tp) for i in range(n_tp)])  11.1 us
    unnamed x46, local copies, waits for them, and re-layouts  7.2 us
    pallas_call x13, Pallas kernels, call(): pl.pallas_call(body, out_shape=out_shape, in_specs=[vmem] * len(args), ou...  6.77 us
    ppermute x12, starting transfers between devices, tp_parts(): lax.ppermute(part, 'tp', [(i, (i + k) % n_tp) for i in range(n_tp)])  5.2 us
  transfers between devices with their start and end apart: 15, of which 13 were waited for; matrix products, arithmetic and copies ran while one was open for 7% of the time, Pallas kernels for 0%

profile of v2, /device:TPU:0, one launch (start us, length us, event | category | flops | bytes accessed | tf_op | source)
XLA Modules:
  0.0 130.3 jit_solution(14134549418979479174)
XLA Ops:
  0.7 0.8 copy-done
  1.5 1.0 copy-done.10
  2.5 0.9 copy-done.15
  3.4 0.9 copy-done.17
  4.3 0.9 first.1
  5.2 7.3 %all-to-all-start = ((bf16[8,16,896]{2,1,0:T(8,128)(2,1)}), bf16[8,16,896]{2,1,0:T(8,128)(2,1)S(1)}, u32[]{:S(2)}, u32[]{:S(2)}) async-start(bf16[8,16,896]{2,1,0:T(8,128)(2,1)} %first.1), calls=%async_computation | async-start | bytes 458752 | tf_op jit(solution)/shard_map/all_to_all | solution.py:28
  12.5 0.8 convert_element_type.16
  13.3 0.7 subtract_clamp_fusion
  14.3 0.7 tile.33
  15.0 0.7 broadcast_compare_fusion
  15.8 1.3 reshape.152.fresh_ref
  17.0 1.5 %fusion = (s32[128,1]{1,0:T(8,128)S(1)}, s32[128,1]{1,0:T(8,128)}) fusion(s32[128,1]{1,0:T(8,128)} %tile.33), kind=kLoop, calls=%fused_computation.7 | loop fusion | flops 1024 | bytes 1536 | tf_op jit(solution)/shard_map/mul | solution.py:458
  18.5 2.4 %all-to-all-done.got_ref = bf16[8,16,896]{2,1,0:T(8,128)(2,1)S(1)} async-done(((bf16[8,16,896]{2,1,0:T(8,128)(2,1)}), bf16[8,16,896]{2,1,0:T(8,128)(2,1)S(1)}, u32[]{:S(2)}, u32[]{:S(2)}) %all-to-all-start) | async-done | bytes 229408 | tf_op jit(solution)/shard_map/all_to_all | solution.py:28
  20.9 1.0 copy-done.8
  21.9 0.8 copy-done.13
  22.8 1.0 attend.2
  23.7 11.0 %all_to_all.45.got_ref = bf16[8,16,640]{2,1,0:T(8,128)(2,1)S(1)} all-to-all(bf16[8,16,640]{2,1,0:T(8,128)(2,1)S(1)} %get-tuple-element.15), channel_id=1, replica_groups=mesh['seq'=8,'tp'=4] {'seq'}, dimensions={0} | all-to-all | bytes 327680 | tf_op jit(solution)/shard_map/all_to_all | solution.py:28
  34.7 0.5 combine.2.refs_1_
  35.2 1.6 %collective-permute-start.1 = (f32[16,256]{1,0:T(8,128)S(1)}, f32[16,256]{1,0:T(8,128)S(1)}, u32[]{:S(2)}, u32[]{:S(2)}) collective-permute-start(f32[16,256]{1,0:T(8,128)S(1)} %combine.2.refs_1_), channel_id=1, source_target_pairs={{0,2},{1,3},{2,0},{3,1},{4,6},{5,7},{6,4},{7,5},{8,10},{9,11},{10,... | collective-permute-start | bytes 49160 | tf_op jit(solution)/shard_map/ppermute | solution.py:422
  37.0 2.0 %collective-permute-done.1.refs_3_ = f32[16,256]{1,0:T(8,128)S(1)} collective-permute-done((f32[16,256]{1,0:T(8,128)S(1)}, f32[16,256]{1,0:T(8,128)S(1)}, u32[]{:S(2)}, u32[]{:S(2)}) %collective-permute-start.1) | collective-permute-done | bytes 16416 | tf_op jit(solution)/shard_map/ppermute | solution.py:422
  39.0 0.9 collective-permute-done.refs_2_
  40.0 1.6 %copy-done.2 = bf16[2,256,2048]{2,1,0:T(8,128)(2,1)S(1)} copy-done((bf16[2,256,2048]{2,1,0:T(8,128)(2,1)S(1)}, bf16[2,256,2048]{2,1,0:T(8,128)(2,1)}, u32[]{:S(2)}) %copy-start.2) | copy-done | bytes 2097176
  42.0 10.1 %all_to_all.46.got_ref = bf16[8,16,640]{2,1,0:T(8,128)(2,1)S(1)} all-to-all(bf16[8,16,640]{2,1,0:T(8,128)(2,1)S(1)} %get-tuple-element.17), channel_id=1, replica_groups=mesh['seq'=8,'tp'=4] {'seq'}, dimensions={0} | all-to-all | bytes 327680 | tf_op jit(solution)/shard_map/all_to_all | solution.py:28
  52.3 9.3 %all_to_all.47.got_ref = bf16[8,16,256]{2,1,0:T(8,128)(2,1)S(1)} all-to-all(bf16[8,16,256]{2,1,0:T(8,128)(2,1)S(1)} %silu.2), channel_id=1, replica_groups=mesh['seq'=8,'tp'=4] {'seq'}, dimensions={0} | all-to-all | bytes 131072 | tf_op jit(solution)/shard_map/all_to_all | solution.py:28
  61.8 0.7 collective-permute-start.4
  62.7 0.5 collective-permute-done.5.refs_4_
  63.2 2.4 %collective-permute-done.4.refs_3_ = f32[16,256]{1,0:T(8,128)S(1)} collective-permute-done((f32[16,256]{1,0:T(8,128)S(1)}, f32[16,256]{1,0:T(8,128)S(1)}, u32[]{:S(2)}, u32[]{:S(2)}) %collective-permute-start.4) | collective-permute-done | bytes 16416 | tf_op jit(solution)/shard_map/ppermute | solution.py:422
  65.9 10.6 %all_to_all.48.got_ref = bf16[8,16,896]{2,1,0:T(8,128)(2,1)S(1)} all-to-all(bf16[8,16,896]{2,1,0:T(8,128)(2,1)S(1)} %get-tuple-element.19), channel_id=1, replica_groups=mesh['seq'=8,'tp'=4] {'seq'}, dimensions={0} | all-to-all | bytes 458752 | tf_op jit(solution)/shard_map/all_to_all | solution.py:28
  76.5 1.0 attend.3
  77.5 10.7 %all_to_all.49.got_ref = bf16[8,16,640]{2,1,0:T(8,128)(2,1)S(1)} all-to-all(bf16[8,16,640]{2,1,0:T(8,128)(2,1)S(1)} %get-tuple-element.20), channel_id=1, replica_groups=mesh['seq'=8,'tp'=4] {'seq'}, dimensions={0} | all-to-all | bytes 327680 | tf_op jit(solution)/shard_map/all_to_all | solution.py:28
  88.2 0.5 combine.3.refs_1_
  88.7 0.8 collective-permute-start.7
  89.6 0.5 collective-permute-done.8.refs_4_
  90.2 2.4 %collective-permute-done.7.refs_3_ = f32[16,256]{1,0:T(8,128)S(1)} collective-permute-done((f32[16,256]{1,0:T(8,128)S(1)}, f32[16,256]{1,0:T(8,128)S(1)}, u32[]{:S(2)}, u32[]{:S(2)}) %collective-permute-start.7) | collective-permute-done | bytes 16416 | tf_op jit(solution)/shard_map/ppermute | solution.py:422
  93.1 10.1 %all_to_all.50.got_ref = bf16[8,16,640]{2,1,0:T(8,128)(2,1)S(1)} all-to-all(bf16[8,16,640]{2,1,0:T(8,128)(2,1)S(1)} %get-tuple-element.22), channel_id=1, replica_groups=mesh['seq'=8,'tp'=4] {'seq'}, dimensions={0} | all-to-all | bytes 327680 | tf_op jit(solution)/shard_map/all_to_all | solution.py:28
  103.1 0.8 silu.3
  104.0 3.4 %all-to-all-start.7 = ((bf16[8,16,256]{2,1,0:T(8,128)(2,1)}), bf16[8,16,256]{2,1,0:T(8,128)(2,1)S(1)}, u32[]{:S(2)}, u32[]{:S(2)}) async-start(bf16[8,16,256]{2,1,0:T(8,128)(2,1)} %silu.3), calls=%async_computation.7 | async-start | bytes 131072 | tf_op jit(solution)/shard_map/all_to_all | solution.py:28
  107.3 1.2 slice_select_fusion.1
  108.5 5.6 %all-to-all-done.7.got_ref = bf16[8,16,256]{2,1,0:T(8,128)(2,1)S(1)} async-done(((bf16[8,16,256]{2,1,0:T(8,128)(2,1)}), bf16[8,16,256]{2,1,0:T(8,128)(2,1)S(1)}, u32[]{:S(2)}, u32[]{:S(2)}) %all-to-all-start.7) | async-done | bytes 65568 | tf_op jit(solution)/shard_map/all_to_all | solution.py:28
  114.4 1.3 collective-permute-start.10
  115.9 0.8 pad_maximum_fusion.1
  116.8 1.4 %collective-permute-done.10.refs_3_ = f32[16,256]{1,0:T(8,128)S(1)} collective-permute-done((f32[16,256]{1,0:T(8,128)S(1)}, f32[16,256]{1,0:T(8,128)S(1)}, u32[]{:S(2)}, u32[]{:S(2)}) %collective-permute-start.10) | collective-permute-done | bytes 16416 | tf_op jit(solution)/shard_map/ppermute | solution.py:422
  118.2 0.7 collective-permute-done.9.refs_2_
  118.9 0.6 last.1
  119.5 3.4 %all-to-all-start.8 = ((bf16[8,16,256]{2,1,0:T(8,128)(2,1)}), bf16[8,16,256]{2,1,0:T(8,128)(2,1)S(1)}, u32[]{:S(2)}, u32[]{:S(2)}) async-start(bf16[8,16,256]{2,1,0:T(8,128)(2,1)} %last.1), calls=%async_computation.8 | async-start | bytes 131072 | tf_op jit(solution)/shard_map/all_to_all | solution.py:28
  122.9 0.8 pad_maximum_fusion
  123.7 6.0 %all-to-all-done.8 = bf16[8,16,256]{2,1,0:T(8,128)(2,1)S(1)} async-done(((bf16[8,16,256]{2,1,0:T(8,128)(2,1)}), bf16[8,16,256]{2,1,0:T(8,128)(2,1)S(1)}, u32[]{:S(2)}, u32[]{:S(2)}) %all-to-all-start.8) | async-done | bytes 65568 | tf_op jit(solution)/shard_map/all_to_all | solution.py:28
  129.7 0.6 copy.20
  (67 shorter events, 3.2 us)
Async XLA Ops:
  0.6 0.8 copy-start
  0.6 20.2 %copy-start.7 = (bf16[2,16,64,128]{3,2,1,0:T(8,128)(2,1)S(1)}, bf16[2,16,64,128]{3,2,1,0:T(8,128)(2,1)}, u32[]{:S(2)}) copy-start(bf16[2,16,64,128]{3,2,1,0:T(8,128)(2,1)} %value_ref.3) | copy-start | bytes 1572868
  0.7 20.2 %copy-start.6 = (bf16[2,16,64,128]{3,2,1,0:T(8,128)(2,1)S(1)}, bf16[2,16,64,128]{3,2,1,0:T(8,128)(2,1)}, u32[]{:S(2)}) copy-start(bf16[2,16,64,128]{3,2,1,0:T(8,128)(2,1)} %key_ref.3) | copy-start | bytes 1572868
  1.5 1.0 copy-start.10
  2.5 0.9 copy-start.15
  3.4 0.9 copy-start.17
  5.2 15.7 %all-to-all-start = ((bf16[8,16,896]{2,1,0:T(8,128)(2,1)}), bf16[8,16,896]{2,1,0:T(8,128)(2,1)S(1)}, u32[]{:S(2)}, u32[]{:S(2)}) async-start(bf16[8,16,896]{2,1,0:T(8,128)(2,1)} %first.1), calls=%async_computation | async-start | bytes 458752 | tf_op jit(solution)/shard_map/all_to_all | solution.py:28
  12.4 27.5 %copy-start.1 = (bf16[2,256,2048]{2,1,0:T(8,128)(2,1)S(1)}, bf16[2,256,2048]{2,1,0:T(8,128)(2,1)}, u32[]{:S(2)}) copy-start(bf16[2,256,2048]{2,1,0:T(8,128)(2,1)} %refs_5_.5) | copy-start | bytes 6291460
  20.9 1.0 copy-start.8
  21.9 0.8 copy-start.13
  22.8 12.0 %copy-start.12 = (bf16[2,512,256]{2,1,0:T(8,128)(2,1)S(1)}, bf16[2,512,256]{2,1,0:T(8,128)(2,1)}, u32[]{:S(2)}) copy-start(bf16[2,512,256]{2,1,0:T(8,128)(2,1)} %w_ref.6) | copy-start | bytes 1572868
  35.2 1.8 %collective-permute-start.2 = (f32[16,256]{1,0:T(8,128)S(1)}, f32[16,256]{1,0:T(8,128)S(1)}, u32[]{:S(2)}, u32[]{:S(2)}) collective-permute-start(f32[16,256]{1,0:T(8,128)S(1)} %combine.2.refs_1_), channel_id=1, source_target_pairs={{0,3},{1,0},{2,1},{3,2},{4,7},{5,4},{6,5},{7,6},{8,11},{9,8},{10,9... | collective-permute-start | bytes 49160 | tf_op jit(solution)/shard_map/ppermute | solution.py:422
  35.2 3.8 %collective-permute-start.1 = (f32[16,256]{1,0:T(8,128)S(1)}, f32[16,256]{1,0:T(8,128)S(1)}, u32[]{:S(2)}, u32[]{:S(2)}) collective-permute-start(f32[16,256]{1,0:T(8,128)S(1)} %combine.2.refs_1_), channel_id=1, source_target_pairs={{0,2},{1,3},{2,0},{3,1},{4,6},{5,7},{6,4},{7,5},{8,10},{9,11},{10,... | collective-permute-start | bytes 49160 | tf_op jit(solution)/shard_map/ppermute | solution.py:422
  36.8 3.2 %collective-permute-start = (f32[16,256]{1,0:T(8,128)S(1)}, f32[16,256]{1,0:T(8,128)S(1)}, u32[]{:S(2)}, u32[]{:S(2)}) collective-permute-start(f32[16,256]{1,0:T(8,128)S(1)} %combine.2.refs_1_), channel_id=1, source_target_pairs={{0,1},{1,2},{2,3},{3,0},{4,5},{5,6},{6,7},{7,4},{8,9},{9,10},{10,1... | collective-permute-start | bytes 49160 | tf_op jit(solution)/shard_map/ppermute | solution.py:422
  40.0 1.6 %copy-start.2 = (bf16[2,256,2048]{2,1,0:T(8,128)(2,1)S(1)}, bf16[2,256,2048]{2,1,0:T(8,128)(2,1)}, u32[]{:S(2)}) copy-start(bf16[2,256,2048]{2,1,0:T(8,128)(2,1)} %refs_6_.5) | copy-start | bytes 6291460
  41.6 20.0 %copy-start.4 = (bf16[2,2048,256]{2,1,0:T(8,128)(2,1)S(1)}, bf16[2,2048,256]{2,1,0:T(8,128)(2,1)}, u32[]{:S(2)}) copy-start(bf16[2,2048,256]{2,1,0:T(8,128)(2,1)} %w_ref.7) | copy-start | bytes 6291460
  41.9 23.8 %copy-start.11 = (bf16[2,256,512]{2,1,0:T(8,128)(2,1)S(1)}, bf16[2,256,512]{2,1,0:T(8,128)(2,1)}, u32[]{:S(2)}) copy-start(bf16[2,256,512]{2,1,0:T(8,128)(2,1)} %refs_5_.4) | copy-start | bytes 1572868
  41.9 23.8 %copy-start.16 = (bf16[2,256,128]{2,1,0:T(8,128)(2,1)S(1)}, bf16[2,256,128]{2,1,0:T(8,128)(2,1)}, u32[]{:S(2)}) copy-start(bf16[2,256,128]{2,1,0:T(8,128)(2,1)} %refs_6_.4) | copy-start | bytes 393220
  41.9 23.8 %copy-start.18 = (bf16[2,256,128]{2,1,0:T(8,128)(2,1)S(1)}, bf16[2,256,128]{2,1,0:T(8,128)(2,1)}, u32[]{:S(2)}) copy-start(bf16[2,256,128]{2,1,0:T(8,128)(2,1)} %refs_7_.1) | copy-start | bytes 393220
  42.0 34.6 %copy-start.9 = (s32[1024,1]{1,0:T(8,128)S(1)}, s32[1024,1]{1,0:T(8,128)}, u32[]{:S(2)}) copy-start(s32[1024,1]{1,0:T(8,128)} %reshape.152.fresh_ref) | copy-start | bytes 12292
  42.0 34.6 %copy-start.14 = (s32[128,1]{1,0:T(8,128)S(1)}, s32[128,1]{1,0:T(8,128)}, u32[]{:S(2)}) copy-start(s32[128,1]{1,0:T(8,128)} %get-tuple-element.39.last_ref) | copy-start | bytes 1540
  61.8 1.5 %collective-permute-start.5 = (f32[16,256]{1,0:T(8,128)S(1)}, f32[16,256]{1,0:T(8,128)S(1)}, u32[]{:S(2)}, u32[]{:S(2)}) collective-permute-start(f32[16,256]{1,0:T(8,128)S(1)} %down.2.refs_1_), channel_id=1, source_target_pairs={{0,3},{1,0},{2,1},{3,2},{4,7},{5,4},{6,5},{7,6},{8,11},{9,8},{10,9... | collective-permute-start | bytes 49160 | tf_op jit(solution)/shard_map/ppermute | solution.py:422
  61.8 3.8 %collective-permute-start.4 = (f32[16,256]{1,0:T(8,128)S(1)}, f32[16,256]{1,0:T(8,128)S(1)}, u32[]{:S(2)}, u32[]{:S(2)}) collective-permute-start(f32[16,256]{1,0:T(8,128)S(1)} %down.2.refs_1_), channel_id=1, source_target_pairs={{0,2},{1,3},{2,0},{3,1},{4,6},{5,7},{6,4},{7,5},{8,10},{9,11},{10,... | collective-permute-start | bytes 49160 | tf_op jit(solution)/shard_map/ppermute | solution.py:422
  62.5 3.2 %collective-permute-start.3 = (f32[16,256]{1,0:T(8,128)S(1)}, f32[16,256]{1,0:T(8,128)S(1)}, u32[]{:S(2)}, u32[]{:S(2)}) collective-permute-start(f32[16,256]{1,0:T(8,128)S(1)} %down.2.refs_1_), channel_id=1, source_target_pairs={{0,1},{1,2},{2,3},{3,0},{4,5},{5,6},{6,7},{7,4},{8,9},{9,10},{10,1... | collective-permute-start | bytes 49160 | tf_op jit(solution)/shard_map/ppermute | solution.py:422
  65.7 26.9 %copy-start.3 = (bf16[2,256,2048]{2,1,0:T(8,128)(2,1)S(1)}, bf16[2,256,2048]{2,1,0:T(8,128)(2,1)}, u32[]{:S(2)}) copy-start(bf16[2,256,2048]{2,1,0:T(8,128)(2,1)} %refs_6_.5) | copy-start | bytes 6291460
  88.7 1.5 %collective-permute-start.8 = (f32[16,256]{1,0:T(8,128)S(1)}, f32[16,256]{1,0:T(8,128)S(1)}, u32[]{:S(2)}, u32[]{:S(2)}) collective-permute-start(f32[16,256]{1,0:T(8,128)S(1)} %combine.3.refs_1_), channel_id=1, source_target_pairs={{0,3},{1,0},{2,1},{3,2},{4,7},{5,4},{6,5},{7,6},{8,11},{9,8},{10,9... | collective-permute-start | bytes 49160 | tf_op jit(solution)/shard_map/ppermute | solution.py:422
  88.7 3.9 %collective-permute-start.7 = (f32[16,256]{1,0:T(8,128)S(1)}, f32[16,256]{1,0:T(8,128)S(1)}, u32[]{:S(2)}, u32[]{:S(2)}) collective-permute-start(f32[16,256]{1,0:T(8,128)S(1)} %combine.3.refs_1_), channel_id=1, source_target_pairs={{0,2},{1,3},{2,0},{3,1},{4,6},{5,7},{6,4},{7,5},{8,10},{9,11},{10,... | collective-permute-start | bytes 49160 | tf_op jit(solution)/shard_map/ppermute | solution.py:422
  89.4 3.2 %collective-permute-start.6 = (f32[16,256]{1,0:T(8,128)S(1)}, f32[16,256]{1,0:T(8,128)S(1)}, u32[]{:S(2)}, u32[]{:S(2)}) collective-permute-start(f32[16,256]{1,0:T(8,128)S(1)} %combine.3.refs_1_), channel_id=1, source_target_pairs={{0,1},{1,2},{2,3},{3,0},{4,5},{5,6},{6,7},{7,4},{8,9},{9,10},{10,1... | collective-permute-start | bytes 49160 | tf_op jit(solution)/shard_map/ppermute | solution.py:422
  93.1 21.1 %copy-start.5 = (bf16[2,2048,256]{2,1,0:T(8,128)(2,1)S(1)}, bf16[2,2048,256]{2,1,0:T(8,128)(2,1)}, u32[]{:S(2)}) copy-start(bf16[2,2048,256]{2,1,0:T(8,128)(2,1)} %w_ref.7) | copy-start | bytes 6291460
  104.0 10.2 %all-to-all-start.7 = ((bf16[8,16,256]{2,1,0:T(8,128)(2,1)}), bf16[8,16,256]{2,1,0:T(8,128)(2,1)S(1)}, u32[]{:S(2)}, u32[]{:S(2)}) async-start(bf16[8,16,256]{2,1,0:T(8,128)(2,1)} %silu.3), calls=%async_computation.7 | async-start | bytes 131072 | tf_op jit(solution)/shard_map/all_to_all | solution.py:28
  108.5 7.4 %copy-start.21 = (bf16[1,16,64,128]{3,2,1,0:T(8,128)(2,1)S(1)}, bf16[1,16,64,128]{3,2,1,0:T(8,128)(2,1)}, u32[]{:S(2)}) copy-start(bf16[1,16,64,128]{3,2,1,0:T(8,128)(2,1)} %get-tuple-element.27) | copy-start | bytes 786436
  108.5 7.4 %copy-start.22 = (bf16[1,16,64,128]{3,2,1,0:T(8,128)(2,1)S(1)}, bf16[1,16,64,128]{3,2,1,0:T(8,128)(2,1)}, u32[]{:S(2)}) copy-start(bf16[1,16,64,128]{3,2,1,0:T(8,128)(2,1)} %get-tuple-element.28) | copy-start | bytes 786436
  108.5 14.4 %copy-start.19 = (bf16[1,16,64,128]{3,2,1,0:T(8,128)(2,1)S(1)}, bf16[1,16,64,128]{3,2,1,0:T(8,128)(2,1)}, u32[]{:S(2)}) copy-start(bf16[1,16,64,128]{3,2,1,0:T(8,128)(2,1)} %get-tuple-element.31) | copy-start | bytes 786436
  108.5 14.4 %copy-start.20 = (bf16[1,16,64,128]{3,2,1,0:T(8,128)(2,1)S(1)}, bf16[1,16,64,128]{3,2,1,0:T(8,128)(2,1)}, u32[]{:S(2)}) copy-start(bf16[1,16,64,128]{3,2,1,0:T(8,128)(2,1)} %get-tuple-element.32) | copy-start | bytes 786436
  114.4 2.4 %collective-permute-start.11 = (f32[16,256]{1,0:T(8,128)S(1)}, f32[16,256]{1,0:T(8,128)S(1)}, u32[]{:S(2)}, u32[]{:S(2)}) collective-permute-start(f32[16,256]{1,0:T(8,128)S(1)} %down.3.refs_1_), channel_id=1, source_target_pairs={{0,3},{1,0},{2,1},{3,2},{4,7},{5,4},{6,5},{7,6},{8,11},{9,8},{10,9... | collective-permute-start | bytes 49160 | tf_op jit(solution)/shard_map/ppermute | solution.py:422
  114.4 3.8 %collective-permute-start.10 = (f32[16,256]{1,0:T(8,128)S(1)}, f32[16,256]{1,0:T(8,128)S(1)}, u32[]{:S(2)}, u32[]{:S(2)}) collective-permute-start(f32[16,256]{1,0:T(8,128)S(1)} %down.3.refs_1_), channel_id=1, source_target_pairs={{0,2},{1,3},{2,0},{3,1},{4,6},{5,7},{6,4},{7,5},{8,10},{9,11},{10,... | collective-permute-start | bytes 49160 | tf_op jit(solution)/shard_map/ppermute | solution.py:422
  115.7 3.2 %collective-permute-start.9 = (f32[16,256]{1,0:T(8,128)S(1)}, f32[16,256]{1,0:T(8,128)S(1)}, u32[]{:S(2)}, u32[]{:S(2)}) collective-permute-start(f32[16,256]{1,0:T(8,128)S(1)} %down.3.refs_1_), channel_id=1, source_target_pairs={{0,1},{1,2},{2,3},{3,0},{4,5},{5,6},{6,7},{7,4},{8,9},{9,10},{10,1... | collective-permute-start | bytes 49160 | tf_op jit(solution)/shard_map/ppermute | solution.py:422
  119.5 10.2 %all-to-all-start.8 = ((bf16[8,16,256]{2,1,0:T(8,128)(2,1)}), bf16[8,16,256]{2,1,0:T(8,128)(2,1)S(1)}, u32[]{:S(2)}, u32[]{:S(2)}) async-start(bf16[8,16,256]{2,1,0:T(8,128)(2,1)} %last.1), calls=%async_computation.8 | async-start | bytes 131072 | tf_op jit(solution)/shard_map/all_to_all | solution.py:28

commit v3 on v2

--- a/solution.py
+++ b/solution.py
@@ -205,21 +205,24 @@
     return jnp.dot(a, b, preferred_element_type=jnp.float32)
 
 
-def call(body, out_shape, *args, name):
+def call(body, out_shape, *args, name, held=True, scratch=(), out_specs=None):
     vmem = pl.BlockSpec(memory_space=pltpu.VMEM)
+    where = vmem if held else pl.BlockSpec(memory_space=pltpu.HBM)
     single = not isinstance(out_shape, (tuple, list))
+    args = [pltpu.with_memory_space_constraint(a, pltpu.VMEM if held else pltpu.HBM) for a in args]
     return pl.pallas_call(
         body,
         out_shape=out_shape,
-        in_specs=[vmem] * len(args),
-        out_specs=vmem if single else [vmem] * len(out_shape),
+        in_specs=[where] * len(args),
+        out_specs=out_specs or (vmem if single else [vmem] * len(out_shape)),
+        scratch_shapes=list(scratch),
         compiler_params=pltpu.CompilerParams(vmem_limit_bytes=VMEM_ROOM),
         name=name,
-    )(*[pltpu.with_memory_space_constraint(a, pltpu.VMEM) for a in args])
-
-
-def project_body(layer, own, wq_ref, wk_ref, wv_ref, out_ref):
-    part = [dot32(own, w[layer]).astype(jnp.bfloat16) for w in (wq_ref, wk_ref, wv_ref)]
+    )(*args)
+
+
+def project_body(own, weights, out_ref):
+    part = [dot32(own, w).astype(jnp.bfloat16) for w in weights]
     lane = lane_ids((own.shape[0], LANES))
     part.append(as_hi_lo(square_sum(own), lane))
     for member in range(out_ref.shape[0]):
@@ -229,8 +232,77 @@
             at += piece.shape[1]
 
 
-def first_kernel(own_ref, wq_ref, wk_ref, wv_ref, out_ref):
-    project_body(0, own_ref[...], wq_ref, wk_ref, wv_ref, out_ref)
+def first_kernel(n_more, *refs):
+    hidden_ref, length_ref, position_ref, wq_ref, wk_ref, wv_ref = refs[:6]
+    more = refs[6 : 6 + n_more]
+    own_ref, cos_ref, sin_ref, table_ref, out_ref = refs[6 + n_more : 11 + n_more]
+    more_here = refs[11 + n_more : 11 + 2 * n_more]
+    wq_here, wk_here, wv_here, lengths, positions, sems = refs[11 + 2 * n_more :]
+    span = own_ref.shape[1]
+    start = pl.multiple_of(lax.axis_index("seq") * span, LANES)
+    copies = [
+        pltpu.make_async_copy(position_ref, positions, sems.at[0]),
+        pltpu.make_async_copy(length_ref, lengths, sems.at[1]),
+        pltpu.make_async_copy(hidden_ref.at[:, pl.ds(start, span)], own_ref, sems.at[2]),
+        pltpu.make_async_copy(wq_ref.at[0], wq_here, sems.at[3]),
+        pltpu.make_async_copy(wk_ref.at[0], wk_here, sems.at[4]),
+        pltpu.make_async_copy(wv_ref.at[0], wv_here, sems.at[5]),
+    ]
+    copies += [
+        pltpu.make_async_copy(ref.at[0], here.at[0], sems.at[6 + i])
+        for i, (ref, here) in enumerate(zip(more, more_here))
+    ]
+    for copy in copies:
+        copy.start()
+    copies[0].wait()
+    copies[1].wait()
+    half = HEAD_DIM // 2
+    lane = lane_ids(table_ref.shape)
+    row = lax.broadcasted_iota(jnp.int32, table_ref.shape, 0)
+    place = jnp.zeros(table_ref.shape, jnp.int32)
+    length = jnp.zeros(table_ref.shape, jnp.int32)
+    for b in range(table_ref.shape[0]):
+        place = jnp.where(row == b, positions[b], place)
+        length = jnp.where(row == b, lengths[b], length)
+    inverse = jnp.zeros(table_ref.shape, jnp.float32)
+    for i in range(half):
+        inverse = jnp.where(lane % half == i, 500000.0 ** (-2.0 * i / HEAD_DIM), inverse)
+    angles = place.astype(jnp.float32) * inverse
+    sine = jnp.sin(angles)
+    table_ref[...] = length
+    cos_ref[...] = jnp.cos(angles)
+    sin_ref[...] = jnp.where(lane % HEAD_DIM < half, -sine, sine)
+    for copy in copies[2:6]:
+        copy.wait()
+    project_body(own_ref[...], [wq_here[...], wk_here[...], wv_here[...]], out_ref)
+    for copy in copies[6:]:
+        copy.wait()
+
+
+def store_kernel(keep_ref, length_ref, key_ref, value_ref, *refs):
+    layers, requests, block, _ = key_ref.shape
+    fresh_rows = refs[: 2 * layers]
+    key_out, value_out, token_ref, key_here, value_here, sems = refs[2 * layers :]
+    token_ref[...] = jnp.zeros_like(token_ref)
+    fresh = length_ref[...] - lax.axis_index("seq") * block
+    slot = lax.broadcasted_iota(jnp.int32, (block, LANES), 0)
+    copies = []
+    for layer in range(layers):
+        for i, (old, here, out) in enumerate(
+            [(key_ref, key_here, key_out), (value_ref, value_here, value_out)]
+        ):
+            new = fresh_rows[2 * layer + i][...].astype(jnp.float32)
+            for b in range(requests):
+                row = jnp.where(
+                    slot == fresh[b : b + 1], new[b : b + 1], old[layer, b].astype(jnp.float32)
+                )
+                here[layer, b] = row.astype(jnp.bfloat16)
+            copies.append(
+                pltpu.make_async_copy(here.at[layer], out.at[layer], sems.at[2 * layer + i])
+            )
+            copies[-1].start()
+    for copy in copies:
+        copy.wait()
 
 
 def sum_parts(base_ref, part_refs):
@@ -245,18 +317,36 @@
     wq_ref, wk_ref, wv_ref, own_ref, out_ref = refs[1 + n_parts :]
     own = sum_parts(base_ref, parts)
     own_ref[...] = own
-    project_body(layer, own, wq_ref, wk_ref, wv_ref, out_ref)
-
-
-def last_kernel(n_parts, *refs):
-    base_ref, parts, out_ref = refs[0], refs[1 : 1 + n_parts], refs[1 + n_parts]
-    own = sum_parts(base_ref, parts)
+    project_body(own, [w[layer] for w in (wq_ref, wk_ref, wv_ref)], out_ref)
+
+
+def half_of(value, core):
+    middle = value.shape[1] // 2
+    return jnp.where(core == 0, value[:, :middle], value[:, middle:])
+
+
+def meet_kernel(n_tp, mid_ref, keep_ref, got_ref, token_ref, out_ref):
+    place = lax.axis_index("tp")
+    total = keep_ref[...] + got_ref[...]
+    base = half_of(mid_ref[...].astype(jnp.float32), place % 2)
+    total = (total + jnp.where(place < 2, base, 0.0)).astype(jnp.bfloat16)
     for member in range(out_ref.shape[0]):
-        out_ref[member] = own
+        out_ref[member] = total
+
+
+def last_kernel(n_tp, got_ref, out_ref):
+    span = got_ref.shape[2]
+    for block in range(got_ref.shape[0] // n_tp):
+        for core in range(2):
+            total = got_ref[block * n_tp + core].astype(jnp.float32)
+            for pair in range(1, n_tp // 2):
+                total = total + got_ref[block * n_tp + 2 * pair + core].astype(jnp.float32)
+            at = (2 * block + core) * span
+            out_ref[:, at : at + span] = total.astype(jnp.bfloat16)
 
 
 def attend_kernel(
-    layer, width, heads, kv_heads, got_ref, cos_ref, sin_ref, first_ref, last_ref, fresh_ref,
+    layer, width, heads, kv_heads, got_ref, cos_ref, sin_ref, length_ref,
     key_ref, value_ref, out_ref, key_new_ref, value_new_ref,
 ):
     members, requests, _ = got_ref.shape
@@ -300,11 +390,12 @@
     key_new_ref[...] = key_new
     value_new_ref[...] = value_new
 
-    fresh = fresh_ref[...] > 0
+    fresh = length_ref[...] - lax.axis_index("seq") * block
+    slot = lax.broadcasted_iota(jnp.int32, (block, LANES), 0)
     keys = []
     values = []
     for b in range(requests):
-        here = fresh[b * block : (b + 1) * block]
+        here = slot == fresh[b : b + 1]
         k = key_ref[layer, b].astype(jnp.float32)
         v = value_ref[layer, b].astype(jnp.float32)
         keys.append(jnp.where(here, key_new[b : b + 1].astype(jnp.float32), k).astype(jnp.bfloat16))
@@ -316,8 +407,13 @@
     scores = lax.dot_general(
         query, keys, (((1,), (1,)), ((), ())), preferred_element_type=jnp.float32
     ) * (1.0 / math.sqrt(HEAD_DIM))
+    begin = lax.broadcasted_iota(jnp.int32, (requests, LANES), 0) * block
+    end = begin + jnp.clip(fresh + 1, 0, block)
+    copies = scores.shape[1] // LANES
+    begin = jnp.concatenate([jnp.concatenate([begin] * heads, axis=0)] * copies, axis=1)
+    end = jnp.concatenate([jnp.concatenate([end] * heads, axis=0)] * copies, axis=1)
     column = lane_ids(scores.shape)
-    live = (column >= first_ref[...]) & (column < last_ref[...])
+    live = (column >= begin) & (column < end)
     scores = jnp.where(live, scores, neg_fill)
     top = jnp.max(scores, axis=1, keepdims=True)
     weights = jnp.where(live, jnp.exp(scores - top), 0.0)
@@ -390,8 +486,8 @@
     side = as_hi_lo(square_sum(mid), lane_ids((mid.shape[0], LANES)))
     members = out_ref.shape[0]
     own = gate_ref.shape[2] // members
-    for member in range(members):
-        cols = slice(member * own, (member + 1) * own)
+    for member, owner in enumerate(member_order(members)):
+        cols = slice(owner * own, (owner + 1) * own)
         out_ref[member, :, :own] = dot32(mid, gate_ref[layer, :, cols]).astype(jnp.bfloat16)
         out_ref[member, :, own : 2 * own] = dot32(mid, up_ref[layer, :, cols]).astype(jnp.bfloat16)
         out_ref[member, :, 2 * own :] = side
@@ -411,17 +507,41 @@
         out_ref[member] = hidden
 
 
+def in_order(got_ref):
+    order = member_order(got_ref.shape[0])
+    return jnp.concatenate([got_ref[order.index(m)] for m in range(len(order))], axis=1)
+
+
 def down_kernel(layer, got_ref, w_ref, out_ref):
-    hidden = jnp.concatenate([got_ref[m] for m in range(got_ref.shape[0])], axis=1)
+    hidden = in_order(got_ref)
     out_ref[...] = dot32(hidden, w_ref[layer])
 
 
+def down_last_kernel(layer, got_ref, w_ref, keep_ref, give_ref):
+    hidden = in_order(got_ref)
+    part = dot32(hidden, w_ref[layer])
+    core = lax.axis_index("tp") % 2
+    keep_ref[...] = half_of(part, core)
+    give_ref[...] = half_of(part, 1 - core)
+
+
+def member_order(n_seq):
+    return [0, 7, 2, 5, 1, 6, 3, 4] if n_seq == 8 else list(range(n_seq))
+
+
 def make_with_kernels(n_seq, n_tp):
+    order = member_order(n_seq)
+    groups = [[s * n_tp + t for s in order] for t in range(n_tp)]
+
+    def swap(chunks):
+        return lax.all_to_all(chunks, ("seq", "tp"), 0, 0, axis_index_groups=groups)
+
     def tp_parts(part):
-        return [part] + [
+        got = [
             lax.ppermute(part, "tp", [(i, (i + k) % n_tp) for i in range(n_tp)])
             for k in range(1, n_tp)
         ]
+        return [part] + got
 
     def per_device(
         hidden_in,
@@ -437,10 +557,8 @@
         key_cache,
         value_cache,
     ):
-        seq_index = lax.axis_index("seq")
         requests, width = hidden_in.shape
         col_count = out_weight.shape[2]
-        block_len = key_cache.shape[2]
         kv_width = key_cache.shape[3]
         query_width = query_weight.shape[2]
         heads = query_width // HEAD_DIM
@@ -451,65 +569,65 @@
         def shape(dims, kind):
             return pltpu.VMEM(dims, kind)
 
-        slots = seq_index * block_len + jnp.arange(block_len, dtype=jnp.int32)
-        new_slot = slots[None, :] == lengths[:, None]
-        fresh = new_slot.astype(jnp.int32).reshape(requests * block_len, 1)
-        row_request = jnp.arange(heads * requests, dtype=jnp.int32) % requests
-        first = row_request * block_len
-        count = jnp.clip(lengths + 1 - seq_index * block_len, 0, block_len)
-        last = first + jnp.tile(count, heads)
-        half = HEAD_DIM // 2
-        inverse = 500000.0 ** (-(2.0 * jnp.arange(half, dtype=jnp.float32)) / HEAD_DIM)
-        angles = positions.astype(jnp.float32)[:, None] * inverse[None, :]
-        cosine = jnp.cos(angles)
-        sine = jnp.sin(angles)
-        cosine = jnp.tile(cosine, (1, LANES // half))
-        sine = jnp.tile(jnp.concatenate([-sine, sine], axis=1), (1, LANES // HEAD_DIM))
-
-        own = lax.dynamic_slice_in_dim(hidden_in, seq_index * col_count, col_count, 1)
         packed_shape = shape((n_seq, requests, query_width + 2 * kv_width + LANES), bf16)
         part_shape = shape((requests, col_count), f32)
         own_shape = shape((requests, col_count), bf16)
         new_shape = shape((requests, kv_width), bf16)
-        key_layers = []
-        value_layers = []
+        fresh_rows = []
+        packed_weights = (query_weight, key_weight, value_weight)
+        table_shape = (requests, LANES)
+        stored = (key_cache, value_cache, out_weight, gate_weight, up_weight)
+        own, cosine, sine, length_table, packed, *early = call(
+            functools.partial(first_kernel, len(stored)),
+            (
+                own_shape,
+                shape(table_shape, f32),
+                shape(table_shape, f32),
+                shape(table_shape, jnp.int32),
+                packed_shape,
+            )
+            + tuple(shape((1,) + a.shape[1:], bf16) for a in stored),
+            hidden_in,
+            lengths,
+            positions,
+            *packed_weights,
+            *stored,
+            name="first",
+            held=False,
+            scratch=[pltpu.VMEM(w.shape[1:], bf16) for w in packed_weights]
+            + [pltpu.SMEM((requests,), jnp.int32)] * 2
+            + [pltpu.SemaphoreType.DMA((6 + len(stored),))],
+        )
         parts = None
         mid = None
         for layer in range(LAYERS):
-            weights = (query_weight, key_weight, value_weight)
-            if parts is None:
-                packed = call(first_kernel, packed_shape, own, *weights, name="first")
-            else:
+            keys, values, out_here, gate_here, up_here = early if layer == 0 else stored
+            if layer > 0:
                 own, packed = call(
                     functools.partial(next_kernel, layer, n_tp),
                     (own_shape, packed_shape),
                     mid,
                     *parts,
-                    *weights,
+                    *packed_weights,
                     name="next",
                 )
             packed, key_new, value_new = call(
                 functools.partial(attend_kernel, layer, width, heads, kv_heads),
                 (shape((n_seq, requests, query_width + LANES), bf16), new_shape, new_shape),
-                seq_swap(packed),
+                swap(packed),
                 cosine,
                 sine,
-                first[:, None],
-                last[:, None],
-                fresh,
-                key_cache,
-                value_cache,
+                length_table,
+                keys,
+                values,
                 name="attend",
-            )
-            key_layers.append(jnp.where(new_slot[:, :, None], key_new[:, None, :], key_cache[layer]))
-            value_layers.append(
-                jnp.where(new_slot[:, :, None], value_new[:, None, :], value_cache[layer])
-            )
+                )
+            fresh_rows += [key_new, value_new]
             part = call(
                 functools.partial(combine_kernel, layer, heads),
                 part_shape,
-                seq_swap(packed),
-                out_weight,
+                swap(packed),
+                out_here,
                 name="combine",
             )
             mid, packed = call(
@@ -517,33 +635,63 @@
                 (own_shape, shape((n_seq, requests, 2 * ff_own + LANES), bf16)),
                 own,
                 *tp_parts(part),
-                gate_weight,
-                up_weight,
+                gate_here,
+                up_here,
                 name="widen",
             )
             hidden = call(
                 functools.partial(silu_kernel, width),
                 shape((n_seq, requests, ff_own), bf16),
-                seq_swap(packed),
+                swap(packed),
                 name="silu",
             )
-            part = call(
-                functools.partial(down_kernel, layer),
-                part_shape,
-                seq_swap(hidden),
-                down_weight,
-                name="down",
-            )
-            parts = tp_parts(part)
+            hidden = swap(hidden)
+            if layer + 1 < LAYERS:
+                part = call(
+                    functools.partial(down_kernel, layer), part_shape, hidden, down_weight, name="down"
+                )
+                parts = tp_parts(part)
+        half_shape = shape((requests, col_count // 2), f32)
+        keep, give = call(
+            functools.partial(down_last_kernel, LAYERS - 1),
+            (half_shape, half_shape),
+            hidden,
+            down_weight,
+            name="down_last",
+        )
+        give = lax.ppermute(give, "tp", [(i, i ^ 1) for i in range(n_tp)])
+        cache_shape = jax.ShapeDtypeStruct(key_cache.shape, bf16)
+        hbm = pl.BlockSpec(memory_space=pltpu.HBM)
+        key_out, value_out, token = call(
+            store_kernel,
+            (cache_shape, cache_shape, shape((8, LANES), f32)),
+            keep,
+            length_table,
+            key_cache,
+            value_cache,
+            *fresh_rows,
+            name="store",
+            out_specs=[hbm, hbm, pl.BlockSpec(memory_space=pltpu.VMEM)],
+            scratch=[pltpu.VMEM(key_cache.shape, bf16)] * 2
+            + [pltpu.SemaphoreType.DMA((2 * LAYERS,))],
+        )
+        stream = call(
+            functools.partial(meet_kernel, n_tp),
+            shape((n_seq * n_tp, requests, col_count // 2), bf16),
+            mid,
+            keep,
+            give,
+            token,
+            name="meet",
+        )
+        stream = lax.all_to_all(stream, ("seq", "tp"), 0, 0)
         stream = call(
             functools.partial(last_kernel, n_tp),
-            shape((n_seq, requests, col_count), bf16),
-            mid,
-            *parts,
+            jax.ShapeDtypeStruct((requests, width), bf16),
+            stream,
             name="last",
         )
-        stream = seq_swap(stream).transpose(1, 0, 2).reshape(requests, width)
-        return (stream, jnp.stack(key_layers), jnp.stack(value_layers))
+        return (stream, key_out, value_out)
 
     return per_device
 
@@ -554,7 +702,8 @@
     def per_device(*args):
         gate_weight, key_cache = args[7], args[10]
         aligned = (
-            args[6].shape[2] % LANES == 0
+            args[6].shape[2] % (2 * LANES) == 0
+            and n_tp % 2 == 0
             and gate_weight.shape[2] // n_seq % LANES == 0
             and key_cache.shape[3] == LANES
         )

time: 131 us -> 115 us (0.88)
  blocking collectives: 61.8 us -> 92.3 us
  waiting for transfers between devices: 25.1 us -> 9.01 us
  starting transfers between devices: 19.2 us -> 3.77 us
  local copies, waits for them, and re-layouts: 10 us -> 0.03 us
  other arithmetic: 6.75 us -> 0 us
  Pallas kernels: 6.77 us -> 8.43 us
    all_to_all x6 -> x9, blocking collectives: 61.8 us -> 92.3 us  [the longest x8 82.1 us: swap(): return lax.all_to_all(chunks, ('seq', 'tp'), 0, 0, axis_index_groups=groups)]
    all_to_all x3 -> x0, waiting for transfers between devices: 14 us -> none  [seq_swap(): return lax.all_to_all(chunks, 'seq', 0, 0)]
    all_to_all x3 -> x0, starting transfers between devices: 14 us -> none  [seq_swap(): return lax.all_to_all(chunks, 'seq', 0, 0)]
    unnamed x46 -> x18, local copies, waits for them, and re-layouts: 7.2 us -> 0.03 us
    ppermute x12 -> x9, waiting for transfers between devices: 11.1 us -> 8.96 us  [tp_parts(): lax.ppermute(part, 'tp', [(i, (i + k) % n_tp) for i in range(n_tp)])]
    another operation x2 -> x0, other arithmetic: 1.68 us -> none  [per_device(): return (stream, jnp.stack(key_layers), jnp.stack(value_layers))]
    pallas_call x13 -> x15, Pallas kernels: 6.77 us -> 8.43 us  [call(): pl.pallas_call(body, out_shape=out_shape, in_specs=[where] * len(args), o...]
    mul x1 -> x0, other arithmetic: 1.48 us -> none  [per_device(): first = row_request * block_len]
  transfers between devices with their start and end apart: 15 -> 10, of which waited for: 13 -> 8; matrix products, arithmetic and copies ran while one was open for 7% -> 0% of each run, Pallas kernels for 0% -> 1%
where the time goes in v3:
time: 115 us; the launch traced here: 114 us
  blocking collectives  92.3 us (80%)
  waiting for transfers between devices  9.01 us (8%)
  Pallas kernels  8.43 us (7%)
  starting transfers between devices  3.77 us (3%)
    all_to_all x8, blocking collectives, swap(): return lax.all_to_all(chunks, ('seq', 'tp'), 0, 0, axis_index_groups=groups)  82.1 us
    all_to_all x1, blocking collectives, per_device(): stream = lax.all_to_all(stream, ('seq', 'tp'), 0, 0)  10.2 us
    ppermute x9, waiting for transfers between devices, tp_parts(): lax.ppermute(part, 'tp', [(i, (i + k) % n_tp) for i in range(n_tp)])  8.96 us
    pallas_call x15, Pallas kernels, call(): pl.pallas_call(body, out_shape=out_shape, in_specs=[where] * len(args), o...  8.43 us
    ppermute x9, starting transfers between devices, tp_parts(): lax.ppermute(part, 'tp', [(i, (i + k) % n_tp) for i in range(n_tp)])  3.76 us
  transfers between devices with their start and end apart: 10, of which 8 were waited for; matrix products, arithmetic and copies ran while one was open for 0% of the time, Pallas kernels for 1%

profile of v3, /device:TPU:0, one launch (start us, length us, event | category | flops | bytes accessed | tf_op | source)
XLA Modules:
  0.0 114.2 jit_solution(16183680010827235535)
XLA Ops:
  0.6 2.1 %first.1 = (bf16[16,256]{1,0:T(8,128)(2,1)S(1)}, f32[16,128]{1,0:T(8,128)S(1)}, f32[16,128]{1,0:T(8,128)S(1)}, s32[16,128]{1,0:T(8,128)S(1)}, bf16[8,16,896]{2,1...) custom-call(bf16[16,2048]{1,0:T(8,128)(2,1)} %refs_0_.1, ...), custom_call_target="tpu_custom_call" | custom-call | tf_op jit(solution)/shard_map/first/pallas_call | solution.py:213
  2.7 15.3 %all_to_all.45.got_ref = bf16[8,16,896]{2,1,0:T(8,128)(2,1)S(1)} all-to-all(bf16[8,16,896]{2,1,0:T(8,128)(2,1)S(1)} %get-tuple-element.31), channel_id=1, replica_groups={{0,28,8,20,4,24,12,16},{1,29,9,21,5,25,13,17},{2,30,10,22,6,26,14,18},{..., dimensions={0} | all-to-all | bytes 458752 | tf_op jit(solution)/shard_map/all_to_all | solution.py:537
  18.0 0.9 attend.2
  18.9 9.5 %all_to_all.46.got_ref = bf16[8,16,640]{2,1,0:T(8,128)(2,1)S(1)} all-to-all(bf16[8,16,640]{2,1,0:T(8,128)(2,1)S(1)} %get-tuple-element.37), channel_id=1, replica_groups={{0,28,8,20,4,24,12,16},{1,29,9,21,5,25,13,17},{2,30,10,22,6,26,14,18},{..., dimensions={0} | all-to-all | bytes 327680 | tf_op jit(solution)/shard_map/all_to_all | solution.py:537
  28.4 0.5 combine.2.refs_1_
  28.8 0.0 collective-permute-start.2
  28.8 1.6 %collective-permute-start.1 = (f32[16,256]{1,0:T(8,128)S(1)}, f32[16,256]{1,0:T(8,128)S(1)}, u32[]{:S(2)}, u32[]{:S(2)}) collective-permute-start(f32[16,256]{1,0:T(8,128)S(1)} %combine.2.refs_1_), channel_id=1, source_target_pairs={{0,2},{1,3},{2,0},{3,1},{4,6},{5,7},{6,4},{7,5},{8,10},{9,11},{10,... | collective-permute-start | bytes 49160 | tf_op jit(solution)/shard_map/ppermute | solution.py:541
  30.4 0.2 collective-permute-start
  30.6 0.0 collective-permute-done.2.refs_4_
  30.6 2.0 %collective-permute-done.1.refs_3_ = f32[16,256]{1,0:T(8,128)S(1)} collective-permute-done((f32[16,256]{1,0:T(8,128)S(1)}, f32[16,256]{1,0:T(8,128)S(1)}, u32[]{:S(2)}, u32[]{:S(2)}) %collective-permute-start.1) | collective-permute-done | bytes 16416 | tf_op jit(solution)/shard_map/ppermute | solution.py:541
  32.6 0.9 collective-permute-done.refs_2_
  33.6 0.4 widen.2
  34.0 9.6 %all_to_all.47.got_ref = bf16[8,16,640]{2,1,0:T(8,128)(2,1)S(1)} all-to-all(bf16[8,16,640]{2,1,0:T(8,128)(2,1)S(1)} %get-tuple-element.42), channel_id=1, replica_groups={{0,28,8,20,4,24,12,16},{1,29,9,21,5,25,13,17},{2,30,10,22,6,26,14,18},{..., dimensions={0} | all-to-all | bytes 327680 | tf_op jit(solution)/shard_map/all_to_all | solution.py:537
  43.6 0.2 silu.2
  43.8 9.3 %all_to_all.48.got_ref = bf16[8,16,256]{2,1,0:T(8,128)(2,1)S(1)} all-to-all(bf16[8,16,256]{2,1,0:T(8,128)(2,1)S(1)} %silu.2), channel_id=1, replica_groups={{0,28,8,20,4,24,12,16},{1,29,9,21,5,25,13,17},{2,30,10,22,6,26,14,18},{..., dimensions={0} | all-to-all | bytes 131072 | tf_op jit(solution)/shard_map/all_to_all | solution.py:537
  53.1 0.0 copy-done.2
  53.1 0.2 down.1.refs_1_
  53.3 0.0 collective-permute-start.5
  53.3 0.8 collective-permute-start.4
  54.1 0.2 collective-permute-start.3
  54.3 0.5 collective-permute-done.5.refs_4_
  54.8 2.4 %collective-permute-done.4.refs_3_ = f32[16,256]{1,0:T(8,128)S(1)} collective-permute-done((f32[16,256]{1,0:T(8,128)S(1)}, f32[16,256]{1,0:T(8,128)S(1)}, u32[]{:S(2)}, u32[]{:S(2)}) %collective-permute-start.4) | collective-permute-done | bytes 16416 | tf_op jit(solution)/shard_map/ppermute | solution.py:541
  57.2 0.1 collective-permute-done.3.refs_2_
  57.3 0.0 copy-done.5
  57.3 0.0 copy-done.8
  57.3 0.2 next.1
  57.5 10.2 %all_to_all.49.got_ref = bf16[8,16,896]{2,1,0:T(8,128)(2,1)S(1)} all-to-all(bf16[8,16,896]{2,1,0:T(8,128)(2,1)S(1)} %get-tuple-element.44), channel_id=1, replica_groups={{0,28,8,20,4,24,12,16},{1,29,9,21,5,25,13,17},{2,30,10,22,6,26,14,18},{..., dimensions={0} | all-to-all | bytes 458752 | tf_op jit(solution)/shard_map/all_to_all | solution.py:537
  67.7 0.9 attend.3
  68.6 9.5 %all_to_all.50.got_ref = bf16[8,16,640]{2,1,0:T(8,128)(2,1)S(1)} all-to-all(bf16[8,16,640]{2,1,0:T(8,128)(2,1)S(1)} %get-tuple-element.45), channel_id=1, replica_groups={{0,28,8,20,4,24,12,16},{1,29,9,21,5,25,13,17},{2,30,10,22,6,26,14,18},{..., dimensions={0} | all-to-all | bytes 327680 | tf_op jit(solution)/shard_map/all_to_all | solution.py:537
  78.1 0.0 copy-done.6
  78.1 0.5 combine.3.refs_1_
  78.6 0.0 collective-permute-start.8
  78.6 0.8 collective-permute-start.7
  79.4 0.2 collective-permute-start.6
  79.6 0.5 collective-permute-done.8.refs_4_
  80.1 2.3 %collective-permute-done.7.refs_3_ = f32[16,256]{1,0:T(8,128)S(1)} collective-permute-done((f32[16,256]{1,0:T(8,128)S(1)}, f32[16,256]{1,0:T(8,128)S(1)}, u32[]{:S(2)}, u32[]{:S(2)}) %collective-permute-start.7) | collective-permute-done | bytes 16416 | tf_op jit(solution)/shard_map/ppermute | solution.py:541
  82.4 0.2 collective-permute-done.6.refs_2_
  82.6 0.0 copy-done
  82.6 0.4 widen.3
  83.0 9.6 %all_to_all.51.got_ref = bf16[8,16,640]{2,1,0:T(8,128)(2,1)S(1)} all-to-all(bf16[8,16,640]{2,1,0:T(8,128)(2,1)S(1)} %get-tuple-element.47), channel_id=1, replica_groups={{0,28,8,20,4,24,12,16},{1,29,9,21,5,25,13,17},{2,30,10,22,6,26,14,18},{..., dimensions={0} | all-to-all | bytes 327680 | tf_op jit(solution)/shard_map/all_to_all | solution.py:537
  92.5 0.2 silu.3
  92.7 9.2 %all_to_all.52.got_ref = bf16[8,16,256]{2,1,0:T(8,128)(2,1)S(1)} all-to-all(bf16[8,16,256]{2,1,0:T(8,128)(2,1)S(1)} %silu.3), channel_id=1, replica_groups={{0,28,8,20,4,24,12,16},{1,29,9,21,5,25,13,17},{2,30,10,22,6,26,14,18},{..., dimensions={0} | all-to-all | bytes 131072 | tf_op jit(solution)/shard_map/all_to_all | solution.py:537
  101.9 0.2 down_last.1
  102.2 0.0 collective-permute-start.9
  102.2 1.1 store.1
  103.3 0.1 collective-permute-done.9.got_ref
  103.4 10.2 %all_to_all.53.got_ref = bf16[32,16,128]{2,1,0:T(8,128)(2,1)S(1)} all-to-all(bf16[32,16,128]{2,1,0:T(8,128)(2,1)S(1)} %meet.1), channel_id=1, replica_groups=mesh['seq'=8,'tp'=4] {'seq','tp'}, dimensions={0} | all-to-all | bytes 262144 | tf_op jit(solution)/shard_map/all_to_all | solution.py:687
  113.6 0.6 last.1
  (14 shorter events, 0.0 us)
Async XLA Ops:
  18.0 35.1 %copy-start.2 = (bf16[2,2048,256]{2,1,0:T(8,128)(2,1)S(1)}, bf16[2,2048,256]{2,1,0:T(8,128)(2,1)}, u32[]{:S(2)}) copy-start(bf16[2,2048,256]{2,1,0:T(8,128)(2,1)} %w_ref.5) | copy-start | bytes 6291460
  28.8 1.8 %collective-permute-start.2 = (f32[16,256]{1,0:T(8,128)S(1)}, f32[16,256]{1,0:T(8,128)S(1)}, u32[]{:S(2)}, u32[]{:S(2)}) collective-permute-start(f32[16,256]{1,0:T(8,128)S(1)} %combine.2.refs_1_), channel_id=1, source_target_pairs={{0,3},{1,0},{2,1},{3,2},{4,7},{5,4},{6,5},{7,6},{8,11},{9,8},{10,9... | collective-permute-start | bytes 49160 | tf_op jit(solution)/shard_map/ppermute | solution.py:541
  28.8 3.8 %collective-permute-start.1 = (f32[16,256]{1,0:T(8,128)S(1)}, f32[16,256]{1,0:T(8,128)S(1)}, u32[]{:S(2)}, u32[]{:S(2)}) collective-permute-start(f32[16,256]{1,0:T(8,128)S(1)} %combine.2.refs_1_), channel_id=1, source_target_pairs={{0,2},{1,3},{2,0},{3,1},{4,6},{5,7},{6,4},{7,5},{8,10},{9,11},{10,... | collective-permute-start | bytes 49160 | tf_op jit(solution)/shard_map/ppermute | solution.py:541
  30.4 3.2 %collective-permute-start = (f32[16,256]{1,0:T(8,128)S(1)}, f32[16,256]{1,0:T(8,128)S(1)}, u32[]{:S(2)}, u32[]{:S(2)}) collective-permute-start(f32[16,256]{1,0:T(8,128)S(1)} %combine.2.refs_1_), channel_id=1, source_target_pairs={{0,1},{1,2},{2,3},{3,0},{4,5},{5,6},{6,7},{7,4},{8,9},{9,10},{10,1... | collective-permute-start | bytes 49160 | tf_op jit(solution)/shard_map/ppermute | solution.py:541
  33.6 23.7 %copy-start.5 = (bf16[2,256,512]{2,1,0:T(8,128)(2,1)S(1)}, bf16[2,256,512]{2,1,0:T(8,128)(2,1)}, u32[]{:S(2)}) copy-start(bf16[2,256,512]{2,1,0:T(8,128)(2,1)} %refs_5_.4) | copy-start | bytes 1572868
  33.6 23.7 %copy-start.7 = (bf16[2,256,128]{2,1,0:T(8,128)(2,1)S(1)}, bf16[2,256,128]{2,1,0:T(8,128)(2,1)}, u32[]{:S(2)}) copy-start(bf16[2,256,128]{2,1,0:T(8,128)(2,1)} %refs_6_.4) | copy-start | bytes 393220
  33.6 23.7 %copy-start.8 = (bf16[2,256,128]{2,1,0:T(8,128)(2,1)S(1)}, bf16[2,256,128]{2,1,0:T(8,128)(2,1)}, u32[]{:S(2)}) copy-start(bf16[2,256,128]{2,1,0:T(8,128)(2,1)} %refs_7_.3) | copy-start | bytes 393220
  34.0 33.7 %copy-start.3 = (bf16[2,16,64,128]{3,2,1,0:T(8,128)(2,1)S(1)}, bf16[2,16,64,128]{3,2,1,0:T(8,128)(2,1)}, u32[]{:S(2)}) copy-start(bf16[2,16,64,128]{3,2,1,0:T(8,128)(2,1)} %key_ref.3) | copy-start | bytes 1572868
  34.0 33.7 %copy-start.4 = (bf16[2,16,64,128]{3,2,1,0:T(8,128)(2,1)S(1)}, bf16[2,16,64,128]{3,2,1,0:T(8,128)(2,1)}, u32[]{:S(2)}) copy-start(bf16[2,16,64,128]{3,2,1,0:T(8,128)(2,1)} %value_ref.3) | copy-start | bytes 1572868
  53.1 25.0 %copy-start.6 = (bf16[2,512,256]{2,1,0:T(8,128)(2,1)S(1)}, bf16[2,512,256]{2,1,0:T(8,128)(2,1)}, u32[]{:S(2)}) copy-start(bf16[2,512,256]{2,1,0:T(8,128)(2,1)} %w_ref.4) | copy-start | bytes 1572868
  53.1 29.5 %copy-start.1 = (bf16[2,256,2048]{2,1,0:T(8,128)(2,1)S(1)}, bf16[2,256,2048]{2,1,0:T(8,128)(2,1)}, u32[]{:S(2)}) copy-start(bf16[2,256,2048]{2,1,0:T(8,128)(2,1)} %refs_6_.5) | copy-start | bytes 6291460
  53.3 29.2 %copy-start = (bf16[2,256,2048]{2,1,0:T(8,128)(2,1)S(1)}, bf16[2,256,2048]{2,1,0:T(8,128)(2,1)}, u32[]{:S(2)}) copy-start(bf16[2,256,2048]{2,1,0:T(8,128)(2,1)} %refs_5_.5) | copy-start | bytes 6291460
  53.3 1.5 %collective-permute-start.5 = (f32[16,256]{1,0:T(8,128)S(1)}, f32[16,256]{1,0:T(8,128)S(1)}, u32[]{:S(2)}, u32[]{:S(2)}) collective-permute-start(f32[16,256]{1,0:T(8,128)S(1)} %down.1.refs_1_), channel_id=1, source_target_pairs={{0,3},{1,0},{2,1},{3,2},{4,7},{5,4},{6,5},{7,6},{8,11},{9,8},{10,9... | collective-permute-start | bytes 49160 | tf_op jit(solution)/shard_map/ppermute | solution.py:541
  53.3 3.9 %collective-permute-start.4 = (f32[16,256]{1,0:T(8,128)S(1)}, f32[16,256]{1,0:T(8,128)S(1)}, u32[]{:S(2)}, u32[]{:S(2)}) collective-permute-start(f32[16,256]{1,0:T(8,128)S(1)} %down.1.refs_1_), channel_id=1, source_target_pairs={{0,2},{1,3},{2,0},{3,1},{4,6},{5,7},{6,4},{7,5},{8,10},{9,11},{10,... | collective-permute-start | bytes 49160 | tf_op jit(solution)/shard_map/ppermute | solution.py:541
  54.1 3.2 %collective-permute-start.3 = (f32[16,256]{1,0:T(8,128)S(1)}, f32[16,256]{1,0:T(8,128)S(1)}, u32[]{:S(2)}, u32[]{:S(2)}) collective-permute-start(f32[16,256]{1,0:T(8,128)S(1)} %down.1.refs_1_), channel_id=1, source_target_pairs={{0,1},{1,2},{2,3},{3,0},{4,5},{5,6},{6,7},{7,4},{8,9},{9,10},{10,1... | collective-permute-start | bytes 49160 | tf_op jit(solution)/shard_map/ppermute | solution.py:541
  78.6 1.5 %collective-permute-start.8 = (f32[16,256]{1,0:T(8,128)S(1)}, f32[16,256]{1,0:T(8,128)S(1)}, u32[]{:S(2)}, u32[]{:S(2)}) collective-permute-start(f32[16,256]{1,0:T(8,128)S(1)} %combine.3.refs_1_), channel_id=1, source_target_pairs={{0,3},{1,0},{2,1},{3,2},{4,7},{5,4},{6,5},{7,6},{8,11},{9,8},{10,9... | collective-permute-start | bytes 49160 | tf_op jit(solution)/shard_map/ppermute | solution.py:541
  78.6 3.8 %collective-permute-start.7 = (f32[16,256]{1,0:T(8,128)S(1)}, f32[16,256]{1,0:T(8,128)S(1)}, u32[]{:S(2)}, u32[]{:S(2)}) collective-permute-start(f32[16,256]{1,0:T(8,128)S(1)} %combine.3.refs_1_), channel_id=1, source_target_pairs={{0,2},{1,3},{2,0},{3,1},{4,6},{5,7},{6,4},{7,5},{8,10},{9,11},{10,... | collective-permute-start | bytes 49160 | tf_op jit(solution)/shard_map/ppermute | solution.py:541
  79.4 3.2 %collective-permute-start.6 = (f32[16,256]{1,0:T(8,128)S(1)}, f32[16,256]{1,0:T(8,128)S(1)}, u32[]{:S(2)}, u32[]{:S(2)}) collective-permute-start(f32[16,256]{1,0:T(8,128)S(1)} %combine.3.refs_1_), channel_id=1, source_target_pairs={{0,1},{1,2},{2,3},{3,0},{4,5},{5,6},{6,7},{7,4},{8,9},{9,10},{10,1... | collective-permute-start | bytes 49160 | tf_op jit(solution)/shard_map/ppermute | solution.py:541
  102.2 1.2 %collective-permute-start.9 = (f32[16,128]{1,0:T(8,128)S(1)}, f32[16,128]{1,0:T(8,128)S(1)}, u32[]{:S(2)}, u32[]{:S(2)}) collective-permute-start(f32[16,128]{1,0:T(8,128)S(1)} %get-tuple-element.49), channel_id=1, source_target_pairs={{0,1},{1,0},{2,3},{3,2},{4,5},{5,4},{6,7},{7,6},{8,9},{9,8},{10,11... | collective-permute-start | bytes 24584 | tf_op jit(solution)/shard_map/ppermute | solution.py:662

commit v4 on v3

--- a/solution.py
+++ b/solution.py
@@ -184,6 +184,8 @@
 
 LANES = 128
 VMEM_ROOM = 8 << 20
+QUARTER = LANES // 4
+NEW_AT = 2 * QUARTER
 
 
 def lane_ids(shape):
@@ -194,6 +196,17 @@
     wide = jnp.broadcast_to(value, lane.shape)
     high = wide.astype(jnp.bfloat16).astype(jnp.float32)
     return jnp.where(lane == 0, high, jnp.where(lane == 1, wide - high, 0.0)).astype(jnp.bfloat16)
+
+
+def member_order(n_seq, odd):
+    if n_seq != 8:
+        return list(range(n_seq))
+    return [3, 2, 6, 7, 5, 4, 0, 1] if odd else [0, 1, 3, 2, 6, 7, 5, 4]
+
+
+def position_of(member, n_seq):
+    even, odd = (member_order(n_seq, side).index(member) for side in (False, True))
+    return jnp.where(lax.axis_index("tp") % 2 == 0, even, odd)
 
 
 def square_sum(own):
@@ -221,15 +234,38 @@
     )(*args)
 
 
+def to_row(column):
+    shape = (column.shape[0], LANES)
+    row = lax.broadcasted_iota(jnp.int32, shape, 0)
+    return jnp.sum(jnp.where(lane_ids(shape) == row, column, 0.0), axis=0, keepdims=True)
+
+
+def to_column(line, requests):
+    shape = (requests, LANES)
+    row = lax.broadcasted_iota(jnp.int32, shape, 0)
+    return jnp.sum(jnp.where(lane_ids(shape) == row, line, 0.0), axis=1, keepdims=True)
+
+
 def project_body(own, weights, out_ref):
-    part = [dot32(own, w).astype(jnp.bfloat16) for w in weights]
-    lane = lane_ids((own.shape[0], LANES))
-    part.append(as_hi_lo(square_sum(own), lane))
-    for member in range(out_ref.shape[0]):
-        at = 0
-        for piece in part:
-            out_ref[member, :, at : at + piece.shape[1]] = piece
-            at += piece.shape[1]
+    requests = own.shape[0]
+    members = out_ref.shape[0]
+    per = requests // members
+    query, key, value = [dot32(own, w) for w in weights]
+    width = query.shape[1]
+    query = query.astype(jnp.bfloat16)
+    line = to_row(square_sum(own))
+    high = line.astype(jnp.bfloat16).astype(jnp.float32)
+    row = lax.broadcasted_iota(jnp.int32, (requests, LANES), 0)
+    base = jnp.where(row == 2 * per, high, jnp.where(row == 2 * per + 1, line - high, 0.0))
+    for member in range(members):
+        block = base
+        for r in range(per):
+            at = member * per + r
+            block = jnp.where(row == 2 * r, key[at : at + 1], block)
+            block = jnp.where(row == 2 * r + 1, value[at : at + 1], block)
+        place = position_of(member, members)
+        out_ref[place, :, :width] = query
+        out_ref[place, :, width:] = block.astype(jnp.bfloat16)
 
 
 def first_kernel(n_more, *refs):
@@ -281,22 +317,33 @@
 
 def store_kernel(keep_ref, length_ref, key_ref, value_ref, *refs):
     layers, requests, block, _ = key_ref.shape
-    fresh_rows = refs[: 2 * layers]
-    key_out, value_out, token_ref, key_here, value_here, sems = refs[2 * layers :]
+    sent_refs = refs[:layers]
+    key_out, value_out, token_ref, key_here, value_here, sems = refs[layers:]
     token_ref[...] = jnp.zeros_like(token_ref)
     fresh = length_ref[...] - lax.axis_index("seq") * block
     slot = lax.broadcasted_iota(jnp.int32, (block, LANES), 0)
+    row = lax.broadcasted_iota(jnp.int32, (requests, LANES), 0)
+    quarter_here = lane_ids((requests, LANES)) // QUARTER
     copies = []
     for layer in range(layers):
-        for i, (old, here, out) in enumerate(
-            [(key_ref, key_here, key_out), (value_ref, value_here, value_out)]
-        ):
-            new = fresh_rows[2 * layer + i][...].astype(jnp.float32)
-            for b in range(requests):
-                row = jnp.where(
-                    slot == fresh[b : b + 1], new[b : b + 1], old[layer, b].astype(jnp.float32)
-                )
-                here[layer, b] = row.astype(jnp.bfloat16)
+        members, _, span = sent_refs[layer].shape
+        per = requests // members
+        for member in range(members):
+            sent = sent_refs[layer][position_of(member, members), :, span - LANES :]
+            sent = sent.astype(jnp.float32)
+            wide = jnp.zeros((requests, LANES), jnp.float32)
+            for quarter in range(4):
+                shifted = pltpu.roll(sent, (QUARTER * quarter - NEW_AT) % LANES, 1)
+                wide = jnp.where((quarter_here == quarter) & (row % 4 == quarter), shifted, wide)
+            for r in range(per):
+                b = member * per + r
+                here = slot == fresh[b : b + 1]
+                for i, (old, new_here) in enumerate([(key_ref, key_here), (value_ref, value_here)]):
+                    j = 4 * (2 * r + i)
+                    new = jnp.sum(wide[j : j + 4], axis=0, keepdims=True)
+                    kept = jnp.where(here, new, old[layer, b].astype(jnp.float32))
+                    new_here[layer, b] = kept.astype(jnp.bfloat16)
+        for i, (here, out) in enumerate([(key_here, key_out), (value_here, value_out)]):
             copies.append(
                 pltpu.make_async_copy(here.at[layer], out.at[layer], sems.at[2 * layer + i])
             )
@@ -347,12 +394,14 @@
 
 def attend_kernel(
     layer, width, heads, kv_heads, got_ref, cos_ref, sin_ref, length_ref,
-    key_ref, value_ref, out_ref, key_new_ref, value_new_ref,
+    key_ref, value_ref, out_ref,
 ):
     members, requests, _ = got_ref.shape
     query_width = heads * HEAD_DIM
     repeat = heads // kv_heads
     block = key_ref.shape[2]
+    per = requests // members
+    place = lax.axis_index("seq")
 
     def summed(at):
         total = got_ref[0, :, at : at + LANES].astype(jnp.float32)
@@ -362,74 +411,96 @@
 
     lane = lane_ids((requests, LANES))
     low = lane < HEAD_DIM
-    side = summed(query_width + 2 * kv_heads * HEAD_DIM)
-    spread = (side[:, 0:1] + side[:, 1:2]) * (1.0 / width)
-    inv = lax.rsqrt(spread + eps_norm)
-    cosine = cos_ref[...]
-    sine = sin_ref[...]
+    fresh_sums = summed(query_width)
+    spread = (fresh_sums[2 * per : 2 * per + 1] + fresh_sums[2 * per + 1 : 2 * per + 2]) * (
+        1.0 / width
+    )
+    inv_line = lax.rsqrt(spread + eps_norm)
+    inv = to_column(inv_line, requests)
     half = HEAD_DIM // 2
 
-    def rotated(at):
-        x = summed(at) * inv
-        other = jnp.where(
-            lane % HEAD_DIM < half, pltpu.roll(x, LANES - half, 1), pltpu.roll(x, half, 1)
-        )
+    def rotated(x, cosine, sine):
+        first = lane_ids(x.shape) % HEAD_DIM < half
+        other = jnp.where(first, pltpu.roll(x, LANES - half, 1), pltpu.roll(x, half, 1))
         return x * cosine + other * sine
 
     stacked = []
     for pair in range(heads // 2):
-        x = rotated(pair * LANES)
+        x = rotated(summed(pair * LANES) * inv, cos_ref[...], sin_ref[...])
         turned = pltpu.roll(x, HEAD_DIM, 1)
         if 2 * pair // repeat == 0:
             stacked += [jnp.where(low, x, 0.0), jnp.where(low, turned, 0.0)]
         else:
             stacked += [jnp.where(low, 0.0, turned), jnp.where(low, 0.0, x)]
     query = jnp.concatenate(stacked, axis=0).astype(jnp.bfloat16)
-    key_new = rotated(query_width).astype(jnp.bfloat16)
-    value_new = (summed(query_width + LANES) * inv).astype(jnp.bfloat16)
-    key_new_ref[...] = key_new
-    value_new_ref[...] = value_new
-
-    fresh = length_ref[...] - lax.axis_index("seq") * block
-    slot = lax.broadcasted_iota(jnp.int32, (block, LANES), 0)
-    keys = []
-    values = []
-    for b in range(requests):
-        here = slot == fresh[b : b + 1]
-        k = key_ref[layer, b].astype(jnp.float32)
-        v = value_ref[layer, b].astype(jnp.float32)
-        keys.append(jnp.where(here, key_new[b : b + 1].astype(jnp.float32), k).astype(jnp.bfloat16))
-        values.append(
-            jnp.where(here, value_new[b : b + 1].astype(jnp.float32), v).astype(jnp.bfloat16)
-        )
-    keys = jnp.concatenate(keys, axis=0)
-    values = jnp.concatenate(values, axis=0)
+
+    request = lax.broadcasted_iota(jnp.int32, (requests, LANES), 0)
+    key_new = jnp.zeros((requests, LANES), jnp.float32)
+    value_new = jnp.zeros((requests, LANES), jnp.float32)
+    rows = []
+    for r in range(per):
+        at = place * per + r
+        scale = jnp.sum(
+            jnp.where(lane_ids((1, LANES)) == at, inv_line, 0.0), axis=1, keepdims=True
+        )
+        key = rotated(
+            fresh_sums[2 * r : 2 * r + 1] * scale, cos_ref[pl.ds(at, 1)], sin_ref[pl.ds(at, 1)]
+        )
+        key = key.astype(jnp.bfloat16).astype(jnp.float32)
+        value = (fresh_sums[2 * r + 1 : 2 * r + 2] * scale).astype(jnp.bfloat16).astype(jnp.float32)
+        key_new = jnp.where(request == at, key, key_new)
+        value_new = jnp.where(request == at, value, value_new)
+        rows += [key, value]
+    owned = jnp.concatenate([request // per == place] * heads, axis=0)
+
+    def per_head(x):
+        return jnp.concatenate([x] * heads, axis=0)
+
+    to_scores = 1.0 / math.sqrt(HEAD_DIM)
+    fresh_scores = (
+        jnp.sum(query.astype(jnp.float32) * per_head(key_new), axis=1, keepdims=True) * to_scores
+    )
+    owned_row = owned[:, 0:1]
+    fresh_scores = jnp.where(owned_row, fresh_scores, neg_fill)
+
+    keys = key_ref[layer].reshape(requests * block, LANES)
+    values = value_ref[layer].reshape(requests * block, LANES)
     scores = lax.dot_general(
         query, keys, (((1,), (1,)), ((), ())), preferred_element_type=jnp.float32
-    ) * (1.0 / math.sqrt(HEAD_DIM))
-    begin = lax.broadcasted_iota(jnp.int32, (requests, LANES), 0) * block
-    end = begin + jnp.clip(fresh + 1, 0, block)
+    ) * to_scores
+    begin = request * block
+    end = begin + jnp.clip(length_ref[...] - place * block, 0, block)
     copies = scores.shape[1] // LANES
-    begin = jnp.concatenate([jnp.concatenate([begin] * heads, axis=0)] * copies, axis=1)
-    end = jnp.concatenate([jnp.concatenate([end] * heads, axis=0)] * copies, axis=1)
+    begin = jnp.concatenate([per_head(begin)] * copies, axis=1)
+    end = jnp.concatenate([per_head(end)] * copies, axis=1)
     column = lane_ids(scores.shape)
     live = (column >= begin) & (column < end)
     scores = jnp.where(live, scores, neg_fill)
-    top = jnp.max(scores, axis=1, keepdims=True)
+    top = jnp.maximum(jnp.max(scores, axis=1, keepdims=True), fresh_scores)
     weights = jnp.where(live, jnp.exp(scores - top), 0.0)
-    sums = jnp.sum(weights, axis=1, keepdims=True)
+    fresh_weights = jnp.where(owned_row, jnp.exp(fresh_scores - top), 0.0)
+    sums = jnp.sum(weights, axis=1, keepdims=True) + fresh_weights
     acc = dot32(weights.astype(jnp.bfloat16), values)
+    acc = acc + fresh_weights.astype(jnp.bfloat16).astype(jnp.float32) * per_head(value_new)
     turned = pltpu.roll(acc, HEAD_DIM, 1)
 
     side = jnp.zeros((requests, LANES), jnp.float32)
     for h in range(heads):
-        rows = slice(h * requests, (h + 1) * requests)
+        part = slice(h * requests, (h + 1) * requests)
         for group in range(5):
-            side = jnp.where(lane == group * heads + h, (top if group < 3 else sums)[rows], side)
+            side = jnp.where(lane == group * heads + h, (top if group < 3 else sums)[part], side)
+    spare = jnp.zeros((requests, LANES), jnp.float32)
+    for j, line in enumerate(rows):
+        spare = jnp.where(request // 4 == j, line, spare)
+    for quarter in range(4):
+        shifted = pltpu.roll(spare, (NEW_AT - QUARTER * quarter) % LANES, 1)
+        side = jnp.where(
+            (lane >= NEW_AT) & (lane < NEW_AT + QUARTER) & (request % 4 == quarter), shifted, side
+        )
     one = side.astype(jnp.bfloat16).astype(jnp.float32)
     two = (side - one).astype(jnp.bfloat16).astype(jnp.float32)
     three = side - one - two
-    second = ((lane >= heads) & (lane < 2 * heads)) | (lane >= 4 * heads)
+    second = ((lane >= heads) & (lane < 2 * heads)) | ((lane >= 4 * heads) & (lane < 5 * heads))
     third = (lane >= 2 * heads) & (lane < 3 * heads)
     side = jnp.where(third, three, jnp.where(second, two, one)).astype(jnp.bfloat16)
     pieces = []
@@ -486,11 +557,12 @@
     side = as_hi_lo(square_sum(mid), lane_ids((mid.shape[0], LANES)))
     members = out_ref.shape[0]
     own = gate_ref.shape[2] // members
-    for member, owner in enumerate(member_order(members)):
-        cols = slice(owner * own, (owner + 1) * own)
-        out_ref[member, :, :own] = dot32(mid, gate_ref[layer, :, cols]).astype(jnp.bfloat16)
-        out_ref[member, :, own : 2 * own] = dot32(mid, up_ref[layer, :, cols]).astype(jnp.bfloat16)
-        out_ref[member, :, 2 * own :] = side
+    for member in range(members):
+        cols = slice(member * own, (member + 1) * own)
+        place = position_of(member, members)
+        out_ref[place, :, :own] = dot32(mid, gate_ref[layer, :, cols]).astype(jnp.bfloat16)
+        out_ref[place, :, own : 2 * own] = dot32(mid, up_ref[layer, :, cols]).astype(jnp.bfloat16)
+        out_ref[place, :, 2 * own :] = side
 
 
 def silu_kernel(width, got_ref, out_ref):
@@ -508,8 +580,8 @@
 
 
 def in_order(got_ref):
-    order = member_order(got_ref.shape[0])
-    return jnp.concatenate([got_ref[order.index(m)] for m in range(len(order))], axis=1)
+    members = got_ref.shape[0]
+    return jnp.concatenate([got_ref[position_of(m, members)] for m in range(members)], axis=1)
 
 
 def down_kernel(layer, got_ref, w_ref, out_ref):
@@ -525,13 +597,8 @@
     give_ref[...] = half_of(part, 1 - core)
 
 
-def member_order(n_seq):
-    return [0, 7, 2, 5, 1, 6, 3, 4] if n_seq == 8 else list(range(n_seq))
-
-
 def make_with_kernels(n_seq, n_tp):
-    order = member_order(n_seq)
-    groups = [[s * n_tp + t for s in order] for t in range(n_tp)]
+    groups = [[s * n_tp + t for s in member_order(n_seq, t % 2 == 1)] for t in range(n_tp)]
 
     def swap(chunks):
         return lax.all_to_all(chunks, ("seq", "tp"), 0, 0, axis_index_groups=groups)
@@ -569,11 +636,10 @@
         def shape(dims, kind):
             return pltpu.VMEM(dims, kind)
 
-        packed_shape = shape((n_seq, requests, query_width + 2 * kv_width + LANES), bf16)
+        packed_shape = shape((n_seq, requests, query_width + LANES), bf16)
         part_shape = shape((requests, col_count), f32)
         own_shape = shape((requests, col_count), bf16)
-        new_shape = shape((requests, kv_width), bf16)
-        fresh_rows = []
+        sent = []
         packed_weights = (query_weight, key_weight, value_weight)
         table_shape = (requests, LANES)
         stored = (key_cache, value_cache, out_weight, gate_weight, up_weight)
@@ -611,9 +677,9 @@
                     *packed_weights,
                     name="next",
                 )
-            packed, key_new, value_new = call(
+            packed = call(
                 functools.partial(attend_kernel, layer, width, heads, kv_heads),
-                (shape((n_seq, requests, query_width + LANES), bf16), new_shape, new_shape),
+                packed_shape,
                 swap(packed),
                 cosine,
                 sine,
@@ -622,11 +688,11 @@
                 values,
                 name="attend",
                 )
-            fresh_rows += [key_new, value_new]
+            sent.append(swap(packed))
             part = call(
                 functools.partial(combine_kernel, layer, heads),
                 part_shape,
-                swap(packed),
+                sent[-1],
                 out_here,
                 name="combine",
             )
@@ -669,7 +735,7 @@
             length_table,
             key_cache,
             value_cache,
-            *fresh_rows,
+            *sent,
             name="store",
             out_specs=[hbm, hbm, pl.BlockSpec(memory_space=pltpu.VMEM)],
             scratch=[pltpu.VMEM(key_cache.shape, bf16)] * 2
@@ -706,6 +772,7 @@
             and n_tp % 2 == 0
             and gate_weight.shape[2] // n_seq % LANES == 0
             and key_cache.shape[3] == LANES
+            and args[0].shape[0] == 2 * n_seq
         )
         make = make_with_kernels if aligned else make_plain
         return make(n_seq, n_tp)(*args)

time: 115 us -> 112 us (0.974)
  blocking collectives: 92.3 us -> 89.4 us
    all_to_all x8, blocking collectives: 82.1 us -> 79.3 us  [swap(): return lax.all_to_all(chunks, ('seq', 'tp'), 0, 0, axis_index_groups=groups)]
where the time goes in v4:
time: 112 us
  blocking collectives  89.4 us (80%)
  waiting for transfers between devices  8.9 us (8%)
  Pallas kernels  8.66 us (8%)
  starting transfers between devices  4.19 us (4%)
    all_to_all x8, blocking collectives, swap(): return lax.all_to_all(chunks, ('seq', 'tp'), 0, 0, axis_index_groups=groups)  79.3 us
    all_to_all x1, blocking collectives, per_device(): stream = lax.all_to_all(stream, ('seq', 'tp'), 0, 0)  10 us
    ppermute x9, waiting for transfers between devices, tp_parts(): lax.ppermute(part, 'tp', [(i, (i + k) % n_tp) for i in range(n_tp)])  8.9 us
    pallas_call x15, Pallas kernels, call(): pl.pallas_call(body, out_shape=out_shape, in_specs=[where] * len(args), o...  8.66 us
    ppermute x9, starting transfers between devices, tp_parts(): lax.ppermute(part, 'tp', [(i, (i + k) % n_tp) for i in range(n_tp)])  4.18 us
  transfers between devices with their start and end apart: 10, of which 8 were waited for; matrix products, arithmetic and copies ran while one was open for 0% of the time, Pallas kernels for 1%

profile of v4, /device:TPU:0, one launch (start us, length us, event | category | flops | bytes accessed | tf_op | source)
XLA Modules:
  0.0 111.9 jit_solution(15591137024523657799)
XLA Ops:
  0.6 2.1 %first.1 = (bf16[16,256]{1,0:T(8,128)(2,1)S(1)}, f32[16,128]{1,0:T(8,128)S(1)}, f32[16,128]{1,0:T(8,128)S(1)}, s32[16,128]{1,0:T(8,128)S(1)}, bf16[8,16,640]{2,1...) custom-call(bf16[16,2048]{1,0:T(8,128)(2,1)} %refs_0_.1, ...), custom_call_target="tpu_custom_call" | custom-call | tf_op jit(solution)/shard_map/first/pallas_call | solution.py:226
  2.7 13.9 %all_to_all.45.got_ref = bf16[8,16,640]{2,1,0:T(8,128)(2,1)S(1)} all-to-all(bf16[8,16,640]{2,1,0:T(8,128)(2,1)S(1)} %get-tuple-element.25), channel_id=1, replica_groups={{0,4,12,8,24,28,20,16},{13,9,25,29,21,17,1,5},{2,6,14,10,26,30,22,18},{..., dimensions={0} | all-to-all | bytes 327680 | tf_op jit(solution)/shard_map/all_to_all | solution.py:604
  16.6 0.9 attend.2
  17.5 9.4 %all_to_all.46.got_ref.refs_0_ = bf16[8,16,640]{2,1,0:T(8,128)(2,1)S(1)} all-to-all(bf16[8,16,640]{2,1,0:T(8,128)(2,1)S(1)} %attend.2), channel_id=1, replica_groups={{0,4,12,8,24,28,20,16},{13,9,25,29,21,17,1,5},{2,6,14,10,26,30,22,18},{..., dimensions={0} | all-to-all | bytes 327680 | tf_op jit(solution)/shard_map/all_to_all | solution.py:604
  27.0 0.5 combine.2.refs_1_
  27.4 0.0 collective-permute-start.2
  27.4 1.6 %collective-permute-start.1 = (f32[16,256]{1,0:T(8,128)S(1)}, f32[16,256]{1,0:T(8,128)S(1)}, u32[]{:S(2)}, u32[]{:S(2)}) collective-permute-start(f32[16,256]{1,0:T(8,128)S(1)} %combine.2.refs_1_), channel_id=1, source_target_pairs={{0,2},{1,3},{2,0},{3,1},{4,6},{5,7},{6,4},{7,5},{8,10},{9,11},{10,... | collective-permute-start | bytes 49160 | tf_op jit(solution)/shard_map/ppermute | solution.py:608
  29.0 0.2 collective-permute-start
  29.2 0.0 collective-permute-done.2.refs_4_
  29.2 2.0 %collective-permute-done.1.refs_3_ = f32[16,256]{1,0:T(8,128)S(1)} collective-permute-done((f32[16,256]{1,0:T(8,128)S(1)}, f32[16,256]{1,0:T(8,128)S(1)}, u32[]{:S(2)}, u32[]{:S(2)}) %collective-permute-start.1) | collective-permute-done | bytes 16416 | tf_op jit(solution)/shard_map/ppermute | solution.py:608
  31.2 0.9 collective-permute-done.refs_2_
  32.2 0.4 widen.2
  32.6 9.5 %all_to_all.47.got_ref = bf16[8,16,640]{2,1,0:T(8,128)(2,1)S(1)} all-to-all(bf16[8,16,640]{2,1,0:T(8,128)(2,1)S(1)} %get-tuple-element.35), channel_id=1, replica_groups={{0,4,12,8,24,28,20,16},{13,9,25,29,21,17,1,5},{2,6,14,10,26,30,22,18},{..., dimensions={0} | all-to-all | bytes 327680 | tf_op jit(solution)/shard_map/all_to_all | solution.py:604
  42.1 0.2 silu.2
  42.3 9.1 %all_to_all.48.got_ref = bf16[8,16,256]{2,1,0:T(8,128)(2,1)S(1)} all-to-all(bf16[8,16,256]{2,1,0:T(8,128)(2,1)S(1)} %silu.2), channel_id=1, replica_groups={{0,4,12,8,24,28,20,16},{13,9,25,29,21,17,1,5},{2,6,14,10,26,30,22,18},{..., dimensions={0} | all-to-all | bytes 131072 | tf_op jit(solution)/shard_map/all_to_all | solution.py:604
  51.4 0.0 copy-done.2
  51.4 0.2 down.1.refs_1_
  51.7 0.0 collective-permute-start.5
  51.7 1.0 collective-permute-start.4
  52.6 0.2 collective-permute-start.3
  52.8 0.3 collective-permute-done.5.refs_4_
  53.1 2.4 %collective-permute-done.4.refs_3_ = f32[16,256]{1,0:T(8,128)S(1)} collective-permute-done((f32[16,256]{1,0:T(8,128)S(1)}, f32[16,256]{1,0:T(8,128)S(1)}, u32[]{:S(2)}, u32[]{:S(2)}) %collective-permute-start.4) | collective-permute-done | bytes 16416 | tf_op jit(solution)/shard_map/ppermute | solution.py:608
  55.5 0.3 collective-permute-done.3.refs_2_
  55.8 0.0 copy-done.5
  55.8 0.0 copy-done.8
  55.8 0.2 next.1
  56.0 9.3 %all_to_all.49.got_ref = bf16[8,16,640]{2,1,0:T(8,128)(2,1)S(1)} all-to-all(bf16[8,16,640]{2,1,0:T(8,128)(2,1)S(1)} %get-tuple-element.37), channel_id=1, replica_groups={{0,4,12,8,24,28,20,16},{13,9,25,29,21,17,1,5},{2,6,14,10,26,30,22,18},{..., dimensions={0} | all-to-all | bytes 327680 | tf_op jit(solution)/shard_map/all_to_all | solution.py:604
  65.3 0.0 copy-done.3
  65.3 0.9 attend.3
  66.2 9.6 %all_to_all.50.got_ref.refs_1_ = bf16[8,16,640]{2,1,0:T(8,128)(2,1)S(1)} all-to-all(bf16[8,16,640]{2,1,0:T(8,128)(2,1)S(1)} %attend.3), channel_id=1, replica_groups={{0,4,12,8,24,28,20,16},{13,9,25,29,21,17,1,5},{2,6,14,10,26,30,22,18},{..., dimensions={0} | all-to-all | bytes 327680 | tf_op jit(solution)/shard_map/all_to_all | solution.py:604
  75.8 0.5 combine.3.refs_1_
  76.2 0.0 collective-permute-start.8
  76.3 1.0 collective-permute-start.7
  77.3 0.2 collective-permute-start.6
  77.5 0.3 collective-permute-done.8.refs_4_
  77.7 2.3 %collective-permute-done.7.refs_3_ = f32[16,256]{1,0:T(8,128)S(1)} collective-permute-done((f32[16,256]{1,0:T(8,128)S(1)}, f32[16,256]{1,0:T(8,128)S(1)}, u32[]{:S(2)}, u32[]{:S(2)}) %collective-permute-start.7) | collective-permute-done | bytes 16416 | tf_op jit(solution)/shard_map/ppermute | solution.py:608
  80.1 0.4 collective-permute-done.6.refs_2_
  80.4 0.0 copy-done.1
  80.5 0.4 widen.3
  80.8 9.4 %all_to_all.51.got_ref = bf16[8,16,640]{2,1,0:T(8,128)(2,1)S(1)} all-to-all(bf16[8,16,640]{2,1,0:T(8,128)(2,1)S(1)} %get-tuple-element.39), channel_id=1, replica_groups={{0,4,12,8,24,28,20,16},{13,9,25,29,21,17,1,5},{2,6,14,10,26,30,22,18},{..., dimensions={0} | all-to-all | bytes 327680 | tf_op jit(solution)/shard_map/all_to_all | solution.py:604
  90.3 0.2 silu.3
  90.4 9.1 %all_to_all.52.got_ref = bf16[8,16,256]{2,1,0:T(8,128)(2,1)S(1)} all-to-all(bf16[8,16,256]{2,1,0:T(8,128)(2,1)S(1)} %silu.3), channel_id=1, replica_groups={{0,4,12,8,24,28,20,16},{13,9,25,29,21,17,1,5},{2,6,14,10,26,30,22,18},{..., dimensions={0} | all-to-all | bytes 131072 | tf_op jit(solution)/shard_map/all_to_all | solution.py:604
  99.5 0.2 down_last.1
  99.8 0.0 collective-permute-start.9
  99.8 1.4 %store.1 = (bf16[2,16,64,128]{3,2,1,0:T(8,128)(2,1)}, bf16[2,16,64,128]{3,2,1,0:T(8,128)(2,1)}, f32[8,128]{1,0:T(8,128)S(1)}) custom-call(f32[16,128]{1,0:T(8,128)S(1)} %get-tuple-element.40.keep_ref, s32[16,128]{1,0:T(8,128)S(1)} %get-tuple-element.28.length_ref, bf16[2,16,64,128]{3,2,1,0:T(8,128)(2,1)S(1)} %copy-done.3, ...), custom_call_target="tpu_custom_call" | custom-call | tf_op jit(solution)/shard_map/store/pallas_call | solution.py:226
  101.2 0.0 collective-permute-done.9.got_ref
  101.2 10.0 %all_to_all.53.got_ref = bf16[32,16,128]{2,1,0:T(8,128)(2,1)S(1)} all-to-all(bf16[32,16,128]{2,1,0:T(8,128)(2,1)S(1)} %meet.1), channel_id=1, replica_groups=mesh['seq'=8,'tp'=4] {'seq','tp'}, dimensions={0} | all-to-all | bytes 262144 | tf_op jit(solution)/shard_map/all_to_all | solution.py:753
  111.2 0.6 last.1
  (14 shorter events, 0.0 us)
Async XLA Ops:
  16.6 34.8 %copy-start.2 = (bf16[2,2048,256]{2,1,0:T(8,128)(2,1)S(1)}, bf16[2,2048,256]{2,1,0:T(8,128)(2,1)}, u32[]{:S(2)}) copy-start(bf16[2,2048,256]{2,1,0:T(8,128)(2,1)} %w_ref.5) | copy-start | bytes 6291460
  27.4 1.8 %collective-permute-start.2 = (f32[16,256]{1,0:T(8,128)S(1)}, f32[16,256]{1,0:T(8,128)S(1)}, u32[]{:S(2)}, u32[]{:S(2)}) collective-permute-start(f32[16,256]{1,0:T(8,128)S(1)} %combine.2.refs_1_), channel_id=1, source_target_pairs={{0,3},{1,0},{2,1},{3,2},{4,7},{5,4},{6,5},{7,6},{8,11},{9,8},{10,9... | collective-permute-start | bytes 49160 | tf_op jit(solution)/shard_map/ppermute | solution.py:608
  27.4 3.8 %collective-permute-start.1 = (f32[16,256]{1,0:T(8,128)S(1)}, f32[16,256]{1,0:T(8,128)S(1)}, u32[]{:S(2)}, u32[]{:S(2)}) collective-permute-start(f32[16,256]{1,0:T(8,128)S(1)} %combine.2.refs_1_), channel_id=1, source_target_pairs={{0,2},{1,3},{2,0},{3,1},{4,6},{5,7},{6,4},{7,5},{8,10},{9,11},{10,... | collective-permute-start | bytes 49160 | tf_op jit(solution)/shard_map/ppermute | solution.py:608
  29.0 3.2 %collective-permute-start = (f32[16,256]{1,0:T(8,128)S(1)}, f32[16,256]{1,0:T(8,128)S(1)}, u32[]{:S(2)}, u32[]{:S(2)}) collective-permute-start(f32[16,256]{1,0:T(8,128)S(1)} %combine.2.refs_1_), channel_id=1, source_target_pairs={{0,1},{1,2},{2,3},{3,0},{4,5},{5,6},{6,7},{7,4},{8,9},{9,10},{10,1... | collective-permute-start | bytes 49160 | tf_op jit(solution)/shard_map/ppermute | solution.py:608
  32.2 23.6 %copy-start.5 = (bf16[2,256,512]{2,1,0:T(8,128)(2,1)S(1)}, bf16[2,256,512]{2,1,0:T(8,128)(2,1)}, u32[]{:S(2)}) copy-start(bf16[2,256,512]{2,1,0:T(8,128)(2,1)} %refs_5_.4) | copy-start | bytes 1572868
  32.2 23.6 %copy-start.7 = (bf16[2,256,128]{2,1,0:T(8,128)(2,1)S(1)}, bf16[2,256,128]{2,1,0:T(8,128)(2,1)}, u32[]{:S(2)}) copy-start(bf16[2,256,128]{2,1,0:T(8,128)(2,1)} %refs_6_.4) | copy-start | bytes 393220
  32.2 23.6 %copy-start.8 = (bf16[2,256,128]{2,1,0:T(8,128)(2,1)S(1)}, bf16[2,256,128]{2,1,0:T(8,128)(2,1)}, u32[]{:S(2)}) copy-start(bf16[2,256,128]{2,1,0:T(8,128)(2,1)} %refs_7_.3) | copy-start | bytes 393220
  32.6 32.7 %copy-start.3 = (bf16[2,16,64,128]{3,2,1,0:T(8,128)(2,1)S(1)}, bf16[2,16,64,128]{3,2,1,0:T(8,128)(2,1)}, u32[]{:S(2)}) copy-start(bf16[2,16,64,128]{3,2,1,0:T(8,128)(2,1)} %key_ref.3) | copy-start | bytes 1572868
  32.6 32.7 %copy-start.4 = (bf16[2,16,64,128]{3,2,1,0:T(8,128)(2,1)S(1)}, bf16[2,16,64,128]{3,2,1,0:T(8,128)(2,1)}, u32[]{:S(2)}) copy-start(bf16[2,16,64,128]{3,2,1,0:T(8,128)(2,1)} %value_ref.3) | copy-start | bytes 1572868
  51.4 24.4 %copy-start.6 = (bf16[2,512,256]{2,1,0:T(8,128)(2,1)S(1)}, bf16[2,512,256]{2,1,0:T(8,128)(2,1)}, u32[]{:S(2)}) copy-start(bf16[2,512,256]{2,1,0:T(8,128)(2,1)} %w_ref.4) | copy-start | bytes 1572868
  51.4 29.0 %copy-start.1 = (bf16[2,256,2048]{2,1,0:T(8,128)(2,1)S(1)}, bf16[2,256,2048]{2,1,0:T(8,128)(2,1)}, u32[]{:S(2)}) copy-start(bf16[2,256,2048]{2,1,0:T(8,128)(2,1)} %refs_6_.5) | copy-start | bytes 6291460
  51.7 28.8 %copy-start = (bf16[2,256,2048]{2,1,0:T(8,128)(2,1)S(1)}, bf16[2,256,2048]{2,1,0:T(8,128)(2,1)}, u32[]{:S(2)}) copy-start(bf16[2,256,2048]{2,1,0:T(8,128)(2,1)} %refs_5_.5) | copy-start | bytes 6291460
  51.7 1.5 %collective-permute-start.5 = (f32[16,256]{1,0:T(8,128)S(1)}, f32[16,256]{1,0:T(8,128)S(1)}, u32[]{:S(2)}, u32[]{:S(2)}) collective-permute-start(f32[16,256]{1,0:T(8,128)S(1)} %down.1.refs_1_), channel_id=1, source_target_pairs={{0,3},{1,0},{2,1},{3,2},{4,7},{5,4},{6,5},{7,6},{8,11},{9,8},{10,9... | collective-permute-start | bytes 49160 | tf_op jit(solution)/shard_map/ppermute | solution.py:608
  51.7 3.8 %collective-permute-start.4 = (f32[16,256]{1,0:T(8,128)S(1)}, f32[16,256]{1,0:T(8,128)S(1)}, u32[]{:S(2)}, u32[]{:S(2)}) collective-permute-start(f32[16,256]{1,0:T(8,128)S(1)} %down.1.refs_1_), channel_id=1, source_target_pairs={{0,2},{1,3},{2,0},{3,1},{4,6},{5,7},{6,4},{7,5},{8,10},{9,11},{10,... | collective-permute-start | bytes 49160 | tf_op jit(solution)/shard_map/ppermute | solution.py:608
  52.6 3.2 %collective-permute-start.3 = (f32[16,256]{1,0:T(8,128)S(1)}, f32[16,256]{1,0:T(8,128)S(1)}, u32[]{:S(2)}, u32[]{:S(2)}) collective-permute-start(f32[16,256]{1,0:T(8,128)S(1)} %down.1.refs_1_), channel_id=1, source_target_pairs={{0,1},{1,2},{2,3},{3,0},{4,5},{5,6},{6,7},{7,4},{8,9},{9,10},{10,1... | collective-permute-start | bytes 49160 | tf_op jit(solution)/shard_map/ppermute | solution.py:608
  76.2 1.5 %collective-permute-start.8 = (f32[16,256]{1,0:T(8,128)S(1)}, f32[16,256]{1,0:T(8,128)S(1)}, u32[]{:S(2)}, u32[]{:S(2)}) collective-permute-start(f32[16,256]{1,0:T(8,128)S(1)} %combine.3.refs_1_), channel_id=1, source_target_pairs={{0,3},{1,0},{2,1},{3,2},{4,7},{5,4},{6,5},{7,6},{8,11},{9,8},{10,9... | collective-permute-start | bytes 49160 | tf_op jit(solution)/shard_map/ppermute | solution.py:608
  76.3 3.8 %collective-permute-start.7 = (f32[16,256]{1,0:T(8,128)S(1)}, f32[16,256]{1,0:T(8,128)S(1)}, u32[]{:S(2)}, u32[]{:S(2)}) collective-permute-start(f32[16,256]{1,0:T(8,128)S(1)} %combine.3.refs_1_), channel_id=1, source_target_pairs={{0,2},{1,3},{2,0},{3,1},{4,6},{5,7},{6,4},{7,5},{8,10},{9,11},{10,... | collective-permute-start | bytes 49160 | tf_op jit(solution)/shard_map/ppermute | solution.py:608
  77.3 3.2 %collective-permute-start.6 = (f32[16,256]{1,0:T(8,128)S(1)}, f32[16,256]{1,0:T(8,128)S(1)}, u32[]{:S(2)}, u32[]{:S(2)}) collective-permute-start(f32[16,256]{1,0:T(8,128)S(1)} %combine.3.refs_1_), channel_id=1, source_target_pairs={{0,1},{1,2},{2,3},{3,0},{4,5},{5,6},{6,7},{7,4},{8,9},{9,10},{10,1... | collective-permute-start | bytes 49160 | tf_op jit(solution)/shard_map/ppermute | solution.py:608
  99.8 1.4 %collective-permute-start.9 = (f32[16,128]{1,0:T(8,128)S(1)}, f32[16,128]{1,0:T(8,128)S(1)}, u32[]{:S(2)}, u32[]{:S(2)}) collective-permute-start(f32[16,128]{1,0:T(8,128)S(1)} %get-tuple-element.41), channel_id=1, source_target_pairs={{0,1},{1,0},{2,3},{3,2},{4,5},{5,4},{6,7},{7,6},{8,9},{9,8},{10,11... | collective-permute-start | bytes 24584 | tf_op jit(solution)/shard_map/ppermute | solution.py:728

commit v5 on v4

--- a/solution.py
+++ b/solution.py
@@ -204,6 +204,10 @@
     return [3, 2, 6, 7, 5, 4, 0, 1] if odd else [0, 1, 3, 2, 6, 7, 5, 4]
 
 
+def whole_order(n_seq, n_tp):
+    return [s * n_tp + (t ^ (t >> 1)) for s in member_order(n_seq, False) for t in range(n_tp)]
+
+
 def position_of(member, n_seq):
     even, odd = (member_order(n_seq, side).index(member) for side in (False, True))
     return jnp.where(lax.axis_index("tp") % 2 == 0, even, odd)
@@ -218,15 +222,18 @@
     return jnp.dot(a, b, preferred_element_type=jnp.float32)
 
 
-def call(body, out_shape, *args, name, held=True, scratch=(), out_specs=None):
-    vmem = pl.BlockSpec(memory_space=pltpu.VMEM)
-    where = vmem if held else pl.BlockSpec(memory_space=pltpu.HBM)
+def call(body, out_shape, *args, name, held=None, scratch=(), out_specs=None):
+    vmem, hbm = [pl.BlockSpec(memory_space=m) for m in (pltpu.VMEM, pltpu.HBM)]
+    held = len(args) if held is None else held
     single = not isinstance(out_shape, (tuple, list))
-    args = [pltpu.with_memory_space_constraint(a, pltpu.VMEM if held else pltpu.HBM) for a in args]
+    args = [
+        pltpu.with_memory_space_constraint(a, pltpu.VMEM if i < held else pltpu.HBM)
+        for i, a in enumerate(args)
+    ]
     return pl.pallas_call(
         body,
         out_shape=out_shape,
-        in_specs=[where] * len(args),
+        in_specs=[vmem if i < held else hbm for i in range(len(args))],
         out_specs=out_specs or (vmem if single else [vmem] * len(out_shape)),
         scratch_shapes=list(scratch),
         compiler_params=pltpu.CompilerParams(vmem_limit_bytes=VMEM_ROOM),
@@ -315,7 +322,7 @@
         copy.wait()
 
 
-def store_kernel(keep_ref, length_ref, key_ref, value_ref, *refs):
+def store_kernel(part_ref, length_ref, key_ref, value_ref, *refs):
     layers, requests, block, _ = key_ref.shape
     sent_refs = refs[:layers]
     key_out, value_out, token_ref, key_here, value_here, sems = refs[layers:]
@@ -372,7 +379,7 @@
     return jnp.where(core == 0, value[:, :middle], value[:, middle:])
 
 
-def meet_kernel(n_tp, mid_ref, keep_ref, got_ref, token_ref, out_ref):
+def meet_kernel(n_tp, mid_ref, keep_ref, got_ref, out_ref):
     place = lax.axis_index("tp")
     total = keep_ref[...] + got_ref[...]
     base = half_of(mid_ref[...].astype(jnp.float32), place % 2)
@@ -383,11 +390,12 @@
 
 def last_kernel(n_tp, got_ref, out_ref):
     span = got_ref.shape[2]
+    order = whole_order(got_ref.shape[0] // n_tp, n_tp)
     for block in range(got_ref.shape[0] // n_tp):
         for core in range(2):
-            total = got_ref[block * n_tp + core].astype(jnp.float32)
+            total = got_ref[order.index(block * n_tp + core)].astype(jnp.float32)
             for pair in range(1, n_tp // 2):
-                total = total + got_ref[block * n_tp + 2 * pair + core].astype(jnp.float32)
+                total = total + got_ref[order.index(block * n_tp + 2 * pair + core)].astype(jnp.float32)
             at = (2 * block + core) * span
             out_ref[:, at : at + span] = total.astype(jnp.bfloat16)
 
@@ -432,7 +440,8 @@
             stacked += [jnp.where(low, x, 0.0), jnp.where(low, turned, 0.0)]
         else:
             stacked += [jnp.where(low, 0.0, turned), jnp.where(low, 0.0, x)]
-    query = jnp.concatenate(stacked, axis=0).astype(jnp.bfloat16)
+    query = jnp.concatenate(stacked, axis=0).astype(jnp.bfloat16).astype(jnp.float32)
+    query = query * (1.0 / math.sqrt(HEAD_DIM))
 
     request = lax.broadcasted_iota(jnp.int32, (requests, LANES), 0)
     key_new = jnp.zeros((requests, LANES), jnp.float32)
@@ -456,18 +465,18 @@
     def per_head(x):
         return jnp.concatenate([x] * heads, axis=0)
 
-    to_scores = 1.0 / math.sqrt(HEAD_DIM)
-    fresh_scores = (
-        jnp.sum(query.astype(jnp.float32) * per_head(key_new), axis=1, keepdims=True) * to_scores
-    )
+    fresh_scores = jnp.sum(query * per_head(key_new), axis=1, keepdims=True)
     owned_row = owned[:, 0:1]
     fresh_scores = jnp.where(owned_row, fresh_scores, neg_fill)
 
     keys = key_ref[layer].reshape(requests * block, LANES)
     values = value_ref[layer].reshape(requests * block, LANES)
     scores = lax.dot_general(
-        query, keys, (((1,), (1,)), ((), ())), preferred_element_type=jnp.float32
-    ) * to_scores
+        query.astype(jnp.bfloat16),
+        keys,
+        (((1,), (1,)), ((), ())),
+        preferred_element_type=jnp.float32,
+    )
     begin = request * block
     end = begin + jnp.clip(length_ref[...] - place * block, 0, block)
     copies = scores.shape[1] // LANES
@@ -477,8 +486,9 @@
     live = (column >= begin) & (column < end)
     scores = jnp.where(live, scores, neg_fill)
     top = jnp.maximum(jnp.max(scores, axis=1, keepdims=True), fresh_scores)
-    weights = jnp.where(live, jnp.exp(scores - top), 0.0)
-    fresh_weights = jnp.where(owned_row, jnp.exp(fresh_scores - top), 0.0)
+    top = jnp.maximum(top, 0.5 * neg_fill)
+    weights = jnp.exp(scores - top)
+    fresh_weights = jnp.exp(fresh_scores - top)
     sums = jnp.sum(weights, axis=1, keepdims=True) + fresh_weights
     acc = dot32(weights.astype(jnp.bfloat16), values)
     acc = acc + fresh_weights.astype(jnp.bfloat16).astype(jnp.float32) * per_head(value_new)
@@ -551,7 +561,8 @@
 
 def widen_kernel(layer, n_parts, *refs):
     base_ref, parts = refs[0], refs[1 : 1 + n_parts]
-    gate_ref, up_ref, mid_ref, out_ref = refs[1 + n_parts :]
+    gate_ref, up_ref = refs[1 + n_parts : 3 + n_parts]
+    mid_ref, out_ref = refs[-2:]
     mid = sum_parts(base_ref, parts)
     mid_ref[...] = mid
     side = as_hi_lo(square_sum(mid), lane_ids((mid.shape[0], LANES)))
@@ -659,7 +670,7 @@
             *packed_weights,
             *stored,
             name="first",
-            held=False,
+            held=0,
             scratch=[pltpu.VMEM(w.shape[1:], bf16) for w in packed_weights]
             + [pltpu.SMEM((requests,), jnp.int32)] * 2
             + [pltpu.SemaphoreType.DMA((6 + len(stored),))],
@@ -667,7 +678,6 @@
         parts = None
         mid = None
         for layer in range(LAYERS):
-            keys, values, out_here, gate_here, up_here = early if layer == 0 else stored
             if layer > 0:
                 own, packed = call(
                     functools.partial(next_kernel, layer, n_tp),
@@ -677,6 +687,7 @@
                     *packed_weights,
                     name="next",
                 )
+            keys, values, out_here, gate_here, up_here = early if layer == 0 else stored
             packed = call(
                 functools.partial(attend_kernel, layer, width, heads, kv_heads),
                 packed_shape,
@@ -687,7 +698,7 @@
                 keys,
                 values,
                 name="attend",
-                )
+            )
             sent.append(swap(packed))
             part = call(
                 functools.partial(combine_kernel, layer, heads),
@@ -696,13 +707,33 @@
                 out_here,
                 name="combine",
             )
+            parts = tp_parts(part)
+            tokens = []
+            if layer + 1 == LAYERS:
+                cache_shape = jax.ShapeDtypeStruct(key_cache.shape, bf16)
+                hbm = pl.BlockSpec(memory_space=pltpu.HBM)
+                key_out, value_out, token = call(
+                    store_kernel,
+                    (cache_shape, cache_shape, shape((8, LANES), f32)),
+                    part,
+                    length_table,
+                    key_cache,
+                    value_cache,
+                    *sent,
+                    name="store",
+                    out_specs=[hbm, hbm, pl.BlockSpec(memory_space=pltpu.VMEM)],
+                    scratch=[pltpu.VMEM(key_cache.shape, bf16)] * 2
+                    + [pltpu.SemaphoreType.DMA((2 * LAYERS,))],
+                )
+                tokens = [token]
             mid, packed = call(
                 functools.partial(widen_kernel, layer, n_tp),
                 (own_shape, shape((n_seq, requests, 2 * ff_own + LANES), bf16)),
                 own,
-                *tp_parts(part),
+                *parts,
                 gate_here,
                 up_here,
+                *tokens,
                 name="widen",
             )
             hidden = call(
@@ -726,31 +757,16 @@
             name="down_last",
         )
         give = lax.ppermute(give, "tp", [(i, i ^ 1) for i in range(n_tp)])
-        cache_shape = jax.ShapeDtypeStruct(key_cache.shape, bf16)
-        hbm = pl.BlockSpec(memory_space=pltpu.HBM)
-        key_out, value_out, token = call(
-            store_kernel,
-            (cache_shape, cache_shape, shape((8, LANES), f32)),
-            keep,
-            length_table,
-            key_cache,
-            value_cache,
-            *sent,
-            name="store",
-            out_specs=[hbm, hbm, pl.BlockSpec(memory_space=pltpu.VMEM)],
-            scratch=[pltpu.VMEM(key_cache.shape, bf16)] * 2
-            + [pltpu.SemaphoreType.DMA((2 * LAYERS,))],
-        )
         stream = call(
             functools.partial(meet_kernel, n_tp),
             shape((n_seq * n_tp, requests, col_count // 2), bf16),
             mid,
             keep,
             give,
-            token,
             name="meet",
         )
-        stream = lax.all_to_all(stream, ("seq", "tp"), 0, 0)
+        everyone = [whole_order(n_seq, n_tp)]
+        stream = lax.all_to_all(stream, ("seq", "tp"), 0, 0, axis_index_groups=everyone)
         stream = call(
             functools.partial(last_kernel, n_tp),
             jax.ShapeDtypeStruct((requests, width), bf16),

time: 112 us -> 112 us (level)
    ppermute x9, waiting for transfers between devices: 8.9 us -> 7.48 us  [tp_parts(): lax.ppermute(part, 'tp', [(i, (i + k) % n_tp) for i in range(n_tp)])]
    ppermute x1, waiting for transfers between devices: 0.01 us -> 1.18 us  [per_device(): give = lax.ppermute(give, 'tp', [(i, i ^ 1) for i in range(n_tp)])]
where the time goes in v5:
time: 112 us; the launch traced here: 111 us
  blocking collectives  89.2 us (80%)
  waiting for transfers between devices  8.66 us (8%)
  Pallas kernels  8.61 us (8%)
  starting transfers between devices  4.14 us (4%)
    all_to_all x8, blocking collectives, swap(): return lax.all_to_all(chunks, ('seq', 'tp'), 0, 0, axis_index_groups=groups)  79.9 us
    all_to_all x1, blocking collectives, per_device(): lax.all_to_all(stream, ('seq', 'tp'), 0, 0, axis_index_groups=everyone)  9.36 us
    pallas_call x15, Pallas kernels, call(): pl.pallas_call(body, out_shape=out_shape, in_specs=[vmem if i < held else...  8.61 us
    ppermute x9, waiting for transfers between devices, tp_parts(): lax.ppermute(part, 'tp', [(i, (i + k) % n_tp) for i in range(n_tp)])  7.48 us
    ppermute x9, starting transfers between devices, tp_parts(): lax.ppermute(part, 'tp', [(i, (i + k) % n_tp) for i in range(n_tp)])  4.14 us
  transfers between devices with their start and end apart: 10, of which 8 were waited for; matrix products, arithmetic and copies ran while one was open for 0% of the time, Pallas kernels for 1%

profile of v5, /device:TPU:0, one launch (start us, length us, event | category | flops | bytes accessed | tf_op | source)
XLA Modules:
  0.0 111.4 jit_solution(13112792947278475825)
XLA Ops:
  0.6 2.1 %first.1 = (bf16[16,256]{1,0:T(8,128)(2,1)S(1)}, f32[16,128]{1,0:T(8,128)S(1)}, f32[16,128]{1,0:T(8,128)S(1)}, s32[16,128]{1,0:T(8,128)S(1)}, bf16[8,16,640]{2,1...) custom-call(bf16[16,2048]{1,0:T(8,128)(2,1)} %refs_0_.1, ...), custom_call_target="tpu_custom_call" | custom-call | tf_op jit(solution)/shard_map/first/pallas_call | solution.py:233
  2.7 13.9 %all_to_all.45.got_ref = bf16[8,16,640]{2,1,0:T(8,128)(2,1)S(1)} all-to-all(bf16[8,16,640]{2,1,0:T(8,128)(2,1)S(1)} %get-tuple-element.25), channel_id=1, replica_groups={{0,4,12,8,24,28,20,16},{13,9,25,29,21,17,1,5},{2,6,14,10,26,30,22,18},{..., dimensions={0} | all-to-all | bytes 327680 | tf_op jit(solution)/shard_map/all_to_all | solution.py:615
  16.6 0.9 attend.2
  17.5 9.4 %all_to_all.46.got_ref.refs_0_ = bf16[8,16,640]{2,1,0:T(8,128)(2,1)S(1)} all-to-all(bf16[8,16,640]{2,1,0:T(8,128)(2,1)S(1)} %attend.2), channel_id=1, replica_groups={{0,4,12,8,24,28,20,16},{13,9,25,29,21,17,1,5},{2,6,14,10,26,30,22,18},{..., dimensions={0} | all-to-all | bytes 327680 | tf_op jit(solution)/shard_map/all_to_all | solution.py:615
  26.9 0.5 combine.2.refs_1_
  27.4 0.0 collective-permute-start.2
  27.4 1.6 %collective-permute-start.1 = (f32[16,256]{1,0:T(8,128)S(1)}, f32[16,256]{1,0:T(8,128)S(1)}, u32[]{:S(2)}, u32[]{:S(2)}) collective-permute-start(f32[16,256]{1,0:T(8,128)S(1)} %combine.2.refs_1_), channel_id=1, source_target_pairs={{0,2},{1,3},{2,0},{3,1},{4,6},{5,7},{6,4},{7,5},{8,10},{9,11},{10,... | collective-permute-start | bytes 49160 | tf_op jit(solution)/shard_map/ppermute | solution.py:619
  29.0 0.2 collective-permute-start
  29.2 0.0 collective-permute-done.2.refs_4_
  29.2 2.0 %collective-permute-done.1.refs_3_ = f32[16,256]{1,0:T(8,128)S(1)} collective-permute-done((f32[16,256]{1,0:T(8,128)S(1)}, f32[16,256]{1,0:T(8,128)S(1)}, u32[]{:S(2)}, u32[]{:S(2)}) %collective-permute-start.1) | collective-permute-done | bytes 16416 | tf_op jit(solution)/shard_map/ppermute | solution.py:619
  31.2 0.9 collective-permute-done.refs_2_
  32.2 0.4 widen.2
  32.6 9.5 %all_to_all.47.got_ref = bf16[8,16,640]{2,1,0:T(8,128)(2,1)S(1)} all-to-all(bf16[8,16,640]{2,1,0:T(8,128)(2,1)S(1)} %get-tuple-element.35), channel_id=1, replica_groups={{0,4,12,8,24,28,20,16},{13,9,25,29,21,17,1,5},{2,6,14,10,26,30,22,18},{..., dimensions={0} | all-to-all | bytes 327680 | tf_op jit(solution)/shard_map/all_to_all | solution.py:615
  42.1 0.2 silu.2
  42.3 9.1 %all_to_all.48.got_ref = bf16[8,16,256]{2,1,0:T(8,128)(2,1)S(1)} all-to-all(bf16[8,16,256]{2,1,0:T(8,128)(2,1)S(1)} %silu.2), channel_id=1, replica_groups={{0,4,12,8,24,28,20,16},{13,9,25,29,21,17,1,5},{2,6,14,10,26,30,22,18},{..., dimensions={0} | all-to-all | bytes 131072 | tf_op jit(solution)/shard_map/all_to_all | solution.py:615
  51.4 0.0 copy-done.2
  51.4 0.2 down.1.refs_1_
  51.6 0.0 collective-permute-start.5
  51.6 0.9 collective-permute-start.4
  52.6 0.2 collective-permute-start.3
  52.8 0.3 collective-permute-done.5.refs_4_
  53.1 2.3 %collective-permute-done.4.refs_3_ = f32[16,256]{1,0:T(8,128)S(1)} collective-permute-done((f32[16,256]{1,0:T(8,128)S(1)}, f32[16,256]{1,0:T(8,128)S(1)}, u32[]{:S(2)}, u32[]{:S(2)}) %collective-permute-start.4) | collective-permute-done | bytes 16416 | tf_op jit(solution)/shard_map/ppermute | solution.py:619
  55.4 0.3 collective-permute-done.3.refs_2_
  55.8 0.0 copy-start.1
  55.8 0.2 next.1
  56.0 0.0 copy-start
  56.0 9.5 %all_to_all.49.got_ref = bf16[8,16,640]{2,1,0:T(8,128)(2,1)S(1)} all-to-all(bf16[8,16,640]{2,1,0:T(8,128)(2,1)S(1)} %get-tuple-element.37), channel_id=1, replica_groups={{0,4,12,8,24,28,20,16},{13,9,25,29,21,17,1,5},{2,6,14,10,26,30,22,18},{..., dimensions={0} | all-to-all | bytes 327680 | tf_op jit(solution)/shard_map/all_to_all | solution.py:615
  65.5 0.9 attend.3
  66.4 9.6 %all_to_all.50.got_ref.refs_1_ = bf16[8,16,640]{2,1,0:T(8,128)(2,1)S(1)} all-to-all(bf16[8,16,640]{2,1,0:T(8,128)(2,1)S(1)} %attend.3), channel_id=1, replica_groups={{0,4,12,8,24,28,20,16},{13,9,25,29,21,17,1,5},{2,6,14,10,26,30,22,18},{..., dimensions={0} | all-to-all | bytes 327680 | tf_op jit(solution)/shard_map/all_to_all | solution.py:615
  76.0 0.0 copy-done.6
  76.0 0.5 combine.3.part_ref.refs_1_
  76.5 0.0 collective-permute-start.8
  76.5 1.0 collective-permute-start.7
  77.5 0.2 collective-permute-start.6
  77.7 1.4 %store.1 = (bf16[2,16,64,128]{3,2,1,0:T(8,128)(2,1)}, bf16[2,16,64,128]{3,2,1,0:T(8,128)(2,1)}, f32[8,128]{1,0:T(8,128)S(1)}) custom-call(f32[16,256]{1,0:T(8,128)S(1)} %combine.3.part_ref.refs_1_, s32[16,128]{1,0:T(8,128)S(1)} %get-tuple-element.28.length_ref, bf16[2,16,64,128]{3,2,1,0:T(8,128)(2,1)S(1)} %copy-done.3, ...), custom_call_target="tpu_custom_call" | custom-call | tf_op jit(solution)/shard_map/store/pallas_call | solution.py:233
  79.1 0.0 collective-permute-done.8.refs_4_
  79.1 1.2 %collective-permute-done.7.refs_3_ = f32[16,256]{1,0:T(8,128)S(1)} collective-permute-done((f32[16,256]{1,0:T(8,128)S(1)}, f32[16,256]{1,0:T(8,128)S(1)}, u32[]{:S(2)}, u32[]{:S(2)}) %collective-permute-start.7) | collective-permute-done | bytes 16416 | tf_op jit(solution)/shard_map/ppermute | solution.py:619
  80.3 0.3 collective-permute-done.6.refs_2_
  80.7 0.0 copy-done.1
  80.7 0.4 widen.3
  81.1 9.4 %all_to_all.51.got_ref = bf16[8,16,640]{2,1,0:T(8,128)(2,1)S(1)} all-to-all(bf16[8,16,640]{2,1,0:T(8,128)(2,1)S(1)} %get-tuple-element.40), channel_id=1, replica_groups={{0,4,12,8,24,28,20,16},{13,9,25,29,21,17,1,5},{2,6,14,10,26,30,22,18},{..., dimensions={0} | all-to-all | bytes 327680 | tf_op jit(solution)/shard_map/all_to_all | solution.py:615
  90.5 0.2 silu.3
  90.6 9.3 %all_to_all.52.got_ref = bf16[8,16,256]{2,1,0:T(8,128)(2,1)S(1)} all-to-all(bf16[8,16,256]{2,1,0:T(8,128)(2,1)S(1)} %silu.3), channel_id=1, replica_groups={{0,4,12,8,24,28,20,16},{13,9,25,29,21,17,1,5},{2,6,14,10,26,30,22,18},{..., dimensions={0} | all-to-all | bytes 131072 | tf_op jit(solution)/shard_map/all_to_all | solution.py:615
  100.0 0.2 down_last.1
  100.2 0.0 collective-permute-start.9
  100.2 1.2 %collective-permute-done.9.got_ref = f32[16,128]{1,0:T(8,128)S(1)} collective-permute-done((f32[16,128]{1,0:T(8,128)S(1)}, f32[16,128]{1,0:T(8,128)S(1)}, u32[]{:S(2)}, u32[]{:S(2)}) %collective-permute-start.9) | collective-permute-done | bytes 8224 | tf_op jit(solution)/shard_map/ppermute | solution.py:759
  101.4 9.4 %all_to_all.53.got_ref = bf16[32,16,128]{2,1,0:T(8,128)(2,1)S(1)} all-to-all(bf16[32,16,128]{2,1,0:T(8,128)(2,1)S(1)} %meet.1), channel_id=1, replica_groups={{0,1,3,2,4,5,7,6,12,13,15,14,8,9,11,10,24,25,27,26,28,29,31,30,20,21,23..., dimensions={0} | all-to-all | bytes 262144 | tf_op jit(solution)/shard_map/all_to_all | solution.py:769
  110.8 0.6 last.1
  (14 shorter events, 0.0 us)
Async XLA Ops:
  16.6 34.8 %copy-start.2 = (bf16[2,2048,256]{2,1,0:T(8,128)(2,1)S(1)}, bf16[2,2048,256]{2,1,0:T(8,128)(2,1)}, u32[]{:S(2)}) copy-start(bf16[2,2048,256]{2,1,0:T(8,128)(2,1)} %w_ref.5) | copy-start | bytes 6291460
  27.4 1.8 %collective-permute-start.2 = (f32[16,256]{1,0:T(8,128)S(1)}, f32[16,256]{1,0:T(8,128)S(1)}, u32[]{:S(2)}, u32[]{:S(2)}) collective-permute-start(f32[16,256]{1,0:T(8,128)S(1)} %combine.2.refs_1_), channel_id=1, source_target_pairs={{0,3},{1,0},{2,1},{3,2},{4,7},{5,4},{6,5},{7,6},{8,11},{9,8},{10,9... | collective-permute-start | bytes 49160 | tf_op jit(solution)/shard_map/ppermute | solution.py:619
  27.4 3.8 %collective-permute-start.1 = (f32[16,256]{1,0:T(8,128)S(1)}, f32[16,256]{1,0:T(8,128)S(1)}, u32[]{:S(2)}, u32[]{:S(2)}) collective-permute-start(f32[16,256]{1,0:T(8,128)S(1)} %combine.2.refs_1_), channel_id=1, source_target_pairs={{0,2},{1,3},{2,0},{3,1},{4,6},{5,7},{6,4},{7,5},{8,10},{9,11},{10,... | collective-permute-start | bytes 49160 | tf_op jit(solution)/shard_map/ppermute | solution.py:619
  29.0 3.2 %collective-permute-start = (f32[16,256]{1,0:T(8,128)S(1)}, f32[16,256]{1,0:T(8,128)S(1)}, u32[]{:S(2)}, u32[]{:S(2)}) collective-permute-start(f32[16,256]{1,0:T(8,128)S(1)} %combine.2.refs_1_), channel_id=1, source_target_pairs={{0,1},{1,2},{2,3},{3,0},{4,5},{5,6},{6,7},{7,4},{8,9},{9,10},{10,1... | collective-permute-start | bytes 49160 | tf_op jit(solution)/shard_map/ppermute | solution.py:619
  32.2 23.6 %copy-start.5 = (bf16[2,256,512]{2,1,0:T(8,128)(2,1)S(1)}, bf16[2,256,512]{2,1,0:T(8,128)(2,1)}, u32[]{:S(2)}) copy-start(bf16[2,256,512]{2,1,0:T(8,128)(2,1)} %refs_5_.4) | copy-start | bytes 1572868
  32.2 23.6 %copy-start.7 = (bf16[2,256,128]{2,1,0:T(8,128)(2,1)S(1)}, bf16[2,256,128]{2,1,0:T(8,128)(2,1)}, u32[]{:S(2)}) copy-start(bf16[2,256,128]{2,1,0:T(8,128)(2,1)} %refs_6_.4) | copy-start | bytes 393220
  32.2 23.6 %copy-start.8 = (bf16[2,256,128]{2,1,0:T(8,128)(2,1)S(1)}, bf16[2,256,128]{2,1,0:T(8,128)(2,1)}, u32[]{:S(2)}) copy-start(bf16[2,256,128]{2,1,0:T(8,128)(2,1)} %refs_7_.3) | copy-start | bytes 393220
  32.6 32.9 %copy-start.3 = (bf16[2,16,64,128]{3,2,1,0:T(8,128)(2,1)S(1)}, bf16[2,16,64,128]{3,2,1,0:T(8,128)(2,1)}, u32[]{:S(2)}) copy-start(bf16[2,16,64,128]{3,2,1,0:T(8,128)(2,1)} %key_ref.3) | copy-start | bytes 1572868
  32.6 32.9 %copy-start.4 = (bf16[2,16,64,128]{3,2,1,0:T(8,128)(2,1)S(1)}, bf16[2,16,64,128]{3,2,1,0:T(8,128)(2,1)}, u32[]{:S(2)}) copy-start(bf16[2,16,64,128]{3,2,1,0:T(8,128)(2,1)} %value_ref.3) | copy-start | bytes 1572868
  51.4 24.6 %copy-start.6 = (bf16[2,512,256]{2,1,0:T(8,128)(2,1)S(1)}, bf16[2,512,256]{2,1,0:T(8,128)(2,1)}, u32[]{:S(2)}) copy-start(bf16[2,512,256]{2,1,0:T(8,128)(2,1)} %w_ref.4) | copy-start | bytes 1572868
  51.6 1.5 %collective-permute-start.5 = (f32[16,256]{1,0:T(8,128)S(1)}, f32[16,256]{1,0:T(8,128)S(1)}, u32[]{:S(2)}, u32[]{:S(2)}) collective-permute-start(f32[16,256]{1,0:T(8,128)S(1)} %down.1.refs_1_), channel_id=1, source_target_pairs={{0,3},{1,0},{2,1},{3,2},{4,7},{5,4},{6,5},{7,6},{8,11},{9,8},{10,9... | collective-permute-start | bytes 49160 | tf_op jit(solution)/shard_map/ppermute | solution.py:619
  51.6 3.8 %collective-permute-start.4 = (f32[16,256]{1,0:T(8,128)S(1)}, f32[16,256]{1,0:T(8,128)S(1)}, u32[]{:S(2)}, u32[]{:S(2)}) collective-permute-start(f32[16,256]{1,0:T(8,128)S(1)} %down.1.refs_1_), channel_id=1, source_target_pairs={{0,2},{1,3},{2,0},{3,1},{4,6},{5,7},{6,4},{7,5},{8,10},{9,11},{10,... | collective-permute-start | bytes 49160 | tf_op jit(solution)/shard_map/ppermute | solution.py:619
  52.6 3.2 %collective-permute-start.3 = (f32[16,256]{1,0:T(8,128)S(1)}, f32[16,256]{1,0:T(8,128)S(1)}, u32[]{:S(2)}, u32[]{:S(2)}) collective-permute-start(f32[16,256]{1,0:T(8,128)S(1)} %down.1.refs_1_), channel_id=1, source_target_pairs={{0,1},{1,2},{2,3},{3,0},{4,5},{5,6},{6,7},{7,4},{8,9},{9,10},{10,1... | collective-permute-start | bytes 49160 | tf_op jit(solution)/shard_map/ppermute | solution.py:619
  55.8 24.9 %copy-start.1 = (bf16[2,256,2048]{2,1,0:T(8,128)(2,1)S(1)}, bf16[2,256,2048]{2,1,0:T(8,128)(2,1)}, u32[]{:S(2)}) copy-start(bf16[2,256,2048]{2,1,0:T(8,128)(2,1)} %refs_6_.5) | copy-start | bytes 6291460
  56.0 24.7 %copy-start = (bf16[2,256,2048]{2,1,0:T(8,128)(2,1)S(1)}, bf16[2,256,2048]{2,1,0:T(8,128)(2,1)}, u32[]{:S(2)}) copy-start(bf16[2,256,2048]{2,1,0:T(8,128)(2,1)} %refs_5_.5) | copy-start | bytes 6291460
  76.5 2.6 %collective-permute-start.8 = (f32[16,256]{1,0:T(8,128)S(1)}, f32[16,256]{1,0:T(8,128)S(1)}, u32[]{:S(2)}, u32[]{:S(2)}) collective-permute-start(f32[16,256]{1,0:T(8,128)S(1)} %combine.3.part_ref.refs_1_), channel_id=1, source_target_pairs={{0,3},{1,0},{2,1},{3,2},{4,7},{5,4},{6,5},{7,6},{8,11},{9,8},{10,9... | collective-permute-start | bytes 49160 | tf_op jit(solution)/shard_map/ppermute | solution.py:619
  76.5 3.8 %collective-permute-start.7 = (f32[16,256]{1,0:T(8,128)S(1)}, f32[16,256]{1,0:T(8,128)S(1)}, u32[]{:S(2)}, u32[]{:S(2)}) collective-permute-start(f32[16,256]{1,0:T(8,128)S(1)} %combine.3.part_ref.refs_1_), channel_id=1, source_target_pairs={{0,2},{1,3},{2,0},{3,1},{4,6},{5,7},{6,4},{7,5},{8,10},{9,11},{10,... | collective-permute-start | bytes 49160 | tf_op jit(solution)/shard_map/ppermute | solution.py:619
  77.5 3.2 %collective-permute-start.6 = (f32[16,256]{1,0:T(8,128)S(1)}, f32[16,256]{1,0:T(8,128)S(1)}, u32[]{:S(2)}, u32[]{:S(2)}) collective-permute-start(f32[16,256]{1,0:T(8,128)S(1)} %combine.3.part_ref.refs_1_), channel_id=1, source_target_pairs={{0,1},{1,2},{2,3},{3,0},{4,5},{5,6},{6,7},{7,4},{8,9},{9,10},{10,1... | collective-permute-start | bytes 49160 | tf_op jit(solution)/shard_map/ppermute | solution.py:619
  100.2 1.2 %collective-permute-start.9 = (f32[16,128]{1,0:T(8,128)S(1)}, f32[16,128]{1,0:T(8,128)S(1)}, u32[]{:S(2)}, u32[]{:S(2)}) collective-permute-start(f32[16,128]{1,0:T(8,128)S(1)} %get-tuple-element.42), channel_id=1, source_target_pairs={{0,1},{1,0},{2,3},{3,2},{4,5},{5,4},{6,7},{7,6},{8,9},{9,8},{10,11... | collective-permute-start | bytes 24584 | tf_op jit(solution)/shard_map/ppermute | solution.py:759

commit v6 on v5

--- a/solution.py
+++ b/solution.py
@@ -322,6 +322,18 @@
         copy.wait()
 
 
+def load_kernel(n_more, *refs):
+    more, more_here, sems = refs[1 : 1 + n_more], refs[1 + n_more : 1 + 2 * n_more], refs[-1]
+    copies = [
+        pltpu.make_async_copy(ref.at[0], here.at[0], sems.at[i])
+        for i, (ref, here) in enumerate(zip(more, more_here))
+    ]
+    for copy in copies:
+        copy.start()
+    for copy in copies:
+        copy.wait()
+
+
 def store_kernel(part_ref, length_ref, key_ref, value_ref, *refs):
     layers, requests, block, _ = key_ref.shape
     sent_refs = refs[:layers]
@@ -653,7 +665,8 @@
         sent = []
         packed_weights = (query_weight, key_weight, value_weight)
         table_shape = (requests, LANES)
-        stored = (key_cache, value_cache, out_weight, gate_weight, up_weight)
+        stored = (key_cache, value_cache, out_weight)
+        wide = (gate_weight, up_weight)
         own, cosine, sine, length_table, packed, *early = call(
             functools.partial(first_kernel, len(stored)),
             (
@@ -687,7 +700,7 @@
                     *packed_weights,
                     name="next",
                 )
-            keys, values, out_here, gate_here, up_here = early if layer == 0 else stored
+            keys, values, out_here = early if layer == 0 else stored
             packed = call(
                 functools.partial(attend_kernel, layer, width, heads, kv_heads),
                 packed_shape,
@@ -708,6 +721,17 @@
                 name="combine",
             )
             parts = tp_parts(part)
+            gate_here, up_here = wide
+            if layer == 0:
+                gate_here, up_here = call(
+                    functools.partial(load_kernel, len(wide)),
+                    tuple(shape((1,) + a.shape[1:], bf16) for a in wide),
+                    part,
+                    *wide,
+                    name="load",
+                    held=1,
+                    scratch=[pltpu.SemaphoreType.DMA((len(wide),))],
+                )
             tokens = []
             if layer + 1 == LAYERS:
                 cache_shape = jax.ShapeDtypeStruct(key_cache.shape, bf16)

time: 112 us -> 111 us (level)
  waiting for transfers between devices: 8.66 us -> 7.08 us
    ppermute x9, waiting for transfers between devices: 7.48 us -> 5.9 us  [tp_parts(): lax.ppermute(part, 'tp', [(i, (i + k) % n_tp) for i in range(n_tp)])]
    pallas_call x15 -> x16, Pallas kernels: 8.61 us -> 9.47 us  [call(): pl.pallas_call(body, out_shape=out_shape, in_specs=[vmem if i < held else...]
  transfers between devices with their start and end apart: 10 -> 10, of which waited for: 8 -> 8; matrix products, arithmetic and copies ran while one was open for 0% -> 0% of each run, Pallas kernels for 1% -> 3%
where the time goes in v6:
time: 111 us
  blocking collectives  89.3 us (80%)
  Pallas kernels  9.47 us (9%)
  waiting for transfers between devices  7.08 us (6%)
  starting transfers between devices  4.26 us (4%)
    all_to_all x8, blocking collectives, swap(): return lax.all_to_all(chunks, ('seq', 'tp'), 0, 0, axis_index_groups=groups)  79.9 us
    pallas_call x16, Pallas kernels, call(): pl.pallas_call(body, out_shape=out_shape, in_specs=[vmem if i < held else...  9.47 us
    all_to_all x1, blocking collectives, per_device(): lax.all_to_all(stream, ('seq', 'tp'), 0, 0, axis_index_groups=everyone)  9.36 us
    ppermute x9, waiting for transfers between devices, tp_parts(): lax.ppermute(part, 'tp', [(i, (i + k) % n_tp) for i in range(n_tp)])  5.9 us
    ppermute x9, starting transfers between devices, tp_parts(): lax.ppermute(part, 'tp', [(i, (i + k) % n_tp) for i in range(n_tp)])  4.25 us
  transfers between devices with their start and end apart: 10, of which 8 were waited for; matrix products, arithmetic and copies ran while one was open for 0% of the time, Pallas kernels for 3%

profile of v6, /device:TPU:0, one launch (start us, length us, event | category | flops | bytes accessed | tf_op | source)
XLA Modules:
  0.0 110.9 jit_solution(14562026846114148986)
XLA Ops:
  0.6 1.4 %first.1 = (bf16[16,256]{1,0:T(8,128)(2,1)S(1)}, f32[16,128]{1,0:T(8,128)S(1)}, f32[16,128]{1,0:T(8,128)S(1)}, s32[16,128]{1,0:T(8,128)S(1)}, bf16[8,16,640]{2,1...) custom-call(bf16[16,2048]{1,0:T(8,128)(2,1)} %refs_0_.1, ...), custom_call_target="tpu_custom_call" | custom-call | tf_op jit(solution)/shard_map/first/pallas_call | solution.py:233
  2.0 13.9 %all_to_all.45.got_ref = bf16[8,16,640]{2,1,0:T(8,128)(2,1)S(1)} all-to-all(bf16[8,16,640]{2,1,0:T(8,128)(2,1)S(1)} %get-tuple-element.25), channel_id=1, replica_groups={{0,4,12,8,24,28,20,16},{13,9,25,29,21,17,1,5},{2,6,14,10,26,30,22,18},{..., dimensions={0} | all-to-all | bytes 327680 | tf_op jit(solution)/shard_map/all_to_all | solution.py:627
  15.9 0.9 attend.2
  16.8 9.4 %all_to_all.46.got_ref.refs_0_ = bf16[8,16,640]{2,1,0:T(8,128)(2,1)S(1)} all-to-all(bf16[8,16,640]{2,1,0:T(8,128)(2,1)S(1)} %attend.2), channel_id=1, replica_groups={{0,4,12,8,24,28,20,16},{13,9,25,29,21,17,1,5},{2,6,14,10,26,30,22,18},{..., dimensions={0} | all-to-all | bytes 327680 | tf_op jit(solution)/shard_map/all_to_all | solution.py:627
  26.2 0.5 combine.2.refs_0_.refs_1_
  26.7 0.0 collective-permute-start.2
  26.7 1.6 %collective-permute-start.1 = (f32[16,256]{1,0:T(8,128)S(1)}, f32[16,256]{1,0:T(8,128)S(1)}, u32[]{:S(2)}, u32[]{:S(2)}) collective-permute-start(f32[16,256]{1,0:T(8,128)S(1)} %combine.2.refs_0_.refs_1_), channel_id=1, source_target_pairs={{0,2},{1,3},{2,0},{3,1},{4,6},{5,7},{6,4},{7,5},{8,10},{9,11},{10,... | collective-permute-start | bytes 49160 | tf_op jit(solution)/shard_map/ppermute | solution.py:631
  28.3 0.2 collective-permute-start
  28.5 1.6 %load.1 = (bf16[1,256,2048]{2,1,0:T(8,128)(2,1)S(1)}, bf16[1,256,2048]{2,1,0:T(8,128)(2,1)S(1)}) custom-call(f32[16,256]{1,0:T(8,128)S(1)} %combine.2.refs_0_.refs_1_, bf16[2,256,2048]{2,1,0:T(8,128)(2,1)} %refs_5_.5, bf16[2,256,2048]{2,1,0:T(8,128)(2,1)} %refs_6_.5), custom_call_target="tpu_custom_call" | custom-call | tf_op jit(solution)/shard_map/load/pallas_call | solution.py:233
  30.1 0.0 copy-start.2
  30.1 0.0 collective-permute-done.2.refs_4_
  30.1 0.4 collective-permute-done.1.refs_3_
  30.5 0.9 collective-permute-done.refs_2_
  31.5 0.4 widen.2
  31.9 9.5 %all_to_all.47.got_ref = bf16[8,16,640]{2,1,0:T(8,128)(2,1)S(1)} all-to-all(bf16[8,16,640]{2,1,0:T(8,128)(2,1)S(1)} %get-tuple-element.35), channel_id=1, replica_groups={{0,4,12,8,24,28,20,16},{13,9,25,29,21,17,1,5},{2,6,14,10,26,30,22,18},{..., dimensions={0} | all-to-all | bytes 327680 | tf_op jit(solution)/shard_map/all_to_all | solution.py:627
  41.4 0.2 silu.2
  41.6 9.2 %all_to_all.48.got_ref = bf16[8,16,256]{2,1,0:T(8,128)(2,1)S(1)} all-to-all(bf16[8,16,256]{2,1,0:T(8,128)(2,1)S(1)} %silu.2), channel_id=1, replica_groups={{0,4,12,8,24,28,20,16},{13,9,25,29,21,17,1,5},{2,6,14,10,26,30,22,18},{..., dimensions={0} | all-to-all | bytes 131072 | tf_op jit(solution)/shard_map/all_to_all | solution.py:627
  50.8 0.2 down.1.refs_1_
  51.1 0.0 collective-permute-start.5
  51.1 0.8 collective-permute-start.4
  51.9 0.2 collective-permute-start.3
  52.1 0.5 collective-permute-done.5.refs_4_
  52.5 2.3 %collective-permute-done.4.refs_3_ = f32[16,256]{1,0:T(8,128)S(1)} collective-permute-done((f32[16,256]{1,0:T(8,128)S(1)}, f32[16,256]{1,0:T(8,128)S(1)}, u32[]{:S(2)}, u32[]{:S(2)}) %collective-permute-start.4) | collective-permute-done | bytes 16416 | tf_op jit(solution)/shard_map/ppermute | solution.py:631
  54.9 0.2 collective-permute-done.3.refs_2_
  55.0 0.0 copy-done.7
  55.0 0.0 copy-start.1
  55.1 0.2 next.1
  55.2 0.0 copy-start
  55.3 9.5 %all_to_all.49.got_ref = bf16[8,16,640]{2,1,0:T(8,128)(2,1)S(1)} all-to-all(bf16[8,16,640]{2,1,0:T(8,128)(2,1)S(1)} %get-tuple-element.37), channel_id=1, replica_groups={{0,4,12,8,24,28,20,16},{13,9,25,29,21,17,1,5},{2,6,14,10,26,30,22,18},{..., dimensions={0} | all-to-all | bytes 327680 | tf_op jit(solution)/shard_map/all_to_all | solution.py:627
  64.8 0.9 attend.3
  65.7 9.5 %all_to_all.50.got_ref.refs_1_ = bf16[8,16,640]{2,1,0:T(8,128)(2,1)S(1)} all-to-all(bf16[8,16,640]{2,1,0:T(8,128)(2,1)S(1)} %attend.3), channel_id=1, replica_groups={{0,4,12,8,24,28,20,16},{13,9,25,29,21,17,1,5},{2,6,14,10,26,30,22,18},{..., dimensions={0} | all-to-all | bytes 327680 | tf_op jit(solution)/shard_map/all_to_all | solution.py:627
  75.2 0.5 combine.3.part_ref.refs_1_
  75.7 0.0 collective-permute-start.8
  75.7 1.3 %collective-permute-start.7 = (f32[16,256]{1,0:T(8,128)S(1)}, f32[16,256]{1,0:T(8,128)S(1)}, u32[]{:S(2)}, u32[]{:S(2)}) collective-permute-start(f32[16,256]{1,0:T(8,128)S(1)} %combine.3.part_ref.refs_1_), channel_id=1, source_target_pairs={{0,2},{1,3},{2,0},{3,1},{4,6},{5,7},{6,4},{7,5},{8,10},{9,11},{10,... | collective-permute-start | bytes 49160 | tf_op jit(solution)/shard_map/ppermute | solution.py:631
  76.9 0.2 collective-permute-start.6
  77.1 1.4 %store.1 = (bf16[2,16,64,128]{3,2,1,0:T(8,128)(2,1)}, bf16[2,16,64,128]{3,2,1,0:T(8,128)(2,1)}, f32[8,128]{1,0:T(8,128)S(1)}) custom-call(f32[16,256]{1,0:T(8,128)S(1)} %combine.3.part_ref.refs_1_, s32[16,128]{1,0:T(8,128)S(1)} %get-tuple-element.28.length_ref, bf16[2,16,64,128]{3,2,1,0:T(8,128)(2,1)S(1)} %copy-done.3, ...), custom_call_target="tpu_custom_call" | custom-call | tf_op jit(solution)/shard_map/store/pallas_call | solution.py:233
  78.5 0.0 collective-permute-done.8.refs_4_
  78.5 0.9 collective-permute-done.7.refs_3_
  79.5 0.6 collective-permute-done.6.refs_2_
  80.1 0.4 widen.3
  80.5 9.4 %all_to_all.51.got_ref = bf16[8,16,640]{2,1,0:T(8,128)(2,1)S(1)} all-to-all(bf16[8,16,640]{2,1,0:T(8,128)(2,1)S(1)} %get-tuple-element.40), channel_id=1, replica_groups={{0,4,12,8,24,28,20,16},{13,9,25,29,21,17,1,5},{2,6,14,10,26,30,22,18},{..., dimensions={0} | all-to-all | bytes 327680 | tf_op jit(solution)/shard_map/all_to_all | solution.py:627
  89.9 0.2 silu.3
  90.1 9.3 %all_to_all.52.got_ref = bf16[8,16,256]{2,1,0:T(8,128)(2,1)S(1)} all-to-all(bf16[8,16,256]{2,1,0:T(8,128)(2,1)S(1)} %silu.3), channel_id=1, replica_groups={{0,4,12,8,24,28,20,16},{13,9,25,29,21,17,1,5},{2,6,14,10,26,30,22,18},{..., dimensions={0} | all-to-all | bytes 131072 | tf_op jit(solution)/shard_map/all_to_all | solution.py:627
  99.4 0.2 down_last.1
  99.6 0.0 collective-permute-start.9
  99.7 1.2 %collective-permute-done.9.got_ref = f32[16,128]{1,0:T(8,128)S(1)} collective-permute-done((f32[16,128]{1,0:T(8,128)S(1)}, f32[16,128]{1,0:T(8,128)S(1)}, u32[]{:S(2)}, u32[]{:S(2)}) %collective-permute-start.9) | collective-permute-done | bytes 8224 | tf_op jit(solution)/shard_map/ppermute | solution.py:783
  100.8 9.4 %all_to_all.53.got_ref = bf16[32,16,128]{2,1,0:T(8,128)(2,1)S(1)} all-to-all(bf16[32,16,128]{2,1,0:T(8,128)(2,1)S(1)} %meet.1), channel_id=1, replica_groups={{0,1,3,2,4,5,7,6,12,13,15,14,8,9,11,10,24,25,27,26,28,29,31,30,20,21,23..., dimensions={0} | all-to-all | bytes 262144 | tf_op jit(solution)/shard_map/all_to_all | solution.py:793
  110.2 0.6 last.1
  (15 shorter events, 0.0 us)
Async XLA Ops:
  26.7 3.4 %collective-permute-start.2 = (f32[16,256]{1,0:T(8,128)S(1)}, f32[16,256]{1,0:T(8,128)S(1)}, u32[]{:S(2)}, u32[]{:S(2)}) collective-permute-start(f32[16,256]{1,0:T(8,128)S(1)} %combine.2.refs_0_.refs_1_), channel_id=1, source_target_pairs={{0,3},{1,0},{2,1},{3,2},{4,7},{5,4},{6,5},{7,6},{8,11},{9,8},{10,9... | collective-permute-start | bytes 49160 | tf_op jit(solution)/shard_map/ppermute | solution.py:631
  26.7 3.8 %collective-permute-start.1 = (f32[16,256]{1,0:T(8,128)S(1)}, f32[16,256]{1,0:T(8,128)S(1)}, u32[]{:S(2)}, u32[]{:S(2)}) collective-permute-start(f32[16,256]{1,0:T(8,128)S(1)} %combine.2.refs_0_.refs_1_), channel_id=1, source_target_pairs={{0,2},{1,3},{2,0},{3,1},{4,6},{5,7},{6,4},{7,5},{8,10},{9,11},{10,... | collective-permute-start | bytes 49160 | tf_op jit(solution)/shard_map/ppermute | solution.py:631
  28.3 3.2 %collective-permute-start = (f32[16,256]{1,0:T(8,128)S(1)}, f32[16,256]{1,0:T(8,128)S(1)}, u32[]{:S(2)}, u32[]{:S(2)}) collective-permute-start(f32[16,256]{1,0:T(8,128)S(1)} %combine.2.refs_0_.refs_1_), channel_id=1, source_target_pairs={{0,1},{1,2},{2,3},{3,0},{4,5},{5,6},{6,7},{7,4},{8,9},{9,10},{10,1... | collective-permute-start | bytes 49160 | tf_op jit(solution)/shard_map/ppermute | solution.py:631
  30.1 20.8 %copy-start.2 = (bf16[2,2048,256]{2,1,0:T(8,128)(2,1)S(1)}, bf16[2,2048,256]{2,1,0:T(8,128)(2,1)}, u32[]{:S(2)}) copy-start(bf16[2,2048,256]{2,1,0:T(8,128)(2,1)} %w_ref.5) | copy-start | bytes 6291460
  31.5 23.6 %copy-start.5 = (bf16[2,256,512]{2,1,0:T(8,128)(2,1)S(1)}, bf16[2,256,512]{2,1,0:T(8,128)(2,1)}, u32[]{:S(2)}) copy-start(bf16[2,256,512]{2,1,0:T(8,128)(2,1)} %refs_5_.4) | copy-start | bytes 1572868
  31.5 23.6 %copy-start.7 = (bf16[2,256,128]{2,1,0:T(8,128)(2,1)S(1)}, bf16[2,256,128]{2,1,0:T(8,128)(2,1)}, u32[]{:S(2)}) copy-start(bf16[2,256,128]{2,1,0:T(8,128)(2,1)} %refs_6_.4) | copy-start | bytes 393220
  31.5 23.6 %copy-start.8 = (bf16[2,256,128]{2,1,0:T(8,128)(2,1)S(1)}, bf16[2,256,128]{2,1,0:T(8,128)(2,1)}, u32[]{:S(2)}) copy-start(bf16[2,256,128]{2,1,0:T(8,128)(2,1)} %refs_7_.3) | copy-start | bytes 393220
  31.9 32.9 %copy-start.3 = (bf16[2,16,64,128]{3,2,1,0:T(8,128)(2,1)S(1)}, bf16[2,16,64,128]{3,2,1,0:T(8,128)(2,1)}, u32[]{:S(2)}) copy-start(bf16[2,16,64,128]{3,2,1,0:T(8,128)(2,1)} %key_ref.3) | copy-start | bytes 1572868
  31.9 32.9 %copy-start.4 = (bf16[2,16,64,128]{3,2,1,0:T(8,128)(2,1)S(1)}, bf16[2,16,64,128]{3,2,1,0:T(8,128)(2,1)}, u32[]{:S(2)}) copy-start(bf16[2,16,64,128]{3,2,1,0:T(8,128)(2,1)} %value_ref.3) | copy-start | bytes 1572868
  50.8 24.4 %copy-start.6 = (bf16[2,512,256]{2,1,0:T(8,128)(2,1)S(1)}, bf16[2,512,256]{2,1,0:T(8,128)(2,1)}, u32[]{:S(2)}) copy-start(bf16[2,512,256]{2,1,0:T(8,128)(2,1)} %w_ref.4) | copy-start | bytes 1572868
  51.1 1.5 %collective-permute-start.5 = (f32[16,256]{1,0:T(8,128)S(1)}, f32[16,256]{1,0:T(8,128)S(1)}, u32[]{:S(2)}, u32[]{:S(2)}) collective-permute-start(f32[16,256]{1,0:T(8,128)S(1)} %down.1.refs_1_), channel_id=1, source_target_pairs={{0,3},{1,0},{2,1},{3,2},{4,7},{5,4},{6,5},{7,6},{8,11},{9,8},{10,9... | collective-permute-start | bytes 49160 | tf_op jit(solution)/shard_map/ppermute | solution.py:631
  51.1 3.8 %collective-permute-start.4 = (f32[16,256]{1,0:T(8,128)S(1)}, f32[16,256]{1,0:T(8,128)S(1)}, u32[]{:S(2)}, u32[]{:S(2)}) collective-permute-start(f32[16,256]{1,0:T(8,128)S(1)} %down.1.refs_1_), channel_id=1, source_target_pairs={{0,2},{1,3},{2,0},{3,1},{4,6},{5,7},{6,4},{7,5},{8,10},{9,11},{10,... | collective-permute-start | bytes 49160 | tf_op jit(solution)/shard_map/ppermute | solution.py:631
  51.9 3.2 %collective-permute-start.3 = (f32[16,256]{1,0:T(8,128)S(1)}, f32[16,256]{1,0:T(8,128)S(1)}, u32[]{:S(2)}, u32[]{:S(2)}) collective-permute-start(f32[16,256]{1,0:T(8,128)S(1)} %down.1.refs_1_), channel_id=1, source_target_pairs={{0,1},{1,2},{2,3},{3,0},{4,5},{5,6},{6,7},{7,4},{8,9},{9,10},{10,1... | collective-permute-start | bytes 49160 | tf_op jit(solution)/shard_map/ppermute | solution.py:631
  55.0 25.1 %copy-start.1 = (bf16[2,256,2048]{2,1,0:T(8,128)(2,1)S(1)}, bf16[2,256,2048]{2,1,0:T(8,128)(2,1)}, u32[]{:S(2)}) copy-start(bf16[2,256,2048]{2,1,0:T(8,128)(2,1)} %refs_6_.5) | copy-start | bytes 6291460
  55.2 24.9 %copy-start = (bf16[2,256,2048]{2,1,0:T(8,128)(2,1)S(1)}, bf16[2,256,2048]{2,1,0:T(8,128)(2,1)}, u32[]{:S(2)}) copy-start(bf16[2,256,2048]{2,1,0:T(8,128)(2,1)} %refs_5_.5) | copy-start | bytes 6291460
  75.7 2.9 %collective-permute-start.8 = (f32[16,256]{1,0:T(8,128)S(1)}, f32[16,256]{1,0:T(8,128)S(1)}, u32[]{:S(2)}, u32[]{:S(2)}) collective-permute-start(f32[16,256]{1,0:T(8,128)S(1)} %combine.3.part_ref.refs_1_), channel_id=1, source_target_pairs={{0,3},{1,0},{2,1},{3,2},{4,7},{5,4},{6,5},{7,6},{8,11},{9,8},{10,9... | collective-permute-start | bytes 49160 | tf_op jit(solution)/shard_map/ppermute | solution.py:631
  75.7 3.8 %collective-permute-start.7 = (f32[16,256]{1,0:T(8,128)S(1)}, f32[16,256]{1,0:T(8,128)S(1)}, u32[]{:S(2)}, u32[]{:S(2)}) collective-permute-start(f32[16,256]{1,0:T(8,128)S(1)} %combine.3.part_ref.refs_1_), channel_id=1, source_target_pairs={{0,2},{1,3},{2,0},{3,1},{4,6},{5,7},{6,4},{7,5},{8,10},{9,11},{10,... | collective-permute-start | bytes 49160 | tf_op jit(solution)/shard_map/ppermute | solution.py:631
  76.9 3.2 %collective-permute-start.6 = (f32[16,256]{1,0:T(8,128)S(1)}, f32[16,256]{1,0:T(8,128)S(1)}, u32[]{:S(2)}, u32[]{:S(2)}) collective-permute-start(f32[16,256]{1,0:T(8,128)S(1)} %combine.3.part_ref.refs_1_), channel_id=1, source_target_pairs={{0,1},{1,2},{2,3},{3,0},{4,5},{5,6},{6,7},{7,4},{8,9},{9,10},{10,1... | collective-permute-start | bytes 49160 | tf_op jit(solution)/shard_map/ppermute | solution.py:631
  99.6 1.2 %collective-permute-start.9 = (f32[16,128]{1,0:T(8,128)S(1)}, f32[16,128]{1,0:T(8,128)S(1)}, u32[]{:S(2)}, u32[]{:S(2)}) collective-permute-start(f32[16,128]{1,0:T(8,128)S(1)} %get-tuple-element.42), channel_id=1, source_target_pairs={{0,1},{1,0},{2,3},{3,2},{4,5},{5,4},{6,7},{7,6},{8,9},{9,8},{10,11... | collective-permute-start | bytes 24584 | tf_op jit(solution)/shard_map/ppermute | solution.py:783

commit v7 on v6

--- a/solution.py
+++ b/solution.py
@@ -372,9 +372,9 @@
 
 
 def sum_parts(base_ref, part_refs):
-    total = part_refs[0][...]
+    total = part_refs[0][...].astype(jnp.float32)
     for ref in part_refs[1:]:
-        total = total + ref[...]
+        total = total + ref[...].astype(jnp.float32)
     return (base_ref[...].astype(jnp.float32) + total).astype(jnp.bfloat16)
 
 
@@ -568,7 +568,7 @@
             piece = got_ref[m, :, pair * LANES : (pair + 1) * LANES].astype(jnp.float32)
             acc = acc + piece * spread(factors[m], pair)
         attended.append((acc / spread(total, pair)).astype(jnp.bfloat16))
-    out_ref[...] = dot32(jnp.concatenate(attended, axis=1), w_ref[layer])
+    out_ref[...] = dot32(jnp.concatenate(attended, axis=1), w_ref[layer]).astype(jnp.bfloat16)
 
 
 def widen_kernel(layer, n_parts, *refs):
@@ -609,7 +609,7 @@
 
 def down_kernel(layer, got_ref, w_ref, out_ref):
     hidden = in_order(got_ref)
-    out_ref[...] = dot32(hidden, w_ref[layer])
+    out_ref[...] = dot32(hidden, w_ref[layer]).astype(jnp.bfloat16)
 
 
 def down_last_kernel(layer, got_ref, w_ref, keep_ref, give_ref):
@@ -660,7 +660,7 @@
             return pltpu.VMEM(dims, kind)
 
         packed_shape = shape((n_seq, requests, query_width + LANES), bf16)
-        part_shape = shape((requests, col_count), f32)
+        part_shape = shape((requests, col_count), bf16)
         own_shape = shape((requests, col_count), bf16)
         sent = []
         packed_weights = (query_weight, key_weight, value_weight)

time: 111 us -> 111 us (level)
  transfers between devices with their start and end apart: 10 -> 10, of which waited for: 8 -> 7; matrix products, arithmetic and copies ran while one was open for 0% -> 0% of each run, Pallas kernels for 3% -> 3%
where the time goes in v7:
time: 111 us
  blocking collectives  89.3 us (80%)
  Pallas kernels  9.47 us (9%)
  waiting for transfers between devices  6.9 us (6%)
  starting transfers between devices  4.08 us (4%)
    all_to_all x8, blocking collectives, swap(): return lax.all_to_all(chunks, ('seq', 'tp'), 0, 0, axis_index_groups=groups)  79.9 us
    pallas_call x16, Pallas kernels, call(): pl.pallas_call(body, out_shape=out_shape, in_specs=[vmem if i < held else...  9.47 us
    all_to_all x1, blocking collectives, per_device(): lax.all_to_all(stream, ('seq', 'tp'), 0, 0, axis_index_groups=everyone)  9.37 us
    ppermute x9, waiting for transfers between devices, tp_parts(): lax.ppermute(part, 'tp', [(i, (i + k) % n_tp) for i in range(n_tp)])  5.72 us
    ppermute x9, starting transfers between devices, tp_parts(): lax.ppermute(part, 'tp', [(i, (i + k) % n_tp) for i in range(n_tp)])  4.08 us
  transfers between devices with their start and end apart: 10, of which 7 were waited for; matrix products, arithmetic and copies ran while one was open for 0% of the time, Pallas kernels for 3%

profile of v7, /device:TPU:0, one launch (start us, length us, event | category | flops | bytes accessed | tf_op | source)
XLA Modules:
  0.0 110.5 jit_solution(14429875279475026617)
XLA Ops:
  0.6 1.4 %first.1 = (bf16[16,256]{1,0:T(8,128)(2,1)S(1)}, f32[16,128]{1,0:T(8,128)S(1)}, f32[16,128]{1,0:T(8,128)S(1)}, s32[16,128]{1,0:T(8,128)S(1)}, bf16[8,16,640]{2,1...) custom-call(bf16[16,2048]{1,0:T(8,128)(2,1)} %refs_0_.1, ...), custom_call_target="tpu_custom_call" | custom-call | tf_op jit(solution)/shard_map/first/pallas_call | solution.py:233
  2.0 13.9 %all_to_all.45.got_ref = bf16[8,16,640]{2,1,0:T(8,128)(2,1)S(1)} all-to-all(bf16[8,16,640]{2,1,0:T(8,128)(2,1)S(1)} %get-tuple-element.25), channel_id=1, replica_groups={{0,4,12,8,24,28,20,16},{13,9,25,29,21,17,1,5},{2,6,14,10,26,30,22,18},{..., dimensions={0} | all-to-all | bytes 327680 | tf_op jit(solution)/shard_map/all_to_all | solution.py:627
  15.9 0.9 attend.2
  16.8 9.4 %all_to_all.46.got_ref.refs_0_ = bf16[8,16,640]{2,1,0:T(8,128)(2,1)S(1)} all-to-all(bf16[8,16,640]{2,1,0:T(8,128)(2,1)S(1)} %attend.2), channel_id=1, replica_groups={{0,4,12,8,24,28,20,16},{13,9,25,29,21,17,1,5},{2,6,14,10,26,30,22,18},{..., dimensions={0} | all-to-all | bytes 327680 | tf_op jit(solution)/shard_map/all_to_all | solution.py:627
  26.2 0.5 combine.2.refs_0_.refs_1_
  26.7 0.0 collective-permute-start.2
  26.7 1.6 %collective-permute-start.1 = (bf16[16,256]{1,0:T(8,128)(2,1)S(1)}, bf16[16,256]{1,0:T(8,128)(2,1)S(1)}, u32[]{:S(2)}, u32[]{:S(2)}) collective-permute-start(bf16[16,256]{1,0:T(8,128)(2,1)S(1)} %combine.2.refs_0_.refs_1_), channel_id=1, source_target_pairs={{0,2},{1,3},{2,0},{3,1},{4,6},{5,7},{6,4},{7,5},{8,10},{9,11},{10,... | collective-permute-start | bytes 24584 | tf_op jit(solution)/shard_map/ppermute | solution.py:631
  28.3 0.2 collective-permute-start
  28.5 1.6 %load.1 = (bf16[1,256,2048]{2,1,0:T(8,128)(2,1)S(1)}, bf16[1,256,2048]{2,1,0:T(8,128)(2,1)S(1)}) custom-call(bf16[16,256]{1,0:T(8,128)(2,1)S(1)} %combine.2.refs_0_.refs_1_, bf16[2,256,2048]{2,1,0:T(8,128)(2,1)} %refs_5_.5, bf16[2,256,2048]{2,1,0:T(8,128)(2,1)} %refs_6_.5), custom_call_target="tpu_custom_call" | custom-call | tf_op jit(solution)/shard_map/load/pallas_call | solution.py:233
  30.1 0.0 copy-start.2
  30.1 0.0 collective-permute-done.2.refs_4_
  30.1 0.3 collective-permute-done.1.refs_3_
  30.4 0.9 collective-permute-done.refs_2_
  31.4 0.4 widen.2
  31.8 9.6 %all_to_all.47.got_ref = bf16[8,16,640]{2,1,0:T(8,128)(2,1)S(1)} all-to-all(bf16[8,16,640]{2,1,0:T(8,128)(2,1)S(1)} %get-tuple-element.35), channel_id=1, replica_groups={{0,4,12,8,24,28,20,16},{13,9,25,29,21,17,1,5},{2,6,14,10,26,30,22,18},{..., dimensions={0} | all-to-all | bytes 327680 | tf_op jit(solution)/shard_map/all_to_all | solution.py:627
  41.3 0.2 silu.2
  41.5 9.3 %all_to_all.48.got_ref = bf16[8,16,256]{2,1,0:T(8,128)(2,1)S(1)} all-to-all(bf16[8,16,256]{2,1,0:T(8,128)(2,1)S(1)} %silu.2), channel_id=1, replica_groups={{0,4,12,8,24,28,20,16},{13,9,25,29,21,17,1,5},{2,6,14,10,26,30,22,18},{..., dimensions={0} | all-to-all | bytes 131072 | tf_op jit(solution)/shard_map/all_to_all | solution.py:627
  50.8 0.2 down.1.refs_1_
  51.1 0.0 collective-permute-start.5
  51.1 0.6 collective-permute-start.4
  51.7 0.2 collective-permute-start.3
  51.9 0.6 collective-permute-done.5.refs_4_
  52.5 2.4 %collective-permute-done.4.refs_3_ = bf16[16,256]{1,0:T(8,128)(2,1)S(1)} collective-permute-done((bf16[16,256]{1,0:T(8,128)(2,1)S(1)}, bf16[16,256]{1,0:T(8,128)(2,1)S(1)}, u32[]{:S(2)}, u32[]{:S(2)}) %collective-permute-start.4) | collective-permute-done | bytes 8224 | tf_op jit(solution)/shard_map/ppermute | solution.py:631
  54.8 0.0 collective-permute-done.3.refs_2_
  54.8 0.0 copy-done.5
  54.8 0.0 copy-start.1
  54.9 0.2 next.1
  55.0 0.0 copy-start
  55.1 9.5 %all_to_all.49.got_ref = bf16[8,16,640]{2,1,0:T(8,128)(2,1)S(1)} all-to-all(bf16[8,16,640]{2,1,0:T(8,128)(2,1)S(1)} %get-tuple-element.37), channel_id=1, replica_groups={{0,4,12,8,24,28,20,16},{13,9,25,29,21,17,1,5},{2,6,14,10,26,30,22,18},{..., dimensions={0} | all-to-all | bytes 327680 | tf_op jit(solution)/shard_map/all_to_all | solution.py:627
  64.6 0.9 attend.3
  65.5 9.6 %all_to_all.50.got_ref.refs_1_ = bf16[8,16,640]{2,1,0:T(8,128)(2,1)S(1)} all-to-all(bf16[8,16,640]{2,1,0:T(8,128)(2,1)S(1)} %attend.3), channel_id=1, replica_groups={{0,4,12,8,24,28,20,16},{13,9,25,29,21,17,1,5},{2,6,14,10,26,30,22,18},{..., dimensions={0} | all-to-all | bytes 327680 | tf_op jit(solution)/shard_map/all_to_all | solution.py:627
  75.1 0.5 combine.3.part_ref.refs_1_
  75.5 0.0 collective-permute-start.8
  75.6 1.3 %collective-permute-start.7 = (bf16[16,256]{1,0:T(8,128)(2,1)S(1)}, bf16[16,256]{1,0:T(8,128)(2,1)S(1)}, u32[]{:S(2)}, u32[]{:S(2)}) collective-permute-start(bf16[16,256]{1,0:T(8,128)(2,1)S(1)} %combine.3.part_ref.refs_1_), channel_id=1, source_target_pairs={{0,2},{1,3},{2,0},{3,1},{4,6},{5,7},{6,4},{7,5},{8,10},{9,11},{10,... | collective-permute-start | bytes 24584 | tf_op jit(solution)/shard_map/ppermute | solution.py:631
  76.8 0.2 collective-permute-start.6
  77.0 1.4 %store.1 = (bf16[2,16,64,128]{3,2,1,0:T(8,128)(2,1)}, bf16[2,16,64,128]{3,2,1,0:T(8,128)(2,1)}, f32[8,128]{1,0:T(8,128)S(1)}) custom-call(bf16[16,256]{1,0:T(8,128)(2,1)S(1)} %combine.3.part_ref.refs_1_, s32[16,128]{1,0:T(8,128)S(1)} %get-tuple-element.28.length_ref, bf16[2,16,64,128]{3,2,1,0:T(8,128)(2,1)S(1)} %copy-done.3, ...), custom_call_target="tpu_custom_call" | custom-call | tf_op jit(solution)/shard_map/store/pallas_call | solution.py:233
  78.4 0.0 collective-permute-done.8.refs_4_
  78.4 0.8 collective-permute-done.7.refs_3_
  79.3 0.6 collective-permute-done.6.refs_2_
  79.9 0.4 widen.3
  80.3 9.4 %all_to_all.51.got_ref = bf16[8,16,640]{2,1,0:T(8,128)(2,1)S(1)} all-to-all(bf16[8,16,640]{2,1,0:T(8,128)(2,1)S(1)} %get-tuple-element.40), channel_id=1, replica_groups={{0,4,12,8,24,28,20,16},{13,9,25,29,21,17,1,5},{2,6,14,10,26,30,22,18},{..., dimensions={0} | all-to-all | bytes 327680 | tf_op jit(solution)/shard_map/all_to_all | solution.py:627
  89.7 0.2 silu.3
  89.9 9.1 %all_to_all.52.got_ref = bf16[8,16,256]{2,1,0:T(8,128)(2,1)S(1)} all-to-all(bf16[8,16,256]{2,1,0:T(8,128)(2,1)S(1)} %silu.3), channel_id=1, replica_groups={{0,4,12,8,24,28,20,16},{13,9,25,29,21,17,1,5},{2,6,14,10,26,30,22,18},{..., dimensions={0} | all-to-all | bytes 131072 | tf_op jit(solution)/shard_map/all_to_all | solution.py:627
  99.0 0.2 down_last.1
  99.3 0.0 collective-permute-start.9
  99.3 1.2 %collective-permute-done.9.got_ref = f32[16,128]{1,0:T(8,128)S(1)} collective-permute-done((f32[16,128]{1,0:T(8,128)S(1)}, f32[16,128]{1,0:T(8,128)S(1)}, u32[]{:S(2)}, u32[]{:S(2)}) %collective-permute-start.9) | collective-permute-done | bytes 8224 | tf_op jit(solution)/shard_map/ppermute | solution.py:783
  100.5 9.4 %all_to_all.53.got_ref = bf16[32,16,128]{2,1,0:T(8,128)(2,1)S(1)} all-to-all(bf16[32,16,128]{2,1,0:T(8,128)(2,1)S(1)} %meet.1), channel_id=1, replica_groups={{0,1,3,2,4,5,7,6,12,13,15,14,8,9,11,10,24,25,27,26,28,29,31,30,20,21,23..., dimensions={0} | all-to-all | bytes 262144 | tf_op jit(solution)/shard_map/all_to_all | solution.py:793
  109.9 0.6 last.1
  (15 shorter events, 0.0 us)
Async XLA Ops:
  26.7 3.4 %collective-permute-start.2 = (bf16[16,256]{1,0:T(8,128)(2,1)S(1)}, bf16[16,256]{1,0:T(8,128)(2,1)S(1)}, u32[]{:S(2)}, u32[]{:S(2)}) collective-permute-start(bf16[16,256]{1,0:T(8,128)(2,1)S(1)} %combine.2.refs_0_.refs_1_), channel_id=1, source_target_pairs={{0,3},{1,0},{2,1},{3,2},{4,7},{5,4},{6,5},{7,6},{8,11},{9,8},{10,9... | collective-permute-start | bytes 24584 | tf_op jit(solution)/shard_map/ppermute | solution.py:631
  26.7 3.7 %collective-permute-start.1 = (bf16[16,256]{1,0:T(8,128)(2,1)S(1)}, bf16[16,256]{1,0:T(8,128)(2,1)S(1)}, u32[]{:S(2)}, u32[]{:S(2)}) collective-permute-start(bf16[16,256]{1,0:T(8,128)(2,1)S(1)} %combine.2.refs_0_.refs_1_), channel_id=1, source_target_pairs={{0,2},{1,3},{2,0},{3,1},{4,6},{5,7},{6,4},{7,5},{8,10},{9,11},{10,... | collective-permute-start | bytes 24584 | tf_op jit(solution)/shard_map/ppermute | solution.py:631
  28.3 3.1 %collective-permute-start = (bf16[16,256]{1,0:T(8,128)(2,1)S(1)}, bf16[16,256]{1,0:T(8,128)(2,1)S(1)}, u32[]{:S(2)}, u32[]{:S(2)}) collective-permute-start(bf16[16,256]{1,0:T(8,128)(2,1)S(1)} %combine.2.refs_0_.refs_1_), channel_id=1, source_target_pairs={{0,1},{1,2},{2,3},{3,0},{4,5},{5,6},{6,7},{7,4},{8,9},{9,10},{10,1... | collective-permute-start | bytes 24584 | tf_op jit(solution)/shard_map/ppermute | solution.py:631
  30.1 20.7 %copy-start.2 = (bf16[2,2048,256]{2,1,0:T(8,128)(2,1)S(1)}, bf16[2,2048,256]{2,1,0:T(8,128)(2,1)}, u32[]{:S(2)}) copy-start(bf16[2,2048,256]{2,1,0:T(8,128)(2,1)} %w_ref.5) | copy-start | bytes 6291460
  31.4 23.4 %copy-start.5 = (bf16[2,256,512]{2,1,0:T(8,128)(2,1)S(1)}, bf16[2,256,512]{2,1,0:T(8,128)(2,1)}, u32[]{:S(2)}) copy-start(bf16[2,256,512]{2,1,0:T(8,128)(2,1)} %refs_5_.4) | copy-start | bytes 1572868
  31.4 23.4 %copy-start.7 = (bf16[2,256,128]{2,1,0:T(8,128)(2,1)S(1)}, bf16[2,256,128]{2,1,0:T(8,128)(2,1)}, u32[]{:S(2)}) copy-start(bf16[2,256,128]{2,1,0:T(8,128)(2,1)} %refs_6_.4) | copy-start | bytes 393220
  31.4 23.5 %copy-start.8 = (bf16[2,256,128]{2,1,0:T(8,128)(2,1)S(1)}, bf16[2,256,128]{2,1,0:T(8,128)(2,1)}, u32[]{:S(2)}) copy-start(bf16[2,256,128]{2,1,0:T(8,128)(2,1)} %refs_7_.3) | copy-start | bytes 393220
  31.8 32.8 %copy-start.3 = (bf16[2,16,64,128]{3,2,1,0:T(8,128)(2,1)S(1)}, bf16[2,16,64,128]{3,2,1,0:T(8,128)(2,1)}, u32[]{:S(2)}) copy-start(bf16[2,16,64,128]{3,2,1,0:T(8,128)(2,1)} %key_ref.3) | copy-start | bytes 1572868
  31.8 32.8 %copy-start.4 = (bf16[2,16,64,128]{3,2,1,0:T(8,128)(2,1)S(1)}, bf16[2,16,64,128]{3,2,1,0:T(8,128)(2,1)}, u32[]{:S(2)}) copy-start(bf16[2,16,64,128]{3,2,1,0:T(8,128)(2,1)} %value_ref.3) | copy-start | bytes 1572868
  50.8 24.2 %copy-start.6 = (bf16[2,512,256]{2,1,0:T(8,128)(2,1)S(1)}, bf16[2,512,256]{2,1,0:T(8,128)(2,1)}, u32[]{:S(2)}) copy-start(bf16[2,512,256]{2,1,0:T(8,128)(2,1)} %w_ref.4) | copy-start | bytes 1572868
  51.1 1.4 %collective-permute-start.5 = (bf16[16,256]{1,0:T(8,128)(2,1)S(1)}, bf16[16,256]{1,0:T(8,128)(2,1)S(1)}, u32[]{:S(2)}, u32[]{:S(2)}) collective-permute-start(bf16[16,256]{1,0:T(8,128)(2,1)S(1)} %down.1.refs_1_), channel_id=1, source_target_pairs={{0,3},{1,0},{2,1},{3,2},{4,7},{5,4},{6,5},{7,6},{8,11},{9,8},{10,9... | collective-permute-start | bytes 24584 | tf_op jit(solution)/shard_map/ppermute | solution.py:631
  51.1 3.7 %collective-permute-start.4 = (bf16[16,256]{1,0:T(8,128)(2,1)S(1)}, bf16[16,256]{1,0:T(8,128)(2,1)S(1)}, u32[]{:S(2)}, u32[]{:S(2)}) collective-permute-start(bf16[16,256]{1,0:T(8,128)(2,1)S(1)} %down.1.refs_1_), channel_id=1, source_target_pairs={{0,2},{1,3},{2,0},{3,1},{4,6},{5,7},{6,4},{7,5},{8,10},{9,11},{10,... | collective-permute-start | bytes 24584 | tf_op jit(solution)/shard_map/ppermute | solution.py:631
  51.7 3.2 %collective-permute-start.3 = (bf16[16,256]{1,0:T(8,128)(2,1)S(1)}, bf16[16,256]{1,0:T(8,128)(2,1)S(1)}, u32[]{:S(2)}, u32[]{:S(2)}) collective-permute-start(bf16[16,256]{1,0:T(8,128)(2,1)S(1)} %down.1.refs_1_), channel_id=1, source_target_pairs={{0,1},{1,2},{2,3},{3,0},{4,5},{5,6},{6,7},{7,4},{8,9},{9,10},{10,1... | collective-permute-start | bytes 24584 | tf_op jit(solution)/shard_map/ppermute | solution.py:631
  54.8 25.1 %copy-start.1 = (bf16[2,256,2048]{2,1,0:T(8,128)(2,1)S(1)}, bf16[2,256,2048]{2,1,0:T(8,128)(2,1)}, u32[]{:S(2)}) copy-start(bf16[2,256,2048]{2,1,0:T(8,128)(2,1)} %refs_6_.5) | copy-start | bytes 6291460
  55.0 24.9 %copy-start = (bf16[2,256,2048]{2,1,0:T(8,128)(2,1)S(1)}, bf16[2,256,2048]{2,1,0:T(8,128)(2,1)}, u32[]{:S(2)}) copy-start(bf16[2,256,2048]{2,1,0:T(8,128)(2,1)} %refs_5_.5) | copy-start | bytes 6291460
  75.5 2.9 %collective-permute-start.8 = (bf16[16,256]{1,0:T(8,128)(2,1)S(1)}, bf16[16,256]{1,0:T(8,128)(2,1)S(1)}, u32[]{:S(2)}, u32[]{:S(2)}) collective-permute-start(bf16[16,256]{1,0:T(8,128)(2,1)S(1)} %combine.3.part_ref.refs_1_), channel_id=1, source_target_pairs={{0,3},{1,0},{2,1},{3,2},{4,7},{5,4},{6,5},{7,6},{8,11},{9,8},{10,9... | collective-permute-start | bytes 24584 | tf_op jit(solution)/shard_map/ppermute | solution.py:631
  75.6 3.7 %collective-permute-start.7 = (bf16[16,256]{1,0:T(8,128)(2,1)S(1)}, bf16[16,256]{1,0:T(8,128)(2,1)S(1)}, u32[]{:S(2)}, u32[]{:S(2)}) collective-permute-start(bf16[16,256]{1,0:T(8,128)(2,1)S(1)} %combine.3.part_ref.refs_1_), channel_id=1, source_target_pairs={{0,2},{1,3},{2,0},{3,1},{4,6},{5,7},{6,4},{7,5},{8,10},{9,11},{10,... | collective-permute-start | bytes 24584 | tf_op jit(solution)/shard_map/ppermute | solution.py:631
  76.8 3.1 %collective-permute-start.6 = (bf16[16,256]{1,0:T(8,128)(2,1)S(1)}, bf16[16,256]{1,0:T(8,128)(2,1)S(1)}, u32[]{:S(2)}, u32[]{:S(2)}) collective-permute-start(bf16[16,256]{1,0:T(8,128)(2,1)S(1)} %combine.3.part_ref.refs_1_), channel_id=1, source_target_pairs={{0,1},{1,2},{2,3},{3,0},{4,5},{5,6},{6,7},{7,4},{8,9},{9,10},{10,1... | collective-permute-start | bytes 24584 | tf_op jit(solution)/shard_map/ppermute | solution.py:631
  99.3 1.2 %collective-permute-start.9 = (f32[16,128]{1,0:T(8,128)S(1)}, f32[16,128]{1,0:T(8,128)S(1)}, u32[]{:S(2)}, u32[]{:S(2)}) collective-permute-start(f32[16,128]{1,0:T(8,128)S(1)} %get-tuple-element.42), channel_id=1, source_target_pairs={{0,1},{1,0},{2,3},{3,2},{4,5},{5,4},{6,7},{7,6},{8,9},{9,8},{10,11... | collective-permute-start | bytes 24584 | tf_op jit(solution)/shard_map/ppermute | solution.py:783

commit v8 on v7

--- a/solution.py
+++ b/solution.py
@@ -509,8 +509,8 @@
     side = jnp.zeros((requests, LANES), jnp.float32)
     for h in range(heads):
         part = slice(h * requests, (h + 1) * requests)
-        for group in range(5):
-            side = jnp.where(lane == group * heads + h, (top if group < 3 else sums)[part], side)
+        both = jnp.where(lane < 3 * heads, top[part], sums[part])
+        side = jnp.where((lane % heads == h) & (lane < 5 * heads), both, side)
     spare = jnp.zeros((requests, LANES), jnp.float32)
     for j, line in enumerate(rows):
         spare = jnp.where(request // 4 == j, line, spare)
@@ -558,6 +558,9 @@
     for f, s in zip(factors[1:], sums[1:]):
         total = total + f * s
 
+    scale = 1.0 / total
+    factors = [f * scale for f in factors]
+
     def spread(column, pair):
         return jnp.where(low, column[:, 2 * pair : 2 * pair + 1], column[:, 2 * pair + 1 : 2 * pair + 2])
 
@@ -567,7 +570,7 @@
         for m in range(members):
             piece = got_ref[m, :, pair * LANES : (pair + 1) * LANES].astype(jnp.float32)
             acc = acc + piece * spread(factors[m], pair)
-        attended.append((acc / spread(total, pair)).astype(jnp.bfloat16))
+        attended.append(acc.astype(jnp.bfloat16))
     out_ref[...] = dot32(jnp.concatenate(attended, axis=1), w_ref[layer]).astype(jnp.bfloat16)
 
 

time: 111 us -> 111 us (level)
  no operation moved by 1% of the time
where the time goes in v8:
time: 111 us
  blocking collectives  89.2 us (80%)
  Pallas kernels  9.62 us (9%)
  waiting for transfers between devices  6.94 us (6%)
  starting transfers between devices  4.03 us (4%)
    all_to_all x8, blocking collectives, swap(): return lax.all_to_all(chunks, ('seq', 'tp'), 0, 0, axis_index_groups=groups)  79.9 us
    pallas_call x16, Pallas kernels, call(): pl.pallas_call(body, out_shape=out_shape, in_specs=[vmem if i < held else...  9.62 us
    all_to_all x1, blocking collectives, per_device(): lax.all_to_all(stream, ('seq', 'tp'), 0, 0, axis_index_groups=everyone)  9.37 us
    ppermute x9, waiting for transfers between devices, tp_parts(): lax.ppermute(part, 'tp', [(i, (i + k) % n_tp) for i in range(n_tp)])  5.76 us
    ppermute x9, starting transfers between devices, tp_parts(): lax.ppermute(part, 'tp', [(i, (i + k) % n_tp) for i in range(n_tp)])  4.03 us
  transfers between devices with their start and end apart: 10, of which 7 were waited for; matrix products, arithmetic and copies ran while one was open for 0% of the time, Pallas kernels for 3%

profile of v8, /device:TPU:0, one launch (start us, length us, event | category | flops | bytes accessed | tf_op | source)
XLA Modules:
  0.0 110.6 jit_solution(5556657187623675733)
XLA Ops:
  0.6 1.4 %first.1 = (bf16[16,256]{1,0:T(8,128)(2,1)S(1)}, f32[16,128]{1,0:T(8,128)S(1)}, f32[16,128]{1,0:T(8,128)S(1)}, s32[16,128]{1,0:T(8,128)S(1)}, bf16[8,16,640]{2,1...) custom-call(bf16[16,2048]{1,0:T(8,128)(2,1)} %refs_0_.1, ...), custom_call_target="tpu_custom_call" | custom-call | tf_op jit(solution)/shard_map/first/pallas_call | solution.py:233
  2.0 13.9 %all_to_all.45.got_ref = bf16[8,16,640]{2,1,0:T(8,128)(2,1)S(1)} all-to-all(bf16[8,16,640]{2,1,0:T(8,128)(2,1)S(1)} %get-tuple-element.25), channel_id=1, replica_groups={{0,4,12,8,24,28,20,16},{13,9,25,29,21,17,1,5},{2,6,14,10,26,30,22,18},{..., dimensions={0} | all-to-all | bytes 327680 | tf_op jit(solution)/shard_map/all_to_all | solution.py:630
  15.9 0.9 attend.2
  16.8 9.4 %all_to_all.46.got_ref.refs_0_ = bf16[8,16,640]{2,1,0:T(8,128)(2,1)S(1)} all-to-all(bf16[8,16,640]{2,1,0:T(8,128)(2,1)S(1)} %attend.2), channel_id=1, replica_groups={{0,4,12,8,24,28,20,16},{13,9,25,29,21,17,1,5},{2,6,14,10,26,30,22,18},{..., dimensions={0} | all-to-all | bytes 327680 | tf_op jit(solution)/shard_map/all_to_all | solution.py:630
  26.3 0.5 combine.2.refs_0_.refs_1_
  26.8 0.0 collective-permute-start.2
  26.8 1.6 %collective-permute-start.1 = (bf16[16,256]{1,0:T(8,128)(2,1)S(1)}, bf16[16,256]{1,0:T(8,128)(2,1)S(1)}, u32[]{:S(2)}, u32[]{:S(2)}) collective-permute-start(bf16[16,256]{1,0:T(8,128)(2,1)S(1)} %combine.2.refs_0_.refs_1_), channel_id=1, source_target_pairs={{0,2},{1,3},{2,0},{3,1},{4,6},{5,7},{6,4},{7,5},{8,10},{9,11},{10,... | collective-permute-start | bytes 24584 | tf_op jit(solution)/shard_map/ppermute | solution.py:634
  28.4 0.2 collective-permute-start
  28.6 1.6 %load.1 = (bf16[1,256,2048]{2,1,0:T(8,128)(2,1)S(1)}, bf16[1,256,2048]{2,1,0:T(8,128)(2,1)S(1)}) custom-call(bf16[16,256]{1,0:T(8,128)(2,1)S(1)} %combine.2.refs_0_.refs_1_, bf16[2,256,2048]{2,1,0:T(8,128)(2,1)} %refs_5_.5, bf16[2,256,2048]{2,1,0:T(8,128)(2,1)} %refs_6_.5), custom_call_target="tpu_custom_call" | custom-call | tf_op jit(solution)/shard_map/load/pallas_call | solution.py:233
  30.1 0.0 copy-start.2
  30.1 0.0 collective-permute-done.2.refs_4_
  30.2 0.4 collective-permute-done.1.refs_3_
  30.5 0.9 collective-permute-done.refs_2_
  31.5 0.4 widen.2
  31.9 9.6 %all_to_all.47.got_ref = bf16[8,16,640]{2,1,0:T(8,128)(2,1)S(1)} all-to-all(bf16[8,16,640]{2,1,0:T(8,128)(2,1)S(1)} %get-tuple-element.35), channel_id=1, replica_groups={{0,4,12,8,24,28,20,16},{13,9,25,29,21,17,1,5},{2,6,14,10,26,30,22,18},{..., dimensions={0} | all-to-all | bytes 327680 | tf_op jit(solution)/shard_map/all_to_all | solution.py:630
  41.4 0.2 silu.2
  41.6 9.3 %all_to_all.48.got_ref = bf16[8,16,256]{2,1,0:T(8,128)(2,1)S(1)} all-to-all(bf16[8,16,256]{2,1,0:T(8,128)(2,1)S(1)} %silu.2), channel_id=1, replica_groups={{0,4,12,8,24,28,20,16},{13,9,25,29,21,17,1,5},{2,6,14,10,26,30,22,18},{..., dimensions={0} | all-to-all | bytes 131072 | tf_op jit(solution)/shard_map/all_to_all | solution.py:630
  50.9 0.2 down.1.refs_1_
  51.1 0.0 collective-permute-start.5
  51.2 0.6 collective-permute-start.4
  51.7 0.2 collective-permute-start.3
  51.9 0.6 collective-permute-done.5.refs_4_
  52.5 2.4 %collective-permute-done.4.refs_3_ = bf16[16,256]{1,0:T(8,128)(2,1)S(1)} collective-permute-done((bf16[16,256]{1,0:T(8,128)(2,1)S(1)}, bf16[16,256]{1,0:T(8,128)(2,1)S(1)}, u32[]{:S(2)}, u32[]{:S(2)}) %collective-permute-start.4) | collective-permute-done | bytes 8224 | tf_op jit(solution)/shard_map/ppermute | solution.py:634
  54.9 0.0 collective-permute-done.3.refs_2_
  54.9 0.0 copy-done.8
  54.9 0.0 copy-start.1
  54.9 0.2 next.1
  55.1 0.0 copy-start
  55.1 9.5 %all_to_all.49.got_ref = bf16[8,16,640]{2,1,0:T(8,128)(2,1)S(1)} all-to-all(bf16[8,16,640]{2,1,0:T(8,128)(2,1)S(1)} %get-tuple-element.37), channel_id=1, replica_groups={{0,4,12,8,24,28,20,16},{13,9,25,29,21,17,1,5},{2,6,14,10,26,30,22,18},{..., dimensions={0} | all-to-all | bytes 327680 | tf_op jit(solution)/shard_map/all_to_all | solution.py:630
  64.7 0.9 attend.3
  65.6 9.6 %all_to_all.50.got_ref.refs_1_ = bf16[8,16,640]{2,1,0:T(8,128)(2,1)S(1)} all-to-all(bf16[8,16,640]{2,1,0:T(8,128)(2,1)S(1)} %attend.3), channel_id=1, replica_groups={{0,4,12,8,24,28,20,16},{13,9,25,29,21,17,1,5},{2,6,14,10,26,30,22,18},{..., dimensions={0} | all-to-all | bytes 327680 | tf_op jit(solution)/shard_map/all_to_all | solution.py:630
  75.2 0.5 combine.3.part_ref.refs_1_
  75.7 0.0 collective-permute-start.8
  75.7 1.3 %collective-permute-start.7 = (bf16[16,256]{1,0:T(8,128)(2,1)S(1)}, bf16[16,256]{1,0:T(8,128)(2,1)S(1)}, u32[]{:S(2)}, u32[]{:S(2)}) collective-permute-start(bf16[16,256]{1,0:T(8,128)(2,1)S(1)} %combine.3.part_ref.refs_1_), channel_id=1, source_target_pairs={{0,2},{1,3},{2,0},{3,1},{4,6},{5,7},{6,4},{7,5},{8,10},{9,11},{10,... | collective-permute-start | bytes 24584 | tf_op jit(solution)/shard_map/ppermute | solution.py:634
  77.0 0.2 collective-permute-start.6
  77.2 1.4 %store.1 = (bf16[2,16,64,128]{3,2,1,0:T(8,128)(2,1)}, bf16[2,16,64,128]{3,2,1,0:T(8,128)(2,1)}, f32[8,128]{1,0:T(8,128)S(1)}) custom-call(bf16[16,256]{1,0:T(8,128)(2,1)S(1)} %combine.3.part_ref.refs_1_, s32[16,128]{1,0:T(8,128)S(1)} %get-tuple-element.28.length_ref, bf16[2,16,64,128]{3,2,1,0:T(8,128)(2,1)S(1)} %copy-done.3, ...), custom_call_target="tpu_custom_call" | custom-call | tf_op jit(solution)/shard_map/store/pallas_call | solution.py:233
  78.5 0.0 collective-permute-done.8.refs_4_
  78.5 0.9 collective-permute-done.7.refs_3_
  79.4 0.6 collective-permute-done.6.refs_2_
  80.1 0.4 widen.3
  80.5 9.4 %all_to_all.51.got_ref = bf16[8,16,640]{2,1,0:T(8,128)(2,1)S(1)} all-to-all(bf16[8,16,640]{2,1,0:T(8,128)(2,1)S(1)} %get-tuple-element.40), channel_id=1, replica_groups={{0,4,12,8,24,28,20,16},{13,9,25,29,21,17,1,5},{2,6,14,10,26,30,22,18},{..., dimensions={0} | all-to-all | bytes 327680 | tf_op jit(solution)/shard_map/all_to_all | solution.py:630
  89.9 0.2 silu.3
  90.1 9.1 %all_to_all.52.got_ref = bf16[8,16,256]{2,1,0:T(8,128)(2,1)S(1)} all-to-all(bf16[8,16,256]{2,1,0:T(8,128)(2,1)S(1)} %silu.3), channel_id=1, replica_groups={{0,4,12,8,24,28,20,16},{13,9,25,29,21,17,1,5},{2,6,14,10,26,30,22,18},{..., dimensions={0} | all-to-all | bytes 131072 | tf_op jit(solution)/shard_map/all_to_all | solution.py:630
  99.2 0.2 down_last.1
  99.4 0.0 collective-permute-start.9
  99.4 1.2 %collective-permute-done.9.got_ref = f32[16,128]{1,0:T(8,128)S(1)} collective-permute-done((f32[16,128]{1,0:T(8,128)S(1)}, f32[16,128]{1,0:T(8,128)S(1)}, u32[]{:S(2)}, u32[]{:S(2)}) %collective-permute-start.9) | collective-permute-done | bytes 8224 | tf_op jit(solution)/shard_map/ppermute | solution.py:786
  100.6 9.4 %all_to_all.53.got_ref = bf16[32,16,128]{2,1,0:T(8,128)(2,1)S(1)} all-to-all(bf16[32,16,128]{2,1,0:T(8,128)(2,1)S(1)} %meet.1), channel_id=1, replica_groups={{0,1,3,2,4,5,7,6,12,13,15,14,8,9,11,10,24,25,27,26,28,29,31,30,20,21,23..., dimensions={0} | all-to-all | bytes 262144 | tf_op jit(solution)/shard_map/all_to_all | solution.py:796
  110.0 0.6 last.1
  (15 shorter events, 0.0 us)
Async XLA Ops:
  26.8 3.4 %collective-permute-start.2 = (bf16[16,256]{1,0:T(8,128)(2,1)S(1)}, bf16[16,256]{1,0:T(8,128)(2,1)S(1)}, u32[]{:S(2)}, u32[]{:S(2)}) collective-permute-start(bf16[16,256]{1,0:T(8,128)(2,1)S(1)} %combine.2.refs_0_.refs_1_), channel_id=1, source_target_pairs={{0,3},{1,0},{2,1},{3,2},{4,7},{5,4},{6,5},{7,6},{8,11},{9,8},{10,9... | collective-permute-start | bytes 24584 | tf_op jit(solution)/shard_map/ppermute | solution.py:634
  26.8 3.7 %collective-permute-start.1 = (bf16[16,256]{1,0:T(8,128)(2,1)S(1)}, bf16[16,256]{1,0:T(8,128)(2,1)S(1)}, u32[]{:S(2)}, u32[]{:S(2)}) collective-permute-start(bf16[16,256]{1,0:T(8,128)(2,1)S(1)} %combine.2.refs_0_.refs_1_), channel_id=1, source_target_pairs={{0,2},{1,3},{2,0},{3,1},{4,6},{5,7},{6,4},{7,5},{8,10},{9,11},{10,... | collective-permute-start | bytes 24584 | tf_op jit(solution)/shard_map/ppermute | solution.py:634
  28.4 3.1 %collective-permute-start = (bf16[16,256]{1,0:T(8,128)(2,1)S(1)}, bf16[16,256]{1,0:T(8,128)(2,1)S(1)}, u32[]{:S(2)}, u32[]{:S(2)}) collective-permute-start(bf16[16,256]{1,0:T(8,128)(2,1)S(1)} %combine.2.refs_0_.refs_1_), channel_id=1, source_target_pairs={{0,1},{1,2},{2,3},{3,0},{4,5},{5,6},{6,7},{7,4},{8,9},{9,10},{10,1... | collective-permute-start | bytes 24584 | tf_op jit(solution)/shard_map/ppermute | solution.py:634
  30.1 20.8 %copy-start.2 = (bf16[2,2048,256]{2,1,0:T(8,128)(2,1)S(1)}, bf16[2,2048,256]{2,1,0:T(8,128)(2,1)}, u32[]{:S(2)}) copy-start(bf16[2,2048,256]{2,1,0:T(8,128)(2,1)} %w_ref.5) | copy-start | bytes 6291460
  31.5 23.4 %copy-start.5 = (bf16[2,256,512]{2,1,0:T(8,128)(2,1)S(1)}, bf16[2,256,512]{2,1,0:T(8,128)(2,1)}, u32[]{:S(2)}) copy-start(bf16[2,256,512]{2,1,0:T(8,128)(2,1)} %refs_5_.4) | copy-start | bytes 1572868
  31.5 23.4 %copy-start.7 = (bf16[2,256,128]{2,1,0:T(8,128)(2,1)S(1)}, bf16[2,256,128]{2,1,0:T(8,128)(2,1)}, u32[]{:S(2)}) copy-start(bf16[2,256,128]{2,1,0:T(8,128)(2,1)} %refs_6_.4) | copy-start | bytes 393220
  31.5 23.5 %copy-start.8 = (bf16[2,256,128]{2,1,0:T(8,128)(2,1)S(1)}, bf16[2,256,128]{2,1,0:T(8,128)(2,1)}, u32[]{:S(2)}) copy-start(bf16[2,256,128]{2,1,0:T(8,128)(2,1)} %refs_7_.3) | copy-start | bytes 393220
  31.8 32.8 %copy-start.3 = (bf16[2,16,64,128]{3,2,1,0:T(8,128)(2,1)S(1)}, bf16[2,16,64,128]{3,2,1,0:T(8,128)(2,1)}, u32[]{:S(2)}) copy-start(bf16[2,16,64,128]{3,2,1,0:T(8,128)(2,1)} %key_ref.3) | copy-start | bytes 1572868
  31.9 32.8 %copy-start.4 = (bf16[2,16,64,128]{3,2,1,0:T(8,128)(2,1)S(1)}, bf16[2,16,64,128]{3,2,1,0:T(8,128)(2,1)}, u32[]{:S(2)}) copy-start(bf16[2,16,64,128]{3,2,1,0:T(8,128)(2,1)} %value_ref.3) | copy-start | bytes 1572868
  50.9 24.3 %copy-start.6 = (bf16[2,512,256]{2,1,0:T(8,128)(2,1)S(1)}, bf16[2,512,256]{2,1,0:T(8,128)(2,1)}, u32[]{:S(2)}) copy-start(bf16[2,512,256]{2,1,0:T(8,128)(2,1)} %w_ref.4) | copy-start | bytes 1572868
  51.1 1.4 %collective-permute-start.5 = (bf16[16,256]{1,0:T(8,128)(2,1)S(1)}, bf16[16,256]{1,0:T(8,128)(2,1)S(1)}, u32[]{:S(2)}, u32[]{:S(2)}) collective-permute-start(bf16[16,256]{1,0:T(8,128)(2,1)S(1)} %down.1.refs_1_), channel_id=1, source_target_pairs={{0,3},{1,0},{2,1},{3,2},{4,7},{5,4},{6,5},{7,6},{8,11},{9,8},{10,9... | collective-permute-start | bytes 24584 | tf_op jit(solution)/shard_map/ppermute | solution.py:634
  51.2 3.7 %collective-permute-start.4 = (bf16[16,256]{1,0:T(8,128)(2,1)S(1)}, bf16[16,256]{1,0:T(8,128)(2,1)S(1)}, u32[]{:S(2)}, u32[]{:S(2)}) collective-permute-start(bf16[16,256]{1,0:T(8,128)(2,1)S(1)} %down.1.refs_1_), channel_id=1, source_target_pairs={{0,2},{1,3},{2,0},{3,1},{4,6},{5,7},{6,4},{7,5},{8,10},{9,11},{10,... | collective-permute-start | bytes 24584 | tf_op jit(solution)/shard_map/ppermute | solution.py:634
  51.7 3.2 %collective-permute-start.3 = (bf16[16,256]{1,0:T(8,128)(2,1)S(1)}, bf16[16,256]{1,0:T(8,128)(2,1)S(1)}, u32[]{:S(2)}, u32[]{:S(2)}) collective-permute-start(bf16[16,256]{1,0:T(8,128)(2,1)S(1)} %down.1.refs_1_), channel_id=1, source_target_pairs={{0,1},{1,2},{2,3},{3,0},{4,5},{5,6},{6,7},{7,4},{8,9},{9,10},{10,1... | collective-permute-start | bytes 24584 | tf_op jit(solution)/shard_map/ppermute | solution.py:634
  54.9 25.1 %copy-start.1 = (bf16[2,256,2048]{2,1,0:T(8,128)(2,1)S(1)}, bf16[2,256,2048]{2,1,0:T(8,128)(2,1)}, u32[]{:S(2)}) copy-start(bf16[2,256,2048]{2,1,0:T(8,128)(2,1)} %refs_6_.5) | copy-start | bytes 6291460
  55.1 24.9 %copy-start = (bf16[2,256,2048]{2,1,0:T(8,128)(2,1)S(1)}, bf16[2,256,2048]{2,1,0:T(8,128)(2,1)}, u32[]{:S(2)}) copy-start(bf16[2,256,2048]{2,1,0:T(8,128)(2,1)} %refs_5_.5) | copy-start | bytes 6291460
  75.7 2.8 %collective-permute-start.8 = (bf16[16,256]{1,0:T(8,128)(2,1)S(1)}, bf16[16,256]{1,0:T(8,128)(2,1)S(1)}, u32[]{:S(2)}, u32[]{:S(2)}) collective-permute-start(bf16[16,256]{1,0:T(8,128)(2,1)S(1)} %combine.3.part_ref.refs_1_), channel_id=1, source_target_pairs={{0,3},{1,0},{2,1},{3,2},{4,7},{5,4},{6,5},{7,6},{8,11},{9,8},{10,9... | collective-permute-start | bytes 24584 | tf_op jit(solution)/shard_map/ppermute | solution.py:634
  75.7 3.7 %collective-permute-start.7 = (bf16[16,256]{1,0:T(8,128)(2,1)S(1)}, bf16[16,256]{1,0:T(8,128)(2,1)S(1)}, u32[]{:S(2)}, u32[]{:S(2)}) collective-permute-start(bf16[16,256]{1,0:T(8,128)(2,1)S(1)} %combine.3.part_ref.refs_1_), channel_id=1, source_target_pairs={{0,2},{1,3},{2,0},{3,1},{4,6},{5,7},{6,4},{7,5},{8,10},{9,11},{10,... | collective-permute-start | bytes 24584 | tf_op jit(solution)/shard_map/ppermute | solution.py:634
  77.0 3.1 %collective-permute-start.6 = (bf16[16,256]{1,0:T(8,128)(2,1)S(1)}, bf16[16,256]{1,0:T(8,128)(2,1)S(1)}, u32[]{:S(2)}, u32[]{:S(2)}) collective-permute-start(bf16[16,256]{1,0:T(8,128)(2,1)S(1)} %combine.3.part_ref.refs_1_), channel_id=1, source_target_pairs={{0,1},{1,2},{2,3},{3,0},{4,5},{5,6},{6,7},{7,4},{8,9},{9,10},{10,1... | collective-permute-start | bytes 24584 | tf_op jit(solution)/shard_map/ppermute | solution.py:634
  99.4 1.2 %collective-permute-start.9 = (f32[16,128]{1,0:T(8,128)S(1)}, f32[16,128]{1,0:T(8,128)S(1)}, u32[]{:S(2)}, u32[]{:S(2)}) collective-permute-start(f32[16,128]{1,0:T(8,128)S(1)} %get-tuple-element.42), channel_id=1, source_target_pairs={{0,1},{1,0},{2,3},{3,2},{4,5},{5,4},{6,7},{7,6},{8,9},{9,8},{10,11... | collective-permute-start | bytes 24584 | tf_op jit(solution)/shard_map/ppermute | solution.py:786
